TPU v7x, 32 devices: a whole 2x2x4 slice. The times are simulated.
32 devices in a mesh: slab: 4 (over y, core), filt: 8 (over z, x).
Axes of the slice: x: 2, y: 2, z: 4, core: 2. Of those that a mesh axis runs over, the one named last changes fastest.
Arguments:
- volume: float32 [512, 32, 256], P('filt', 'slab'), may hold values from -6 to 6
- filters: float32 [27, 512, 512], P(None, 'filt'), may hold values from -0.0546875 to 0.0546875
- out_grad: float32 [512, 32, 256], P('filt', 'slab'), may hold values from -6 to 6
Outputs:
- activated: float32 [512, 32, 256], P('filt', 'slab')
- input_grad: float32 [512, 32, 256], P('filt', 'slab')
- weight_grad: float32 [27, 512, 512], P(None, 'filt')
All inputs are finite; a program needn't handle non-finite values.
Results may differ from a plain program's by a relative error of at most 0.00012.
Values sent between devices are 32-bit elements; how exact they have to be, the bound alone decides.
No kernel may reach another device: no remote copies, remote signals or barrier semaphores. Data moves between devices by JAX's collectives and lax.ppermute only.
A program may use at most 128 MiB of HBM per device.

v0:
```python
import functools
import math

import jax
import jax.numpy as jnp
from jax import lax
from jax.experimental import pallas as pl
from jax.experimental.pallas import tpu as pltpu
from jax.sharding import PartitionSpec as P


WIDTH = 16


f32 = jnp.float32
bf16 = jnp.bfloat16


def parts_of(x):
    high = x.astype(bf16)
    low = (x - high.astype(f32)).astype(bf16)
    return high, low


def dot(a, b):
    return lax.dot_general(a, b, (((1,), (0,)), ((), ())), preferred_element_type=f32)


def dot_t(a, b):
    return lax.dot_general(a, b, (((1,), (1,)), ((), ())), preferred_element_type=f32)


def beside(ring, n, rim):
    return jnp.where(ring[ring.shape[0] - 3 + n] > 0, rim, 0.0)


def whole(shape):
    return pl.BlockSpec(shape, lambda *_: (0,) * len(shape))


def limit():
    return pltpu.CompilerParams(vmem_limit_bytes=28 * 2**20)


def cost(flops, moved):
    return pl.CostEstimate(flops=int(flops), bytes_accessed=int(moved), transcendentals=0)


def moved(x, down, across):
    size = x.shape[-1]
    place = lax.broadcasted_iota(jnp.int32, x.shape, 1)
    if across:
        column = place % WIDTH + across
        rolled = pltpu.roll(x, (-across) % size, 1)
        x = jnp.where((column >= 0) & (column < WIDTH), rolled, 0.0)
    if down:
        target = place + down * WIDTH
        rolled = pltpu.roll(x, (-down * WIDTH) % size, 1)
        x = jnp.where((target >= 0) & (target < size), rolled, 0.0)
    return x


def prepare_kernel(chan, filters, ahead, back_high, back_low):
    taps, out_rows, lanes = filters.shape
    third = taps * out_rows // 3
    for a in range(3):
        x = filters[a * 9 : (a + 1) * 9].reshape(third, lanes)
        high, low = parts_of(x)
        for k in range(lanes // chan):
            at = slice(k * chan, (k + 1) * chan)
            ahead[a, k] = jnp.concatenate([high[:, at], low[:, at], high[:, at]], axis=1)
    turned = [filters[a * 9 : (a + 1) * 9].reshape(third, lanes).T for a in (2, 1, 0)]
    high, low = parts_of(jnp.concatenate(turned, axis=1))
    back_high[...] = high
    back_low[...] = low


def prepare(filters, chan):
    taps, out_rows, channels = filters.shape
    lanes = min(128, channels)
    each = lanes // chan
    return pl.pallas_call(
        functools.partial(prepare_kernel, chan),
        grid=(channels // lanes,),
        in_specs=[pl.BlockSpec((taps, out_rows, lanes), lambda i: (0, 0, i))],
        out_specs=[
            pl.BlockSpec((3, each, 9 * out_rows, 3 * chan), lambda i: (0, i, 0, 0)),
            pl.BlockSpec((lanes, taps * out_rows), lambda i: (i, 0)),
            pl.BlockSpec((lanes, taps * out_rows), lambda i: (i, 0)),
        ],
        out_shape=[
            jax.ShapeDtypeStruct((3, channels // chan, 9 * out_rows, 3 * chan), bf16),
            jax.ShapeDtypeStruct((channels, taps * out_rows), bf16),
            jax.ShapeDtypeStruct((channels, taps * out_rows), bf16),
        ],
        cost_estimate=cost(0, 5 * 4 * filters.size),
        name="prepare",
    )(filters)


def rims_kernel(*refs):
    blocks, (last, top) = refs[:-2], refs[-2:]
    at = 0
    for block in blocks:
        rows, depth, _ = block.shape
        planes = jnp.swapaxes(block[...], 0, 1)
        last[at : at + rows] = planes[depth - 1]
        top[at : at + rows] = planes[0]
        at += rows


def rims(blocks):
    rows = sum(b.shape[0] for b in blocks)
    shape = jax.ShapeDtypeStruct((rows, blocks[0].shape[2]), f32)
    return pl.pallas_call(
        rims_kernel,
        out_shape=[shape, shape],
        cost_estimate=cost(0, 4 * sum(b.size for b in blocks)),
        compiler_params=limit(),
        name="rims",
    )(*blocks)


def gathered(answer, out_rows):
    rows = []
    for b in range(3):
        row = None
        for c in range(3):
            at = (3 * b + c) * out_rows
            term = moved(answer[at : at + out_rows], 0, c - 1)
            row = term if row is None else row + term
        rows.append(moved(row, b - 1, 0))
    return rows[0] + rows[1] + rows[2]


def tripled(x):
    high, low = parts_of(x)
    return jnp.concatenate([high, high, low], axis=0)


def forward_kernel(counts, places, rim_places, first, ring, *refs):
    refs = list(refs)

    def take(n):
        taken = refs[:n]
        del refs[:n]
        return taken

    blocks = take(sum(counts))
    (source,) = take(1)
    rims_in = take(2) if rim_places else []
    total_in = None if first else take(3)[0]
    total_out, high_all, low_all, field, high_part, low_part, high_rim, low_rim = take(8)
    weights, rim_weights, sems, fetch_sems = refs
    fetches = [
        pltpu.make_async_copy(source.at[:, ring[place]], weights.at[k], fetch_sems.at[k])
        for k, place in enumerate(places)
    ]
    for k, place in enumerate(rim_places):
        for n in range(2):
            sem = fetch_sems.at[len(fetches)]
            fetches.append(
                pltpu.make_async_copy(source.at[2 * n, ring[place]], rim_weights.at[n, k], sem)
            )
    for fetch in fetches:
        fetch.start()
    depth, out_rows, area = total_out.shape
    chan = field.shape[2] // 3
    copies = []

    def keep(part, target, place, lanes):
        at = pl.ds(pl.multiple_of(ring[place] * chan, chan), chan)
        copies.append(pltpu.make_async_copy(part, target.at[at, lanes], sems.at[len(copies)]))
        copies[-1].start()

    begin = 0
    for k, pieces in enumerate(counts):
        loaded = [jnp.swapaxes(b[...], 0, 1) for b in blocks[begin : begin + pieces]]
        begin += pieces
        for plane in range(depth):
            rows = [b[plane] for b in loaded]
            x = rows[0] if pieces == 1 else jnp.concatenate(rows, axis=0)
            high, low = parts_of(x)
            field[k, plane, 0:chan] = high
            field[k, plane, chan : 2 * chan] = high
            field[k, plane, 2 * chan : 3 * chan] = low
            high_part[k, :, plane * area : (plane + 1) * area] = high
            low_part[k, :, plane * area : (plane + 1) * area] = low
        lanes = pl.ds(area, depth * area)
        keep(high_part.at[k], high_all, places[k], lanes)
        keep(low_part.at[k], low_all, places[k], lanes)
    for n, rim in enumerate(rims_in):
        lanes = pl.ds(n * (depth + 1) * area, area)
        for k in range(len(rim_places)):
            high, low = parts_of(beside(ring, n, rim[k * chan : (k + 1) * chan]))
            high_rim[n, k] = high
            low_rim[n, k] = low
            keep(high_rim.at[n, k], high_all, rim_places[k], lanes)
            keep(low_rim.at[n, k], low_all, rim_places[k], lanes)

    for fetch in fetches:
        fetch.wait()
    for plane in range(depth):
        terms = []
        for a in range(3):
            if 0 <= plane + a - 1 < depth:
                for k in range(len(counts)):
                    terms.append((weights[k, a], field[k, plane + a - 1]))
        for n, edge in enumerate((0, depth - 1)):
            if plane == edge:
                for k in range(len(rim_places)):
                    right = [high_rim[n, k], high_rim[n, k], low_rim[n, k]]
                    terms.append((rim_weights[n, k], jnp.concatenate(right, axis=0)))
        answer = None
        for left, right in terms:
            term = dot(left, right)
            answer = term if answer is None else answer + term
        total = gathered(answer, out_rows)
        if total_in is not None:
            total = total + total_in[plane]
        total_out[plane] = total
    for copy in copies:
        copy.wait()


def forward(ring, sets, places, rim_places, outer, weights, carry, sizes):
    depth, chan, area, channels, out_rows = sizes
    counts = tuple(len(s) for s in sets)
    blocks = [b for s in sets for b in s]
    first = carry is None
    lanes = (depth + 2) * area
    keep = pl.BlockSpec(memory_space=pltpu.HBM)
    in_specs = [whole(b.shape) for b in blocks]
    args = list(blocks)
    in_specs.append(keep)
    args.append(weights)
    if rim_places:
        in_specs += [whole(o.shape) for o in outer]
        args += list(outer)
    aliases = {}
    if not first:
        base = len(args) + 1
        in_specs += [whole((depth, out_rows, area)), keep, keep]
        args += list(carry)
        aliases = {base: 0, base + 1: 1, base + 2: 2}
    rims_held = max(1, len(rim_places))
    return pl.pallas_call(
        functools.partial(forward_kernel, counts, places, rim_places, first),
        grid_spec=pltpu.PrefetchScalarGridSpec(
            num_scalar_prefetch=1,
            grid=(1,),
            in_specs=in_specs,
            out_specs=[whole((depth, out_rows, area)), keep, keep],
            scratch_shapes=[
                pltpu.VMEM((len(sets), depth, 3 * chan, area), bf16),
                pltpu.VMEM((len(sets), chan, depth * area), bf16),
                pltpu.VMEM((len(sets), chan, depth * area), bf16),
                pltpu.VMEM((2, rims_held, chan, area), bf16),
                pltpu.VMEM((2, rims_held, chan, area), bf16),
                pltpu.VMEM((len(sets), 3) + weights.shape[2:], bf16),
                pltpu.VMEM((2, rims_held) + weights.shape[2:], bf16),
                pltpu.SemaphoreType.DMA((2 * len(sets) + 4 * rims_held,)),
                pltpu.SemaphoreType.DMA((len(sets) + 2 * rims_held,)),
            ],
        ),
        out_shape=[
            jax.ShapeDtypeStruct((depth, out_rows, area), f32),
            jax.ShapeDtypeStruct((channels, lanes), bf16),
            jax.ShapeDtypeStruct((channels, lanes), bf16),
        ],
        input_output_aliases=aliases,
        cost_estimate=cost(
            len(sets) * 2 * 81 * out_rows * chan * depth * area, len(sets) * 8 * chan * lanes
        ),
        compiler_params=limit(),
        name="forward",
    )(ring, *args)


def middle_kernel(chan, ring, total, grad, below, above, source, *refs):
    active_out, spread_out, high_all, low_all, high_rim, low_rim, weights, sems, fetch_sems = refs[2:]
    depth, out_rows, area = total.shape
    copies = []
    rim_sums = []
    opposite = ring[high_all.shape[0] // chan // 2]
    fetches = [
        pltpu.make_async_copy(source.at[2 * n, opposite], weights.at[n], fetch_sems.at[n])
        for n in range(2)
    ]
    for fetch in fetches:
        fetch.start()
    for n, rim in enumerate((below, above)):
        value = beside(ring, n, rim[...])
        high, low = parts_of(value)
        high_rim[n] = high
        low_rim[n] = low
        at = pl.ds(pl.multiple_of(opposite * chan, chan), chan)
        lanes = pl.ds(n * (depth + 1) * area, area)
        for m, (part, target) in enumerate(((high_rim, high_all), (low_rim, low_all))):
            copy = pltpu.make_async_copy(part.at[n], target.at[at, lanes], sems.at[n, m])
            copy.start()
            copies.append(copy)
        fetches[n].wait()
        rim_sums.append(gathered(dot(weights[n], tripled(value)), out_rows))
    positives = []
    for plane in range(depth):
        value = total[plane]
        if plane == 0:
            value = value + rim_sums[0]
        if plane == depth - 1:
            value = value + rim_sums[1]
        positives.append(jnp.maximum(value, 0.0))
    positives = jnp.stack(positives)
    active_out[...] = jnp.swapaxes(positives * positives, 0, 1)
    grads = jnp.swapaxes(grad[...], 0, 1)
    nothing = jnp.zeros((9 * out_rows, area), bf16)
    for part in range(2):
        spread_out[part, 0] = nothing
        spread_out[part, depth + 1] = nothing
    for plane in range(depth):
        pre_grad = 2.0 * positives[plane] * grads[plane]
        for c in range(3):
            across = moved(pre_grad, 0, 1 - c)
            for b in range(3):
                high, low = parts_of(moved(across, 1 - b, 0))
                at = (3 * b + c) * out_rows
                spread_out[0, plane + 1, at : at + out_rows] = high
                spread_out[1, plane + 1, at : at + out_rows] = low
    for copy in copies:
        copy.wait()


def middle(ring, carry, grad, outer, weights, chan):
    total, high_all, low_all = carry
    depth, out_rows, area = total.shape
    keep = pl.BlockSpec(memory_space=pltpu.HBM)
    return pl.pallas_call(
        functools.partial(middle_kernel, chan),
        grid_spec=pltpu.PrefetchScalarGridSpec(
            num_scalar_prefetch=1,
            grid=(1,),
            in_specs=[whole(x.shape) for x in (total, grad, *outer)]
            + [keep, keep, keep],
            out_specs=[
                whole((out_rows, depth, area)),
                whole((2, depth + 2, 9 * out_rows, area)),
                keep,
                keep,
            ],
            scratch_shapes=[
                pltpu.VMEM((2, chan, area), bf16),
                pltpu.VMEM((2, chan, area), bf16),
                pltpu.VMEM((2,) + weights.shape[2:], bf16),
                pltpu.SemaphoreType.DMA((2, 2)),
                pltpu.SemaphoreType.DMA((2,)),
            ],
        ),
        out_shape=[
            jax.ShapeDtypeStruct((out_rows, depth, area), f32),
            jax.ShapeDtypeStruct((2, depth + 2, 9 * out_rows, area), bf16),
            jax.ShapeDtypeStruct(high_all.shape, bf16),
            jax.ShapeDtypeStruct(low_all.shape, bf16),
        ],
        input_output_aliases={6: 2, 7: 3},
        cost_estimate=cost(0, 4 * 18 * out_rows * depth * area),
        compiler_params=limit(),
        name="middle",
    )(ring, total, grad, *outer, weights, high_all, low_all)


def inner_kernel(begin, planes, spread, high, low, out):
    deep = high.shape[1]
    count, chan, _ = out.shape
    area = spread.shape[3]
    group = 2 - planes % 2

    def some(i, nothing):
        for j in range(group):
            near = spread[0, pl.ds(begin + i * group + j, 3)].reshape(deep, area)
            far = spread[1, pl.ds(begin + i * group + j, 3)].reshape(deep, area)
            value = dot(high[...], near) + dot(high[...], far) + dot(low[...], near)
            lanes = pl.ds(pl.multiple_of((i * group + j) * area, area), area)
            out[:, :, lanes] = value.reshape(count, chan, area)
        return nothing

    lax.fori_loop(0, planes // group, some, 0)


def outer_kernel(spread, high, low, below, above):
    depth = spread.shape[1] - 2
    third = high.shape[1] // 3
    for out, plane, at in ((below, 1, 2 * third), (above, depth, 0)):
        lanes = slice(at, at + third)
        value = dot(high[:, lanes], spread[0, plane]) + dot(high[:, lanes], spread[1, plane])
        value = value + dot(low[:, lanes], spread[0, plane])
        out[...] = value.reshape(out.shape)


def inner_terms(begin, planes, spread, high, low, chan):
    channels, deep = high.shape
    area = spread.shape[3]
    return pl.pallas_call(
        functools.partial(inner_kernel, begin, planes),
        out_shape=jax.ShapeDtypeStruct((channels // chan, chan, planes * area), f32),
        cost_estimate=cost(6 * channels * deep * planes * area, 2 * spread.size + 4 * high.size),
        compiler_params=limit(),
        name="inner_terms",
    )(spread, high, low)


def outer_terms(spread, high, low, chan):
    channels, deep = high.shape
    shape = jax.ShapeDtypeStruct((channels // chan, chan, spread.shape[3]), f32)
    return pl.pallas_call(
        outer_kernel,
        out_shape=[shape, shape],
        cost_estimate=cost(4 * channels * deep * spread.shape[3], spread.size),
        compiler_params=limit(),
        name="outer_terms",
    )(spread, high, low)


def filter_kernel(tap, ring, spread, high, low, keep_out, send_out, total):
    depth = spread.shape[1] - 2
    rows, area = spread.shape[2:]
    half = rows // 2
    channels = high.shape[0]
    step = min(256, channels)
    for at in range(0, channels, step):
        value = None
        for plane in range(depth):
            lanes = slice((tap + plane) * area, (tap + plane + 1) * area)
            right = high[at : at + step, lanes]
            term = dot_t(spread[0, plane + 1], right) + dot_t(spread[1, plane + 1], right)
            term = term + dot_t(spread[0, plane + 1], low[at : at + step, lanes])
            value = term if value is None else value + term
        total[:, at : at + step] = value
    side = ring[ring.shape[0] - 1]
    mine = pl.multiple_of(side * half, half)
    other = pl.multiple_of((1 - side) * half, half)
    keep_out[...] = total[pl.ds(mine, half), :]
    send_out[...] = total[pl.ds(other, half), :]


def filter_terms(tap, ring, spread, high, low):
    rows = spread.shape[2]
    channels = high.shape[0]
    return pl.pallas_call(
        functools.partial(filter_kernel, tap),
        grid_spec=pltpu.PrefetchScalarGridSpec(
            num_scalar_prefetch=1,
            grid=(1,),
            in_specs=[whole(spread.shape), whole(high.shape), whole(low.shape)],
            out_specs=[whole((rows // 2, channels))] * 2,
            scratch_shapes=[pltpu.VMEM((rows, channels), f32)],
        ),
        out_shape=[jax.ShapeDtypeStruct((rows // 2, channels), f32)] * 2,
        cost_estimate=cost(6 * rows * high.size, 4 * high.size + 2 * spread.size),
        compiler_params=limit(),
        name="filter_terms",
    )(ring, spread, high, low)


def place_kernel(scale, ring, *refs):
    mine, other, out = refs[0], refs[1], refs[-1]
    half = mine.shape[0]
    side = ring[ring.shape[0] - 1]
    out[0, pl.ds(pl.multiple_of(side * half, half), half), :] = mine[...] / scale
    out[0, pl.ds(pl.multiple_of((1 - side) * half, half), half), :] = other[...] / scale


def place(tap, ring, mine, other, carry, scale):
    half, channels = mine.shape
    args = [mine, other]
    in_specs = [whole(mine.shape)] * 2
    aliases = {}
    if carry is not None:
        args.append(carry)
        in_specs.append(pl.BlockSpec(memory_space=pl.ANY))
        aliases = {3: 0}
    return pl.pallas_call(
        functools.partial(place_kernel, scale),
        grid_spec=pltpu.PrefetchScalarGridSpec(
            num_scalar_prefetch=1,
            grid=(1,),
            in_specs=in_specs,
            out_specs=pl.BlockSpec((1, 2 * half, channels), lambda i, s: (tap, 0, 0)),
        ),
        out_shape=jax.ShapeDtypeStruct((3, 2 * half, channels), f32),
        input_output_aliases=aliases,
        cost_estimate=cost(0, 16 * half * channels),
        compiler_params=limit(),
        name="place",
    )(ring, *args)


def local_sum(ring, inner, rim, first):
    value, rim = inner[0], beside(ring, 0 if first else 1, rim[0])
    area = rim.shape[1]
    width = value.shape[1]
    if first:
        return jnp.concatenate([value[:, :area] + rim, value[:, area:]], axis=1)
    return jnp.concatenate([value[:, : width - area], value[:, width - area :] + rim], axis=1)


def opening_kernel(first, ring, inner, rim, up_out, down_out):
    value = local_sum(ring, inner, rim, first)
    half = value.shape[0] // 2
    up_out[...] = value[:half]
    down_out[...] = value[half:]


def running_kernel(first, ring, up_inner, up_rim, down_inner, down_rim, up, down, up_out, down_out):
    value = local_sum(ring, up_inner, up_rim, first)
    size = up.shape[0]
    up_out[0:size] = value[0:size] + up[...]
    if size < value.shape[0]:
        up_out[size:] = value[size:]
    value = local_sum(ring, down_inner, down_rim, first)
    rest = value.shape[0] - size
    down_out[rest:] = value[rest:] + down[...]
    if rest:
        down_out[0:rest] = value[0:rest]


def closing_kernel(ring, *refs):
    chains, out = (refs[0:4], refs[4:8]), refs[8]
    area = out.shape[2]
    values = []
    for first, (inner, rim, up, down) in zip((True, False), chains):
        value = local_sum(ring, inner, rim, first) + up[...] + down[...]
        values += [value[:, at : at + area] for at in range(0, value.shape[1], area)]
    out[...] = jnp.swapaxes(jnp.stack(values), 0, 1)


def summed(kernel, ring, pieces, outs):
    specs, args = [], []
    for piece in pieces:
        if isinstance(piece, tuple):
            array, k = piece
            specs.append(pl.BlockSpec((1,) + array.shape[1:], lambda i, s, k=k: (s[k], 0, 0)))
            args.append(array)
        else:
            specs.append(whole(piece.shape))
            args.append(piece)
    return pl.pallas_call(
        kernel,
        grid_spec=pltpu.PrefetchScalarGridSpec(
            num_scalar_prefetch=1,
            grid=(1,),
            in_specs=specs,
            out_specs=[whole(o) for o in outs],
        ),
        out_shape=[jax.ShapeDtypeStruct(o, f32) for o in outs],
        cost_estimate=cost(0, sum(12 * math.prod(o) for o in outs)),
        compiler_params=limit(),
    )(ring, *args)


def shards(volume, filters, out_grad):
    chan, depth, area = volume.shape
    out_rows = filters.shape[1]
    channels = filters.shape[2]
    count = lax.axis_size("filt")
    slabs = lax.axis_size("slab")
    sizes = (depth, chan, area, channels, out_rows)

    order = list(range(0, count, 2)) + list(range(1, count, 2))[::-1]
    ring_up = [(order[i], order[(i + 1) % count]) for i in range(count)]
    ring_down = [(b, a) for a, b in ring_up]
    rows = [
        [order[(order.index(f) + k) % count] for k in range(count)]
        + [int(s > 0), int(s < slabs - 1), s % 2]
        for s in range(slabs)
        for f in range(count)
    ]
    here = lax.axis_index("slab") * count + lax.axis_index("filt")
    ring = lax.dynamic_index_in_dim(jnp.array(rows, jnp.int32), here, 0, keepdims=False)

    def send(x, pairs):
        return lax.ppermute(x, "filt", pairs)

    deeper = [(i, (i + 1) % slabs) for i in range(slabs)]
    shallower = [(b, a) for a, b in deeper]
    half = count // 2

    ahead, back_high, back_low = prepare(filters, chan)
    ahead = pltpu.with_memory_space_constraint(ahead, pltpu.HBM)

    carry = None
    up = down = volume
    rim_places, outer = (), None
    for step in range(half + 1):
        if step == 0:
            sets, places = [[volume]], (0,)
        elif step < half:
            up, down = send(up, ring_up), send(down, ring_down)
            sets, places = [[up], [down]], (count - step, step)
        else:
            up = send(up[: chan // 2], ring_up)
            down = send(down[chan // 2 :], ring_down)
            sets, places = [[up, down]], (half,)
        last, top = rims([b for blocks in sets for b in blocks])
        carry = forward(ring, sets, places, rim_places, outer, ahead, carry, sizes)
        outer = lax.ppermute(last, "slab", deeper), lax.ppermute(top, "slab", shallower)
        rim_places = places

    activated, spread, high_field, low_field = middle(ring, carry, out_grad, outer, ahead, chan)

    below, above = outer_terms(spread, back_high, back_low, chan)
    from_above = lax.ppermute(below, "slab", shallower)
    from_below = lax.ppermute(above, "slab", deeper)
    run = depth // 2
    inner = []
    for c in range(2):
        inner.append(inner_terms(c * run, run, spread, back_high, back_low, chan))
    edge = [from_below, from_above]

    scale = math.sqrt(depth * slabs * area)

    def swap(x, bit):
        return lax.ppermute(x, "slab", [(i, i ^ bit) for i in range(slabs)])

    weight_grad = None
    for tap in range(3):
        keep, give = filter_terms(tap, ring, spread, high_field, low_field)
        keep = keep + swap(give, 1)
        bit = 2
        while bit < slabs:
            keep = keep + swap(keep, bit)
            bit *= 2
        other = swap(keep, 1)
        weight_grad = place(tap, ring, keep, other, weight_grad, scale)

    piece = (chan, run * area)
    part = (chan // 2, run * area)
    flows = []
    for c in range(2):
        kernel = functools.partial(opening_kernel, c == 0)
        flows.append(summed(kernel, ring, [(inner[c], half), (edge[c], half)], [part, part]))
    for step in range(half - 1, 0, -1):
        for c in range(2):
            up, down = flows[c]
            up, down = send(up, ring_up), send(down, ring_down)
            kernel = functools.partial(running_kernel, c == 0)
            pieces = [(x, p) for p in (step, count - step) for x in (inner[c], edge[c])]
            flows[c] = summed(kernel, ring, pieces + [up, down], [piece, piece])
    pieces = []
    for c in range(2):
        up, down = flows[c]
        pieces += [(inner[c], 0), (edge[c], 0), send(up, ring_up), send(down, ring_down)]
    (input_grad,) = summed(closing_kernel, ring, pieces, [(chan, depth, area)])
    return activated, input_grad, weight_grad.reshape(filters.shape)


def solution(mesh):
    placed = (P("filt", "slab", None), P(None, "filt", None), P("filt", "slab", None))

    def step(*args):
        return shards(*args)

    step = jax.shard_map(
        step,
        mesh=mesh,
        in_specs=placed,
        out_specs=(P("filt", "slab", None), P("filt", "slab", None), P(None, "filt", None)),
        check_vma=False,
    )
    return step
```

profile of v0, /device:TPU:0, one launch (start us, length us, event | category | flops | bytes accessed | tf_op | source)
XLA Modules:
  0.0 186.7 jit_solution(3645905223321887392)
XLA Ops:
  0.6 3.0 %collective-permute-start.4 = (f32[64,8,256]{2,1,0:T(8,128)}, f32[64,8,256]{2,1,0:T(8,128)S(1)}, u32[]{:S(2)}, u32[]{:S(2)}) collective-permute-start(f32[64,8,256]{2,1,0:T(8,128)} %refs_0_.3), channel_id=1, source_target_pairs={{2,0},{4,2},{6,4},{7,6},{5,7},{3,5},{1,3},{0,1},{10,8},{12,10},{14... | collective-permute-start | bytes 1572872 | tf_op jit(solution)/shard_map/ppermute | solution.py:581
  3.8 12.1 %collective-permute-done.4.refs_1_ = f32[64,8,256]{2,1,0:T(8,128)S(1)} collective-permute-done((f32[64,8,256]{2,1,0:T(8,128)}, f32[64,8,256]{2,1,0:T(8,128)S(1)}, u32[]{:S(2)}, u32[]{:S(2)}) %collective-permute-start.4) | collective-permute-done | bytes 524320 | tf_op jit(solution)/shard_map/ppermute | solution.py:581
  15.9 1.7 collective-permute-start.5
  17.9 11.1 %collective-permute-done.5.refs_1_ = f32[64,8,256]{2,1,0:T(8,128)S(1)} collective-permute-done((f32[64,8,256]{2,1,0:T(8,128)S(1)}, f32[64,8,256]{2,1,0:T(8,128)S(1)}, u32[]{:S(2)}, u32[]{:S(2)}) %collective-permute-start.5) | collective-permute-done | bytes 524320 | tf_op jit(solution)/shard_map/ppermute | solution.py:581
  32.2 1.7 collective-permute-start.15
  33.9 7.4 %prepare.1 = (bf16[3,8,576,192]{3,2,1,0:T(8,128)(2,1)}, bf16[512,1728]{1,0:T(8,128)(2,1)}, bf16[512,1728]{1,0:T(8,128)(2,1)}) custom-call(f32[27,64,512]{2,1,0:T(8,128)} %filters.1), custom_call_target="tpu_custom_call" | custom-call | bytes 17694720 | tf_op jit(solution)/shard_map/prepare/pallas_call | solution.py:82
  43.0 3.9 %forward.5 = (f32[8,64,256]{2,1,0:T(8,128)S(1)}, bf16[512,2560]{1,0:T(8,128)(2,1)S(1)}, bf16[512,2560]{1,0:T(8,128)(2,1)S(1)}) custom-call(s32[11]{0:T(128)S(1)} %dynamic-slice_bitcast_fusion.ring, f32[64,8,256]{2,1,0:T(8,128)S(1)} %copy-done.1, bf16[3,8,576,192]{3,2,1,0:T(8,128)(2,1)} %get-tuple-element.59.refs_1_.refs_2_.source), custom_call_target="tpu_custom_call" | custom-call | flops 1358954496 | bytes 1310720 | tf_op jit(solution)/shard_map/forward/pallas_call | solution.py:247
  47.1 1.7 collective-permute-start.13
  48.8 6.1 %forward.6 = (f32[8,64,256]{2,1,0:T(8,128)S(1)}, bf16[512,2560]{1,0:T(8,128)(2,1)S(1)}, bf16[512,2560]{1,0:T(8,128)(2,1)S(1)}) custom-call(s32[11]{0:T(128)S(1)} %dynamic-slice_bitcast_fusion.ring, f32[64,8,256]{2,1,0:T(8,128)S(1)} %collective-permute-done.refs_0_, ...), custom_call_target="tpu_custom_call", output_to_operand_aliasing={{0}: (6, {}), {1}: (7, {}), {2}: (8, {})} | custom-call | flops 2717908992 | bytes 2621440 | tf_op jit(solution)/shard_map/forward/pallas_call | solution.py:247
  55.2 1.7 collective-permute-start.11
  59.1 6.5 %forward.7 = (f32[8,64,256]{2,1,0:T(8,128)S(1)}, bf16[512,2560]{1,0:T(8,128)(2,1)S(1)}, bf16[512,2560]{1,0:T(8,128)(2,1)S(1)}) custom-call(s32[11]{0:T(128)S(1)} %dynamic-slice_bitcast_fusion.ring, f32[64,8,256]{2,1,0:T(8,128)S(1)} %collective-permute-done.1.refs_0_, ...), custom_call_target="tpu_custom_call", output_to_operand_aliasing={{0}: (6, {}), {1}: (7, {}), {2}: (8, {})} | custom-call | flops 2717908992 | bytes 2621440 | tf_op jit(solution)/shard_map/forward/pallas_call | solution.py:247
  65.8 1.7 collective-permute-start.9
  67.6 6.5 %forward.8 = (f32[8,64,256]{2,1,0:T(8,128)S(1)}, bf16[512,2560]{1,0:T(8,128)(2,1)S(1)}, bf16[512,2560]{1,0:T(8,128)(2,1)S(1)}) custom-call(s32[11]{0:T(128)S(1)} %dynamic-slice_bitcast_fusion.ring, f32[64,8,256]{2,1,0:T(8,128)S(1)} %collective-permute-done.2.refs_0_, ...), custom_call_target="tpu_custom_call", output_to_operand_aliasing={{0}: (6, {}), {1}: (7, {}), {2}: (8, {})} | custom-call | flops 2717908992 | bytes 2621440 | tf_op jit(solution)/shard_map/forward/pallas_call | solution.py:247
  74.3 1.7 collective-permute-start.17
  76.0 4.6 %forward.9 = (f32[8,64,256]{2,1,0:T(8,128)S(1)}, bf16[512,2560]{1,0:T(8,128)(2,1)S(1)}, bf16[512,2560]{1,0:T(8,128)(2,1)S(1)}) custom-call(s32[11]{0:T(128)S(1)} %dynamic-slice_bitcast_fusion.ring, f32[32,8,256]{2,1,0:T(8,128)S(1)} %collective-permute-done.3.refs_0_, ...), custom_call_target="tpu_custom_call", output_to_operand_aliasing={{0}: (6, {}), {1}: (7, {}), {2}: (8, {})} | custom-call | flops 1358954496 | bytes 1310720 | tf_op jit(solution)/shard_map/forward/pallas_call | solution.py:247
  80.6 5.3 %middle.1 = (f32[64,8,256]{2,1,0:T(8,128)}, bf16[2,10,576,256]{3,2,1,0:T(8,128)(2,1)S(1)}, bf16[512,2560]{1,0:T(8,128)(2,1)S(1)}, bf16[512,2560]{1,0:T(8,128)(2,1)S(1)}) custom-call(s32[11]{0:T(128)S(1)} %dynamic-slice_bitcast_fusion.ring, f32[8,64,256]{2,1,0:T(8,128)S(1)} %get-tuple-element.80.total, ...), custom_call_target="tpu_custom_call", output_to_operand_aliasing={{2}: (6, {}), {3}: (7, {})} | custom-call | bytes 9437184 | tf_op jit(solution)/shard_map/middle/pallas_call | solution.py:337
  85.9 4.5 %filter_terms.5 = (f32[288,512]{1,0:T(8,128)S(1)}, f32[288,512]{1,0:T(8,128)S(1)}) custom-call(s32[11]{0:T(128)S(1)} %dynamic-slice_bitcast_fusion.ring, bf16[2,10,576,256]{3,2,1,0:T(8,128)(2,1)S(1)} %get-tuple-element.86.spread, bf16[512,2560]{1,0:T(8,128)(2,1)S(1)} %get-tuple-element.107.high, bf16[512,2560]{1,0:T(8,128)(2,1)S(1)} %get-tuple-element.108.low), custom_call_target="tpu_custom_call" | custom-call | flops 4529848320 | bytes 11141120 | tf_op jit(solution)/shard_map/filter_terms/pallas_call | solution.py:448
  90.4 4.5 %filter_terms.4 = (f32[288,512]{1,0:T(8,128)S(1)}, f32[288,512]{1,0:T(8,128)S(1)}) custom-call(s32[11]{0:T(128)S(1)} %dynamic-slice_bitcast_fusion.ring, bf16[2,10,576,256]{3,2,1,0:T(8,128)(2,1)S(1)} %get-tuple-element.86.spread, bf16[512,2560]{1,0:T(8,128)(2,1)S(1)} %get-tuple-element.107.high, bf16[512,2560]{1,0:T(8,128)(2,1)S(1)} %get-tuple-element.108.low), custom_call_target="tpu_custom_call" | custom-call | flops 4529848320 | bytes 11141120 | tf_op jit(solution)/shard_map/filter_terms/pallas_call | solution.py:448
  96.3 1.7 collective-permute-start.27
  98.0 4.4 %filter_terms.3 = (f32[288,512]{1,0:T(8,128)S(1)}, f32[288,512]{1,0:T(8,128)S(1)}) custom-call(s32[11]{0:T(128)S(1)} %dynamic-slice_bitcast_fusion.ring, bf16[2,10,576,256]{3,2,1,0:T(8,128)(2,1)S(1)} %get-tuple-element.86.spread, bf16[512,2560]{1,0:T(8,128)(2,1)S(1)} %get-tuple-element.107.high, bf16[512,2560]{1,0:T(8,128)(2,1)S(1)} %get-tuple-element.108.low), custom_call_target="tpu_custom_call" | custom-call | flops 4529848320 | bytes 11141120 | tf_op jit(solution)/shard_map/filter_terms/pallas_call | solution.py:448
  103.2 6.1 %inner_terms.3.inner.up_inner.down_inner.refs_4_ = f32[8,64,1024]{2,1,0:T(8,128)S(1)} custom-call(bf16[2,10,576,256]{3,2,1,0:T(8,128)(2,1)S(1)} %get-tuple-element.86.spread, bf16[512,1728]{1,0:T(8,128)(2,1)S(1)} %copy-done.2, bf16[512,1728]{1,0:T(8,128)(2,1)S(1)} %copy-done.3), custom_call_target="tpu_custom_call" | custom-call | flops 5435817984 | bytes 9437184 | tf_op jit(solution)/shard_map/inner_terms/pallas_call | solution.py:402
  112.1 6.1 %inner_terms.2.inner.up_inner.down_inner.refs_0_ = f32[8,64,1024]{2,1,0:T(8,128)S(1)} custom-call(bf16[2,10,576,256]{3,2,1,0:T(8,128)(2,1)S(1)} %get-tuple-element.86.spread, bf16[512,1728]{1,0:T(8,128)(2,1)S(1)} %copy-done.2, bf16[512,1728]{1,0:T(8,128)(2,1)S(1)} %copy-done.3), custom_call_target="tpu_custom_call" | custom-call | flops 5435817984 | bytes 9437184 | tf_op jit(solution)/shard_map/inner_terms/pallas_call | solution.py:402
  123.4 1.6 collective-permute-start.30
  126.0 9.1 %collective-permute-done.20.down = f32[32,1024]{1,0:T(8,128)S(1)} collective-permute-done((f32[32,1024]{1,0:T(8,128)S(1)}, f32[32,1024]{1,0:T(8,128)S(1)}, u32[]{:S(2)}, u32[]{:S(2)}) %collective-permute-start.20) | collective-permute-done | bytes 131104 | tf_op jit(solution)/shard_map/ppermute | solution.py:581
  140.0 3.8 %collective-permute-done.21.up = f32[64,1024]{1,0:T(8,128)S(1)} collective-permute-done((f32[64,1024]{1,0:T(8,128)S(1)}, f32[64,1024]{1,0:T(8,128)S(1)}, u32[]{:S(2)}, u32[]{:S(2)}) %collective-permute-start.21) | collective-permute-done | bytes 262176 | tf_op jit(solution)/shard_map/ppermute | solution.py:581
  150.1 11.0 %collective-permute-done.37 = f32[288,512]{1,0:T(8,128)S(1)} collective-permute-done((f32[288,512]{1,0:T(8,128)S(1)}, f32[288,512]{1,0:T(8,128)S(1)}, u32[]{:S(2)}, u32[]{:S(2)}) %collective-permute-start.37) | collective-permute-done | bytes 589856 | tf_op jit(solution)/shard_map/ppermute | solution.py:622
  162.4 1.6 collective-permute-start.34
  165.2 6.0 %collective-permute-done.34.refs_6_ = f32[64,1024]{1,0:T(8,128)S(1)} collective-permute-done((f32[64,1024]{1,0:T(8,128)S(1)}, f32[64,1024]{1,0:T(8,128)S(1)}, u32[]{:S(2)}, u32[]{:S(2)}) %collective-permute-start.34) | collective-permute-done | bytes 262176 | tf_op jit(solution)/shard_map/ppermute | solution.py:581
  173.2 5.7 %collective-permute-done.25.refs_2_ = f32[64,1024]{1,0:T(8,128)S(1)} collective-permute-done((f32[64,1024]{1,0:T(8,128)S(1)}, f32[64,1024]{1,0:T(8,128)S(1)}, u32[]{:S(2)}, u32[]{:S(2)}) %collective-permute-start.25) | collective-permute-done | bytes 262176 | tf_op jit(solution)/shard_map/ppermute | solution.py:581
  181.7 1.7 place.3.refs_2_
  183.4 1.7 place.4.refs_2_
  185.0 1.7 place.5
  (107 shorter events, 37.8 us)
Async XLA Ops:
  0.6 15.2 %collective-permute-start.4 = (f32[64,8,256]{2,1,0:T(8,128)}, f32[64,8,256]{2,1,0:T(8,128)S(1)}, u32[]{:S(2)}, u32[]{:S(2)}) collective-permute-start(f32[64,8,256]{2,1,0:T(8,128)} %refs_0_.3), channel_id=1, source_target_pairs={{2,0},{4,2},{6,4},{7,6},{5,7},{3,5},{1,3},{0,1},{10,8},{12,10},{14... | collective-permute-start | bytes 1572872 | tf_op jit(solution)/shard_map/ppermute | solution.py:581
  3.6 13.9 %collective-permute-start = (f32[64,8,256]{2,1,0:T(8,128)}, f32[64,8,256]{2,1,0:T(8,128)S(1)}, u32[]{:S(2)}, u32[]{:S(2)}) collective-permute-start(f32[64,8,256]{2,1,0:T(8,128)} %refs_0_.3), channel_id=1, source_target_pairs={{0,2},{2,4},{4,6},{6,7},{7,5},{5,3},{3,1},{1,0},{8,10},{10,12},{12... | collective-permute-start | bytes 1572872 | tf_op jit(solution)/shard_map/ppermute | solution.py:581
  15.9 13.1 %collective-permute-start.5 = (f32[64,8,256]{2,1,0:T(8,128)S(1)}, f32[64,8,256]{2,1,0:T(8,128)S(1)}, u32[]{:S(2)}, u32[]{:S(2)}) collective-permute-start(f32[64,8,256]{2,1,0:T(8,128)S(1)} %collective-permute-done.4.refs_1_), channel_id=1, source_target_pairs={{2,0},{4,2},{6,4},{7,6},{5,7},{3,5},{1,3},{0,1},{10,8},{12,10},{14... | collective-permute-start | bytes 1572872 | tf_op jit(solution)/shard_map/ppermute | solution.py:581
  17.5 12.8 %collective-permute-start.1 = (f32[64,8,256]{2,1,0:T(8,128)S(1)}, f32[64,8,256]{2,1,0:T(8,128)S(1)}, u32[]{:S(2)}, u32[]{:S(2)}) collective-permute-start(f32[64,8,256]{2,1,0:T(8,128)S(1)} %collective-permute-done.refs_0_), channel_id=1, source_target_pairs={{0,2},{2,4},{4,6},{6,7},{7,5},{5,3},{3,1},{1,0},{8,10},{10,12},{12... | collective-permute-start | bytes 1572872 | tf_op jit(solution)/shard_map/ppermute | solution.py:581
  29.0 26.2 %collective-permute-start.6 = (f32[64,8,256]{2,1,0:T(8,128)S(1)}, f32[64,8,256]{2,1,0:T(8,128)S(1)}, u32[]{:S(2)}, u32[]{:S(2)}) collective-permute-start(f32[64,8,256]{2,1,0:T(8,128)S(1)} %collective-permute-done.5.refs_1_), channel_id=1, source_target_pairs={{2,0},{4,2},{6,4},{7,6},{5,7},{3,5},{1,3},{0,1},{10,8},{12,10},{14... | collective-permute-start | bytes 1572872 | tf_op jit(solution)/shard_map/ppermute | solution.py:581
  30.3 26.6 %collective-permute-start.2 = (f32[64,8,256]{2,1,0:T(8,128)S(1)}, f32[64,8,256]{2,1,0:T(8,128)S(1)}, u32[]{:S(2)}, u32[]{:S(2)}) collective-permute-start(f32[64,8,256]{2,1,0:T(8,128)S(1)} %collective-permute-done.1.refs_0_), channel_id=1, source_target_pairs={{0,2},{2,4},{4,6},{6,7},{7,5},{5,3},{3,1},{1,0},{8,10},{10,12},{12... | collective-permute-start | bytes 1572872 | tf_op jit(solution)/shard_map/ppermute | solution.py:581
  32.1 15.0 %collective-permute-start.14 = (f32[64,256]{1,0:T(8,128)S(1)}, f32[64,256]{1,0:T(8,128)S(1)}, u32[]{:S(2)}, u32[]{:S(2)}) collective-permute-start(f32[64,256]{1,0:T(8,128)S(1)} %get-tuple-element.66), channel_id=1, source_target_pairs={{0,8},{8,16},{16,24},{24,0},{1,9},{9,17},{17,25},{25,1},{2,10},{10... | collective-permute-start | bytes 196616 | tf_op jit(solution)/shard_map/ppermute | solution.py:605
  32.2 16.6 %collective-permute-start.15 = (f32[64,256]{1,0:T(8,128)S(1)}, f32[64,256]{1,0:T(8,128)S(1)}, u32[]{:S(2)}, u32[]{:S(2)}) collective-permute-start(f32[64,256]{1,0:T(8,128)S(1)} %get-tuple-element.67), channel_id=1, source_target_pairs={{8,0},{16,8},{24,16},{0,24},{9,1},{17,9},{25,17},{1,25},{10,2},{18... | collective-permute-start | bytes 196616 | tf_op jit(solution)/shard_map/ppermute | solution.py:605
  47.0 11.4 %collective-permute-start.12 = (f32[128,256]{1,0:T(8,128)S(1)}, f32[128,256]{1,0:T(8,128)S(1)}, u32[]{:S(2)}, u32[]{:S(2)}) collective-permute-start(f32[128,256]{1,0:T(8,128)S(1)} %get-tuple-element.64), channel_id=1, source_target_pairs={{0,8},{8,16},{16,24},{24,0},{1,9},{9,17},{17,25},{25,1},{2,10},{10... | collective-permute-start | bytes 393224 | tf_op jit(solution)/shard_map/ppermute | solution.py:605
  47.1 12.0 %collective-permute-start.13 = (f32[128,256]{1,0:T(8,128)S(1)}, f32[128,256]{1,0:T(8,128)S(1)}, u32[]{:S(2)}, u32[]{:S(2)}) collective-permute-start(f32[128,256]{1,0:T(8,128)S(1)} %get-tuple-element.65), channel_id=1, source_target_pairs={{8,0},{16,8},{24,16},{0,24},{9,1},{17,9},{25,17},{1,25},{10,2},{18... | collective-permute-start | bytes 393224 | tf_op jit(solution)/shard_map/ppermute | solution.py:605
  55.2 12.4 %collective-permute-start.11 = (f32[128,256]{1,0:T(8,128)S(1)}, f32[128,256]{1,0:T(8,128)S(1)}, u32[]{:S(2)}, u32[]{:S(2)}) collective-permute-start(f32[128,256]{1,0:T(8,128)S(1)} %get-tuple-element.63), channel_id=1, source_target_pairs={{8,0},{16,8},{24,16},{0,24},{9,1},{17,9},{25,17},{1,25},{10,2},{18... | collective-permute-start | bytes 393224 | tf_op jit(solution)/shard_map/ppermute | solution.py:605
  56.9 17.2 %collective-permute-start.7 = (f32[32,8,256]{2,1,0:T(8,128)S(1)}, f32[32,8,256]{2,1,0:T(8,128)S(1)}, u32[]{:S(2)}, u32[]{:S(2)}) collective-permute-start(f32[32,8,256]{2,1,0:T(8,128)S(1)} %slice.9), channel_id=1, source_target_pairs={{2,0},{4,2},{6,4},{7,6},{5,7},{3,5},{1,3},{0,1},{10,8},{12,10},{14... | collective-permute-start | bytes 786440 | tf_op jit(solution)/shard_map/ppermute | solution.py:581
  58.4 15.7 %collective-permute-start.3 = (f32[32,8,256]{2,1,0:T(8,128)S(1)}, f32[32,8,256]{2,1,0:T(8,128)S(1)}, u32[]{:S(2)}, u32[]{:S(2)}) collective-permute-start(f32[32,8,256]{2,1,0:T(8,128)S(1)} %slice.8), channel_id=1, source_target_pairs={{0,2},{2,4},{4,6},{6,7},{7,5},{5,3},{3,1},{1,0},{8,10},{10,12},{12... | collective-permute-start | bytes 786440 | tf_op jit(solution)/shard_map/ppermute | solution.py:581
  96.2 15.4 %collective-permute-start.18 = (f32[8,64,256]{2,1,0:T(8,128)S(1)}, f32[8,64,256]{2,1,0:T(8,128)S(1)}, u32[]{:S(2)}, u32[]{:S(2)}) collective-permute-start(f32[8,64,256]{2,1,0:T(8,128)S(1)} %get-tuple-element.89), channel_id=1, source_target_pairs={{0,8},{8,16},{16,24},{24,0},{1,9},{9,17},{17,25},{25,1},{2,10},{10... | collective-permute-start | bytes 1572872 | tf_op jit(solution)/shard_map/ppermute | solution.py:612
  96.3 13.1 %collective-permute-start.27 = (f32[8,64,256]{2,1,0:T(8,128)S(1)}, f32[8,64,256]{2,1,0:T(8,128)S(1)}, u32[]{:S(2)}, u32[]{:S(2)}) collective-permute-start(f32[8,64,256]{2,1,0:T(8,128)S(1)} %get-tuple-element.98), channel_id=1, source_target_pairs={{8,0},{16,8},{24,16},{0,24},{9,1},{17,9},{25,17},{1,25},{10,2},{18... | collective-permute-start | bytes 1572872 | tf_op jit(solution)/shard_map/ppermute | solution.py:611
  102.5 16.3 %collective-permute-start.42 = (f32[288,512]{1,0:T(8,128)S(1)}, f32[288,512]{1,0:T(8,128)S(1)}, u32[]{:S(2)}, u32[]{:S(2)}) collective-permute-start(f32[288,512]{1,0:T(8,128)S(1)} %get-tuple-element.114), channel_id=1, source_target_pairs={{0,8},{8,0},{16,24},{24,16},{1,9},{9,1},{17,25},{25,17},{2,10},{10... | collective-permute-start | bytes 1769480 | tf_op jit(solution)/shard_map/ppermute | solution.py:622
  102.6 17.9 %collective-permute-start.39 = (f32[288,512]{1,0:T(8,128)S(1)}, f32[288,512]{1,0:T(8,128)S(1)}, u32[]{:S(2)}, u32[]{:S(2)}) collective-permute-start(f32[288,512]{1,0:T(8,128)S(1)} %get-tuple-element.112), channel_id=1, source_target_pairs={{0,8},{8,0},{16,24},{24,16},{1,9},{9,1},{17,25},{25,17},{2,10},{10... | collective-permute-start | bytes 1769480 | tf_op jit(solution)/shard_map/ppermute | solution.py:622
  103.1 21.9 %collective-permute-start.36 = (f32[288,512]{1,0:T(8,128)S(1)}, f32[288,512]{1,0:T(8,128)S(1)}, u32[]{:S(2)}, u32[]{:S(2)}) collective-permute-start(f32[288,512]{1,0:T(8,128)S(1)} %get-tuple-element.110), channel_id=1, source_target_pairs={{0,8},{8,0},{16,24},{24,16},{1,9},{9,1},{17,25},{25,17},{2,10},{10... | collective-permute-start | bytes 1769480 | tf_op jit(solution)/shard_map/ppermute | solution.py:622
  110.0 11.9 %collective-permute-start.28 = (f32[32,1024]{1,0:T(8,128)S(1)}, f32[32,1024]{1,0:T(8,128)S(1)}, u32[]{:S(2)}, u32[]{:S(2)}) collective-permute-start(f32[32,1024]{1,0:T(8,128)S(1)} %get-tuple-element.99), channel_id=1, source_target_pairs={{0,2},{2,4},{4,6},{6,7},{7,5},{5,3},{3,1},{1,0},{8,10},{10,12},{12... | collective-permute-start | bytes 393224 | tf_op jit(solution)/shard_map/ppermute | solution.py:581
  111.6 11.1 %collective-permute-start.29 = (f32[32,1024]{1,0:T(8,128)S(1)}, f32[32,1024]{1,0:T(8,128)S(1)}, u32[]{:S(2)}, u32[]{:S(2)}) collective-permute-start(f32[32,1024]{1,0:T(8,128)S(1)} %get-tuple-element.100), channel_id=1, source_target_pairs={{2,0},{4,2},{6,4},{7,6},{5,7},{3,5},{1,3},{0,1},{10,8},{12,10},{14... | collective-permute-start | bytes 393224 | tf_op jit(solution)/shard_map/ppermute | solution.py:581
  120.5 26.0 %collective-permute-start.43 = (f32[288,512]{1,0:T(8,128)S(1)}, f32[288,512]{1,0:T(8,128)S(1)}, u32[]{:S(2)}, u32[]{:S(2)}) collective-permute-start(f32[288,512]{1,0:T(8,128)S(1)} %add.31), channel_id=1, source_target_pairs={{0,16},{8,24},{16,0},{24,8},{1,17},{9,25},{17,1},{25,9},{2,18},{10... | collective-permute-start | bytes 1769480 | tf_op jit(solution)/shard_map/ppermute | solution.py:622
  121.9 27.5 %collective-permute-start.40 = (f32[288,512]{1,0:T(8,128)S(1)}, f32[288,512]{1,0:T(8,128)S(1)}, u32[]{:S(2)}, u32[]{:S(2)}) collective-permute-start(f32[288,512]{1,0:T(8,128)S(1)} %add.29), channel_id=1, source_target_pairs={{0,16},{8,24},{16,0},{24,8},{1,17},{9,25},{17,1},{25,9},{2,18},{10... | collective-permute-start | bytes 1769480 | tf_op jit(solution)/shard_map/ppermute | solution.py:622
  123.4 13.9 %collective-permute-start.30 = (f32[64,1024]{1,0:T(8,128)S(1)}, f32[64,1024]{1,0:T(8,128)S(1)}, u32[]{:S(2)}, u32[]{:S(2)}) collective-permute-start(f32[64,1024]{1,0:T(8,128)S(1)} %get-tuple-element.101), channel_id=1, source_target_pairs={{0,2},{2,4},{4,6},{6,7},{7,5},{5,3},{3,1},{1,0},{8,10},{10,12},{12... | collective-permute-start | bytes 786440 | tf_op jit(solution)/shard_map/ppermute | solution.py:581
  125.0 13.9 %collective-permute-start.31 = (f32[64,1024]{1,0:T(8,128)S(1)}, f32[64,1024]{1,0:T(8,128)S(1)}, u32[]{:S(2)}, u32[]{:S(2)}) collective-permute-start(f32[64,1024]{1,0:T(8,128)S(1)} %get-tuple-element.102), channel_id=1, source_target_pairs={{2,0},{4,2},{6,4},{7,6},{5,7},{3,5},{1,3},{0,1},{10,8},{12,10},{14... | collective-permute-start | bytes 786440 | tf_op jit(solution)/shard_map/ppermute | solution.py:581
  135.1 25.9 %collective-permute-start.37 = (f32[288,512]{1,0:T(8,128)S(1)}, f32[288,512]{1,0:T(8,128)S(1)}, u32[]{:S(2)}, u32[]{:S(2)}) collective-permute-start(f32[288,512]{1,0:T(8,128)S(1)} %add.27), channel_id=1, source_target_pairs={{0,16},{8,24},{16,0},{24,8},{1,17},{9,25},{17,1},{25,9},{2,18},{10... | collective-permute-start | bytes 1769480 | tf_op jit(solution)/shard_map/ppermute | solution.py:622
  143.8 17.3 %collective-permute-start.32 = (f32[64,1024]{1,0:T(8,128)S(1)}, f32[64,1024]{1,0:T(8,128)S(1)}, u32[]{:S(2)}, u32[]{:S(2)}) collective-permute-start(f32[64,1024]{1,0:T(8,128)S(1)} %get-tuple-element.103), channel_id=1, source_target_pairs={{0,2},{2,4},{4,6},{6,7},{7,5},{5,3},{3,1},{1,0},{8,10},{10,12},{12... | collective-permute-start | bytes 786440 | tf_op jit(solution)/shard_map/ppermute | solution.py:581
  145.4 16.3 %collective-permute-start.33 = (f32[64,1024]{1,0:T(8,128)S(1)}, f32[64,1024]{1,0:T(8,128)S(1)}, u32[]{:S(2)}, u32[]{:S(2)}) collective-permute-start(f32[64,1024]{1,0:T(8,128)S(1)} %get-tuple-element.104), channel_id=1, source_target_pairs={{2,0},{4,2},{6,4},{7,6},{5,7},{3,5},{1,3},{0,1},{10,8},{12,10},{14... | collective-permute-start | bytes 786440 | tf_op jit(solution)/shard_map/ppermute | solution.py:581
  146.5 15.9 %collective-permute-start.23 = (f32[64,1024]{1,0:T(8,128)S(1)}, f32[64,1024]{1,0:T(8,128)S(1)}, u32[]{:S(2)}, u32[]{:S(2)}) collective-permute-start(f32[64,1024]{1,0:T(8,128)S(1)} %get-tuple-element.94), channel_id=1, source_target_pairs={{0,2},{2,4},{4,6},{6,7},{7,5},{5,3},{3,1},{1,0},{8,10},{10,12},{12... | collective-permute-start | bytes 786440 | tf_op jit(solution)/shard_map/ppermute | solution.py:581
  149.4 14.7 %collective-permute-start.24 = (f32[64,1024]{1,0:T(8,128)S(1)}, f32[64,1024]{1,0:T(8,128)S(1)}, u32[]{:S(2)}, u32[]{:S(2)}) collective-permute-start(f32[64,1024]{1,0:T(8,128)S(1)} %get-tuple-element.95), channel_id=1, source_target_pairs={{2,0},{4,2},{6,4},{7,6},{5,7},{3,5},{1,3},{0,1},{10,8},{12,10},{14... | collective-permute-start | bytes 786440 | tf_op jit(solution)/shard_map/ppermute | solution.py:581
  161.0 20.7 %collective-permute-start.44 = (f32[288,512]{1,0:T(8,128)S(1)}, f32[288,512]{1,0:T(8,128)S(1)}, u32[]{:S(2)}, u32[]{:S(2)}) collective-permute-start(f32[288,512]{1,0:T(8,128)S(1)} %add.32.refs_0_), channel_id=1, source_target_pairs={{0,8},{8,0},{16,24},{24,16},{1,9},{9,1},{17,25},{25,17},{2,10},{10... | collective-permute-start | bytes 1769480 | tf_op jit(solution)/shard_map/ppermute | solution.py:622
  161.1 22.2 %collective-permute-start.41 = (f32[288,512]{1,0:T(8,128)S(1)}, f32[288,512]{1,0:T(8,128)S(1)}, u32[]{:S(2)}, u32[]{:S(2)}) collective-permute-start(f32[288,512]{1,0:T(8,128)S(1)} %add.30.refs_0_), channel_id=1, source_target_pairs={{0,8},{8,0},{16,24},{24,16},{1,9},{9,1},{17,25},{25,17},{2,10},{10... | collective-permute-start | bytes 1769480 | tf_op jit(solution)/shard_map/ppermute | solution.py:622
  161.7 23.3 %collective-permute-start.38 = (f32[288,512]{1,0:T(8,128)S(1)}, f32[288,512]{1,0:T(8,128)S(1)}, u32[]{:S(2)}, u32[]{:S(2)}) collective-permute-start(f32[288,512]{1,0:T(8,128)S(1)} %add.28.refs_0_), channel_id=1, source_target_pairs={{0,8},{8,0},{16,24},{24,16},{1,9},{9,1},{17,25},{25,17},{2,10},{10... | collective-permute-start | bytes 1769480 | tf_op jit(solution)/shard_map/ppermute | solution.py:622
  (18 other events, 121.6 us)
where the time goes:
time: 187 us
  Pallas kernels  79 us (42%)
  waiting for transfers between devices  61.7 us (33%)
  starting transfers between devices  41.6 us (22%)
  local copies, waits for them, and re-layouts  2.82 us (2%)
    ppermute x24, waiting for transfers between devices, send(): return lax.ppermute(x, 'filt', pairs)  49.2 us
    pallas_call x5, Pallas kernels, forward(): pl.pallas_call(functools.partial(forward_kernel, counts, places, rim_plac...  27.6 us
    ppermute x24, starting transfers between devices, send(): return lax.ppermute(x, 'filt', pairs)  25.9 us
    pallas_call x3, Pallas kernels, filter_terms(): pl.pallas_call(functools.partial(filter_kernel, tap), grid_spec=pltpu.Pre...  13.3 us
    ppermute x9, waiting for transfers between devices, swap(): return lax.ppermute(x, 'slab', [(i, i ^ bit) for i in range(slabs)])  12.2 us
    pallas_call x2, Pallas kernels, inner_terms(): pl.pallas_call(functools.partial(inner_kernel, begin, planes), out_shape=...  12.1 us
    ppermute x5, starting transfers between devices, shards(): lax.ppermute(top, 'slab', shallower)  8.64 us
    pallas_call x1, Pallas kernels, prepare(): pl.pallas_call(functools.partial(prepare_kernel, chan), grid=(channels //...  7.38 us
  transfers between devices with their start and end apart: 45, of which 10 were waited for; matrix products, arithmetic and copies ran while one was open for 1% of the time, Pallas kernels for 33%

commit v1 on v0

--- a/solution.py
+++ b/solution.py
@@ -131,11 +131,6 @@
             row = term if row is None else row + term
         rows.append(moved(row, b - 1, 0))
     return rows[0] + rows[1] + rows[2]
-
-
-def tripled(x):
-    high, low = parts_of(x)
-    return jnp.concatenate([high, high, low], axis=0)
 
 
 def forward_kernel(counts, places, rim_places, first, ring, *refs):
@@ -277,31 +272,36 @@
     )(ring, *args)
 
 
-def middle_kernel(chan, ring, total, grad, below, above, source, *refs):
+def middle_kernel(places, ring, total, grad, below, above, source, *refs):
     active_out, spread_out, high_all, low_all, high_rim, low_rim, weights, sems, fetch_sems = refs[2:]
     depth, out_rows, area = total.shape
+    chan = below.shape[0] // len(places)
     copies = []
     rim_sums = []
-    opposite = ring[high_all.shape[0] // chan // 2]
-    fetches = [
-        pltpu.make_async_copy(source.at[2 * n, opposite], weights.at[n], fetch_sems.at[n])
-        for n in range(2)
-    ]
-    for fetch in fetches:
-        fetch.start()
+    fetches = {}
+    for n in range(2):
+        for k, place in enumerate(places):
+            fetches[n, k] = pltpu.make_async_copy(
+                source.at[2 * n, ring[place]], weights.at[n, k], fetch_sems.at[n, k]
+            )
+            fetches[n, k].start()
     for n, rim in enumerate((below, above)):
-        value = beside(ring, n, rim[...])
-        high, low = parts_of(value)
-        high_rim[n] = high
-        low_rim[n] = low
-        at = pl.ds(pl.multiple_of(opposite * chan, chan), chan)
-        lanes = pl.ds(n * (depth + 1) * area, area)
-        for m, (part, target) in enumerate(((high_rim, high_all), (low_rim, low_all))):
-            copy = pltpu.make_async_copy(part.at[n], target.at[at, lanes], sems.at[n, m])
-            copy.start()
-            copies.append(copy)
-        fetches[n].wait()
-        rim_sums.append(gathered(dot(weights[n], tripled(value)), out_rows))
+        answer = None
+        for k, place in enumerate(places):
+            value = beside(ring, n, rim[k * chan : (k + 1) * chan])
+            high, low = parts_of(value)
+            high_rim[n, k] = high
+            low_rim[n, k] = low
+            at = pl.ds(pl.multiple_of(ring[place] * chan, chan), chan)
+            lanes = pl.ds(n * (depth + 1) * area, area)
+            for m, (part, target) in enumerate(((high_rim, high_all), (low_rim, low_all))):
+                copy = pltpu.make_async_copy(part.at[n, k], target.at[at, lanes], sems.at[n, k, m])
+                copy.start()
+                copies.append(copy)
+            fetches[n, k].wait()
+            term = dot(weights[n, k], jnp.concatenate([high, high, low], axis=0))
+            answer = term if answer is None else answer + term
+        rim_sums.append(gathered(answer, out_rows))
     positives = []
     for plane in range(depth):
         value = total[plane]
@@ -330,12 +330,12 @@
         copy.wait()
 
 
-def middle(ring, carry, grad, outer, weights, chan):
+def middle(ring, carry, grad, places, outer, weights, chan):
     total, high_all, low_all = carry
     depth, out_rows, area = total.shape
     keep = pl.BlockSpec(memory_space=pltpu.HBM)
     return pl.pallas_call(
-        functools.partial(middle_kernel, chan),
+        functools.partial(middle_kernel, places),
         grid_spec=pltpu.PrefetchScalarGridSpec(
             num_scalar_prefetch=1,
             grid=(1,),
@@ -348,11 +348,11 @@
                 keep,
             ],
             scratch_shapes=[
-                pltpu.VMEM((2, chan, area), bf16),
-                pltpu.VMEM((2, chan, area), bf16),
-                pltpu.VMEM((2,) + weights.shape[2:], bf16),
-                pltpu.SemaphoreType.DMA((2, 2)),
-                pltpu.SemaphoreType.DMA((2,)),
+                pltpu.VMEM((2, len(places), chan, area), bf16),
+                pltpu.VMEM((2, len(places), chan, area), bf16),
+                pltpu.VMEM((2, len(places)) + weights.shape[2:], bf16),
+                pltpu.SemaphoreType.DMA((2, len(places), 2)),
+                pltpu.SemaphoreType.DMA((2, len(places))),
             ],
         ),
         out_shape=[
@@ -590,6 +590,7 @@
     carry = None
     up = down = volume
     rim_places, outer = (), None
+    held, held_places = [], ()
     for step in range(half + 1):
         if step == 0:
             sets, places = [[volume]], (0,)
@@ -600,16 +601,22 @@
             up = send(up[: chan // 2], ring_up)
             down = send(down[chan // 2 :], ring_down)
             sets, places = [[up, down]], (half,)
-        last, top = rims([b for blocks in sets for b in blocks])
+        held += [b for blocks in sets for b in blocks]
+        held_places += places
         carry = forward(ring, sets, places, rim_places, outer, ahead, carry, sizes)
-        outer = lax.ppermute(last, "slab", deeper), lax.ppermute(top, "slab", shallower)
-        rim_places = places
-
-    activated, spread, high_field, low_field = middle(ring, carry, out_grad, outer, ahead, chan)
+        rim_places, outer = (), None
+        if step not in (0, half - 1):
+            last, top = rims(held)
+            outer = lax.ppermute(last, "slab", deeper), lax.ppermute(top, "slab", shallower)
+            rim_places, held, held_places = held_places, [], ()
+
+    activated, spread, high_field, low_field = middle(
+        ring, carry, out_grad, rim_places, outer, ahead, chan
+    )
 
     below, above = outer_terms(spread, back_high, back_low, chan)
+    from_below = lax.ppermute(above, "slab", deeper)
     from_above = lax.ppermute(below, "slab", shallower)
-    from_below = lax.ppermute(above, "slab", deeper)
     run = depth // 2
     inner = []
     for c in range(2):

time: 187 us -> 183 us (0.979)
  starting transfers between devices: 41.6 us -> 38 us
    ppermute x5 -> x3, starting transfers between devices: 8.64 us -> 5.19 us  [shards(): lax.ppermute(top, 'slab', shallower)]
  transfers between devices with their start and end apart: 45 -> 41, of which waited for: 10 -> 10; matrix products, arithmetic and copies ran while one was open for 1% -> 1% of each run, Pallas kernels for 33% -> 34%
where the time goes in v1:
time: 183 us; the launch traced here: 182 us
  Pallas kernels  79.2 us (43%)
  waiting for transfers between devices  61.6 us (34%)
  starting transfers between devices  38 us (21%)
    ppermute x24, waiting for transfers between devices, send(): return lax.ppermute(x, 'filt', pairs)  49.2 us
    pallas_call x5, Pallas kernels, forward(): pl.pallas_call(functools.partial(forward_kernel, counts, places, rim_plac...  27 us
    ppermute x24, starting transfers between devices, send(): return lax.ppermute(x, 'filt', pairs)  25.9 us
    pallas_call x3, Pallas kernels, filter_terms(): pl.pallas_call(functools.partial(filter_kernel, tap), grid_spec=pltpu.Pre...  13.3 us
    ppermute x9, waiting for transfers between devices, swap(): return lax.ppermute(x, 'slab', [(i, i ^ bit) for i in range(slabs)])  12.3 us
    pallas_call x2, Pallas kernels, inner_terms(): pl.pallas_call(functools.partial(inner_kernel, begin, planes), out_shape=...  12.1 us
    pallas_call x1, Pallas kernels, prepare(): pl.pallas_call(functools.partial(prepare_kernel, chan), grid=(channels //...  7.36 us
    pallas_call x9, Pallas kernels, summed(): pl.pallas_call(kernel, grid_spec=pltpu.PrefetchScalarGridSpec(num_scalar_...  6.34 us
  transfers between devices with their start and end apart: 41, of which 10 were waited for; matrix products, arithmetic and copies ran while one was open for 1% of the time, Pallas kernels for 34%

profile of v1, /device:TPU:0, one launch (start us, length us, event | category | flops | bytes accessed | tf_op | source)
XLA Modules:
  0.0 182.3 jit_solution(13422431915415264124)
XLA Ops:
  0.6 3.0 %collective-permute-start.4 = (f32[64,8,256]{2,1,0:T(8,128)}, f32[64,8,256]{2,1,0:T(8,128)S(1)}, u32[]{:S(2)}, u32[]{:S(2)}) collective-permute-start(f32[64,8,256]{2,1,0:T(8,128)} %refs_0_.3), channel_id=1, source_target_pairs={{2,0},{4,2},{6,4},{7,6},{5,7},{3,5},{1,3},{0,1},{10,8},{12,10},{14... | collective-permute-start | bytes 1572872 | tf_op jit(solution)/shard_map/ppermute | solution.py:581
  3.8 12.1 %collective-permute-done.4.refs_2_.refs_1_ = f32[64,8,256]{2,1,0:T(8,128)S(1)} collective-permute-done((f32[64,8,256]{2,1,0:T(8,128)}, f32[64,8,256]{2,1,0:T(8,128)S(1)}, u32[]{:S(2)}, u32[]{:S(2)}) %collective-permute-start.4) | collective-permute-done | bytes 524320 | tf_op jit(solution)/shard_map/ppermute | solution.py:581
  15.9 1.7 collective-permute-start.5
  17.9 11.1 %collective-permute-done.5.refs_1_ = f32[64,8,256]{2,1,0:T(8,128)S(1)} collective-permute-done((f32[64,8,256]{2,1,0:T(8,128)S(1)}, f32[64,8,256]{2,1,0:T(8,128)S(1)}, u32[]{:S(2)}, u32[]{:S(2)}) %collective-permute-start.5) | collective-permute-done | bytes 524320 | tf_op jit(solution)/shard_map/ppermute | solution.py:581
  31.0 7.4 %prepare.1 = (bf16[3,8,576,192]{3,2,1,0:T(8,128)(2,1)}, bf16[512,1728]{1,0:T(8,128)(2,1)}, bf16[512,1728]{1,0:T(8,128)(2,1)}) custom-call(f32[27,64,512]{2,1,0:T(8,128)} %filters.1), custom_call_target="tpu_custom_call" | custom-call | bytes 17694720 | tf_op jit(solution)/shard_map/prepare/pallas_call | solution.py:82
  40.1 3.9 %forward.5 = (f32[8,64,256]{2,1,0:T(8,128)S(1)}, bf16[512,2560]{1,0:T(8,128)(2,1)S(1)}, bf16[512,2560]{1,0:T(8,128)(2,1)S(1)}) custom-call(s32[11]{0:T(128)S(1)} %dynamic-slice_bitcast_fusion.ring, f32[64,8,256]{2,1,0:T(8,128)S(1)} %copy-done, bf16[3,8,576,192]{3,2,1,0:T(8,128)(2,1)} %get-tuple-element.55.refs_1_.refs_2_.source), custom_call_target="tpu_custom_call" | custom-call | flops 1358954496 | bytes 1310720 | tf_op jit(solution)/shard_map/forward/pallas_call | solution.py:242
  44.2 1.7 collective-permute-start.11
  48.1 5.8 %forward.6 = (f32[8,64,256]{2,1,0:T(8,128)S(1)}, bf16[512,2560]{1,0:T(8,128)(2,1)S(1)}, bf16[512,2560]{1,0:T(8,128)(2,1)S(1)}) custom-call(s32[11]{0:T(128)S(1)} %dynamic-slice_bitcast_fusion.ring, f32[64,8,256]{2,1,0:T(8,128)S(1)} %collective-permute-done.refs_1_.refs_0_, ...), custom_call_target="tpu_custom_call", output_to_operand_aliasing={{0}: (4, {}), {1}: (5, {}), {2}: (6, {})} | custom-call | flops 2717908992 | bytes 2621440 | tf_op jit(solution)/shard_map/forward/pallas_call | solution.py:242
  54.2 1.7 collective-permute-start.9
  55.9 6.9 %forward.7 = (f32[8,64,256]{2,1,0:T(8,128)S(1)}, bf16[512,2560]{1,0:T(8,128)(2,1)S(1)}, bf16[512,2560]{1,0:T(8,128)(2,1)S(1)}) custom-call(s32[11]{0:T(128)S(1)} %dynamic-slice_bitcast_fusion.ring, f32[64,8,256]{2,1,0:T(8,128)S(1)} %collective-permute-done.1.refs_0_, ...), custom_call_target="tpu_custom_call", output_to_operand_aliasing={{0}: (6, {}), {1}: (7, {}), {2}: (8, {})} | custom-call | flops 2717908992 | bytes 2621440 | tf_op jit(solution)/shard_map/forward/pallas_call | solution.py:242
  63.1 1.7 collective-permute-start.13
  64.9 6.5 %forward.8 = (f32[8,64,256]{2,1,0:T(8,128)S(1)}, bf16[512,2560]{1,0:T(8,128)(2,1)S(1)}, bf16[512,2560]{1,0:T(8,128)(2,1)S(1)}) custom-call(s32[11]{0:T(128)S(1)} %dynamic-slice_bitcast_fusion.ring, f32[64,8,256]{2,1,0:T(8,128)S(1)} %collective-permute-done.2.refs_0_, ...), custom_call_target="tpu_custom_call", output_to_operand_aliasing={{0}: (6, {}), {1}: (7, {}), {2}: (8, {})} | custom-call | flops 2717908992 | bytes 2621440 | tf_op jit(solution)/shard_map/forward/pallas_call | solution.py:242
  71.4 3.9 %forward.9 = (f32[8,64,256]{2,1,0:T(8,128)S(1)}, bf16[512,2560]{1,0:T(8,128)(2,1)S(1)}, bf16[512,2560]{1,0:T(8,128)(2,1)S(1)}) custom-call(s32[11]{0:T(128)S(1)} %dynamic-slice_bitcast_fusion.ring, f32[32,8,256]{2,1,0:T(8,128)S(1)} %collective-permute-done.3.refs_0_.refs_2_, ...), custom_call_target="tpu_custom_call", output_to_operand_aliasing={{0}: (4, {}), {1}: (5, {}), {2}: (6, {})} | custom-call | flops 1358954496 | bytes 1310720 | tf_op jit(solution)/shard_map/forward/pallas_call | solution.py:242
  75.3 6.2 %middle.1 = (f32[64,8,256]{2,1,0:T(8,128)}, bf16[2,10,576,256]{3,2,1,0:T(8,128)(2,1)S(1)}, bf16[512,2560]{1,0:T(8,128)(2,1)S(1)}, bf16[512,2560]{1,0:T(8,128)(2,1)S(1)}) custom-call(s32[11]{0:T(128)S(1)} %dynamic-slice_bitcast_fusion.ring, f32[8,64,256]{2,1,0:T(8,128)S(1)} %get-tuple-element.72.total, ...), custom_call_target="tpu_custom_call", output_to_operand_aliasing={{2}: (6, {}), {3}: (7, {})} | custom-call | bytes 9437184 | tf_op jit(solution)/shard_map/middle/pallas_call | solution.py:337
  81.5 4.4 %filter_terms.5 = (f32[288,512]{1,0:T(8,128)S(1)}, f32[288,512]{1,0:T(8,128)S(1)}) custom-call(s32[11]{0:T(128)S(1)} %dynamic-slice_bitcast_fusion.ring, bf16[2,10,576,256]{3,2,1,0:T(8,128)(2,1)S(1)} %get-tuple-element.78.spread, bf16[512,2560]{1,0:T(8,128)(2,1)S(1)} %get-tuple-element.99.high, bf16[512,2560]{1,0:T(8,128)(2,1)S(1)} %get-tuple-element.100.low), custom_call_target="tpu_custom_call" | custom-call | flops 4529848320 | bytes 11141120 | tf_op jit(solution)/shard_map/filter_terms/pallas_call | solution.py:448
  86.0 4.5 %filter_terms.4 = (f32[288,512]{1,0:T(8,128)S(1)}, f32[288,512]{1,0:T(8,128)S(1)}) custom-call(s32[11]{0:T(128)S(1)} %dynamic-slice_bitcast_fusion.ring, bf16[2,10,576,256]{3,2,1,0:T(8,128)(2,1)S(1)} %get-tuple-element.78.spread, bf16[512,2560]{1,0:T(8,128)(2,1)S(1)} %get-tuple-element.99.high, bf16[512,2560]{1,0:T(8,128)(2,1)S(1)} %get-tuple-element.100.low), custom_call_target="tpu_custom_call" | custom-call | flops 4529848320 | bytes 11141120 | tf_op jit(solution)/shard_map/filter_terms/pallas_call | solution.py:448
  91.9 1.7 collective-permute-start.23
  93.6 4.4 %filter_terms.3 = (f32[288,512]{1,0:T(8,128)S(1)}, f32[288,512]{1,0:T(8,128)S(1)}) custom-call(s32[11]{0:T(128)S(1)} %dynamic-slice_bitcast_fusion.ring, bf16[2,10,576,256]{3,2,1,0:T(8,128)(2,1)S(1)} %get-tuple-element.78.spread, bf16[512,2560]{1,0:T(8,128)(2,1)S(1)} %get-tuple-element.99.high, bf16[512,2560]{1,0:T(8,128)(2,1)S(1)} %get-tuple-element.100.low), custom_call_target="tpu_custom_call" | custom-call | flops 4529848320 | bytes 11141120 | tf_op jit(solution)/shard_map/filter_terms/pallas_call | solution.py:448
  98.7 6.1 %inner_terms.3.inner.up_inner.down_inner.refs_4_ = f32[8,64,1024]{2,1,0:T(8,128)S(1)} custom-call(bf16[2,10,576,256]{3,2,1,0:T(8,128)(2,1)S(1)} %get-tuple-element.78.spread, bf16[512,1728]{1,0:T(8,128)(2,1)S(1)} %copy-done.1, bf16[512,1728]{1,0:T(8,128)(2,1)S(1)} %copy-done.2), custom_call_target="tpu_custom_call" | custom-call | flops 5435817984 | bytes 9437184 | tf_op jit(solution)/shard_map/inner_terms/pallas_call | solution.py:402
  105.6 1.6 collective-permute-start.24
  107.7 6.1 %inner_terms.2.inner.up_inner.down_inner.refs_0_ = f32[8,64,1024]{2,1,0:T(8,128)S(1)} custom-call(bf16[2,10,576,256]{3,2,1,0:T(8,128)(2,1)S(1)} %get-tuple-element.78.spread, bf16[512,1728]{1,0:T(8,128)(2,1)S(1)} %copy-done.1, bf16[512,1728]{1,0:T(8,128)(2,1)S(1)} %copy-done.2), custom_call_target="tpu_custom_call" | custom-call | flops 5435817984 | bytes 9437184 | tf_op jit(solution)/shard_map/inner_terms/pallas_call | solution.py:402
  114.4 1.6 collective-permute-start.15
  119.0 1.6 collective-permute-start.26
  121.6 9.1 %collective-permute-done.16.down = f32[32,1024]{1,0:T(8,128)S(1)} collective-permute-done((f32[32,1024]{1,0:T(8,128)S(1)}, f32[32,1024]{1,0:T(8,128)S(1)}, u32[]{:S(2)}, u32[]{:S(2)}) %collective-permute-start.16) | collective-permute-done | bytes 131104 | tf_op jit(solution)/shard_map/ppermute | solution.py:581
  135.6 3.9 %collective-permute-done.17.up = f32[64,1024]{1,0:T(8,128)S(1)} collective-permute-done((f32[64,1024]{1,0:T(8,128)S(1)}, f32[64,1024]{1,0:T(8,128)S(1)}, u32[]{:S(2)}, u32[]{:S(2)}) %collective-permute-start.17) | collective-permute-done | bytes 262176 | tf_op jit(solution)/shard_map/ppermute | solution.py:581
  145.7 11.0 %collective-permute-done.33 = f32[288,512]{1,0:T(8,128)S(1)} collective-permute-done((f32[288,512]{1,0:T(8,128)S(1)}, f32[288,512]{1,0:T(8,128)S(1)}, u32[]{:S(2)}, u32[]{:S(2)}) %collective-permute-start.33) | collective-permute-done | bytes 589856 | tf_op jit(solution)/shard_map/ppermute | solution.py:629
  158.0 1.6 collective-permute-start.30
  160.8 6.0 %collective-permute-done.30.refs_6_ = f32[64,1024]{1,0:T(8,128)S(1)} collective-permute-done((f32[64,1024]{1,0:T(8,128)S(1)}, f32[64,1024]{1,0:T(8,128)S(1)}, u32[]{:S(2)}, u32[]{:S(2)}) %collective-permute-start.30) | collective-permute-done | bytes 262176 | tf_op jit(solution)/shard_map/ppermute | solution.py:581
  168.8 5.7 %collective-permute-done.21.refs_2_ = f32[64,1024]{1,0:T(8,128)S(1)} collective-permute-done((f32[64,1024]{1,0:T(8,128)S(1)}, f32[64,1024]{1,0:T(8,128)S(1)}, u32[]{:S(2)}, u32[]{:S(2)}) %collective-permute-start.21) | collective-permute-done | bytes 262176 | tf_op jit(solution)/shard_map/ppermute | solution.py:581
  177.3 1.7 place.3.refs_2_
  178.9 1.7 place.4.refs_2_
  180.6 1.7 place.5
  (95 shorter events, 33.4 us)
Async XLA Ops:
  0.6 15.2 %collective-permute-start.4 = (f32[64,8,256]{2,1,0:T(8,128)}, f32[64,8,256]{2,1,0:T(8,128)S(1)}, u32[]{:S(2)}, u32[]{:S(2)}) collective-permute-start(f32[64,8,256]{2,1,0:T(8,128)} %refs_0_.3), channel_id=1, source_target_pairs={{2,0},{4,2},{6,4},{7,6},{5,7},{3,5},{1,3},{0,1},{10,8},{12,10},{14... | collective-permute-start | bytes 1572872 | tf_op jit(solution)/shard_map/ppermute | solution.py:581
  3.6 13.9 %collective-permute-start = (f32[64,8,256]{2,1,0:T(8,128)}, f32[64,8,256]{2,1,0:T(8,128)S(1)}, u32[]{:S(2)}, u32[]{:S(2)}) collective-permute-start(f32[64,8,256]{2,1,0:T(8,128)} %refs_0_.3), channel_id=1, source_target_pairs={{0,2},{2,4},{4,6},{6,7},{7,5},{5,3},{3,1},{1,0},{8,10},{10,12},{12... | collective-permute-start | bytes 1572872 | tf_op jit(solution)/shard_map/ppermute | solution.py:581
  15.9 13.1 %collective-permute-start.5 = (f32[64,8,256]{2,1,0:T(8,128)S(1)}, f32[64,8,256]{2,1,0:T(8,128)S(1)}, u32[]{:S(2)}, u32[]{:S(2)}) collective-permute-start(f32[64,8,256]{2,1,0:T(8,128)S(1)} %collective-permute-done.4.refs_2_.refs_1_), channel_id=1, source_target_pairs={{2,0},{4,2},{6,4},{7,6},{5,7},{3,5},{1,3},{0,1},{10,8},{12,10},{14... | collective-permute-start | bytes 1572872 | tf_op jit(solution)/shard_map/ppermute | solution.py:581
  17.5 12.8 %collective-permute-start.1 = (f32[64,8,256]{2,1,0:T(8,128)S(1)}, f32[64,8,256]{2,1,0:T(8,128)S(1)}, u32[]{:S(2)}, u32[]{:S(2)}) collective-permute-start(f32[64,8,256]{2,1,0:T(8,128)S(1)} %collective-permute-done.refs_1_.refs_0_), channel_id=1, source_target_pairs={{0,2},{2,4},{4,6},{6,7},{7,5},{5,3},{3,1},{1,0},{8,10},{10,12},{12... | collective-permute-start | bytes 1572872 | tf_op jit(solution)/shard_map/ppermute | solution.py:581
  29.0 17.0 %collective-permute-start.6 = (f32[64,8,256]{2,1,0:T(8,128)S(1)}, f32[64,8,256]{2,1,0:T(8,128)S(1)}, u32[]{:S(2)}, u32[]{:S(2)}) collective-permute-start(f32[64,8,256]{2,1,0:T(8,128)S(1)} %collective-permute-done.5.refs_1_), channel_id=1, source_target_pairs={{2,0},{4,2},{6,4},{7,6},{5,7},{3,5},{1,3},{0,1},{10,8},{12,10},{14... | collective-permute-start | bytes 1572872 | tf_op jit(solution)/shard_map/ppermute | solution.py:581
  30.3 17.1 %collective-permute-start.2 = (f32[64,8,256]{2,1,0:T(8,128)S(1)}, f32[64,8,256]{2,1,0:T(8,128)S(1)}, u32[]{:S(2)}, u32[]{:S(2)}) collective-permute-start(f32[64,8,256]{2,1,0:T(8,128)S(1)} %collective-permute-done.1.refs_0_), channel_id=1, source_target_pairs={{0,2},{2,4},{4,6},{6,7},{7,5},{5,3},{3,1},{1,0},{8,10},{10,12},{12... | collective-permute-start | bytes 1572872 | tf_op jit(solution)/shard_map/ppermute | solution.py:581
  44.2 11.7 %collective-permute-start.11 = (f32[192,256]{1,0:T(8,128)S(1)}, f32[192,256]{1,0:T(8,128)S(1)}, u32[]{:S(2)}, u32[]{:S(2)}) collective-permute-start(f32[192,256]{1,0:T(8,128)S(1)} %get-tuple-element.59), channel_id=1, source_target_pairs={{8,0},{16,8},{24,16},{0,24},{9,1},{17,9},{25,17},{1,25},{10,2},{18... | collective-permute-start | bytes 589832 | tf_op jit(solution)/shard_map/ppermute | solution.py:610
  46.0 16.9 %collective-permute-start.7 = (f32[32,8,256]{2,1,0:T(8,128)S(1)}, f32[32,8,256]{2,1,0:T(8,128)S(1)}, u32[]{:S(2)}, u32[]{:S(2)}) collective-permute-start(f32[32,8,256]{2,1,0:T(8,128)S(1)} %slice.9), channel_id=1, source_target_pairs={{2,0},{4,2},{6,4},{7,6},{5,7},{3,5},{1,3},{0,1},{10,8},{12,10},{14... | collective-permute-start | bytes 786440 | tf_op jit(solution)/shard_map/ppermute | solution.py:581
  47.4 15.4 %collective-permute-start.3 = (f32[32,8,256]{2,1,0:T(8,128)S(1)}, f32[32,8,256]{2,1,0:T(8,128)S(1)}, u32[]{:S(2)}, u32[]{:S(2)}) collective-permute-start(f32[32,8,256]{2,1,0:T(8,128)S(1)} %slice.8), channel_id=1, source_target_pairs={{0,2},{2,4},{4,6},{6,7},{7,5},{5,3},{3,1},{1,0},{8,10},{10,12},{12... | collective-permute-start | bytes 786440 | tf_op jit(solution)/shard_map/ppermute | solution.py:581
  54.1 10.8 %collective-permute-start.8 = (f32[128,256]{1,0:T(8,128)S(1)}, f32[128,256]{1,0:T(8,128)S(1)}, u32[]{:S(2)}, u32[]{:S(2)}) collective-permute-start(f32[128,256]{1,0:T(8,128)S(1)} %get-tuple-element.56), channel_id=1, source_target_pairs={{0,8},{8,16},{16,24},{24,0},{1,9},{9,17},{17,25},{25,1},{2,10},{10... | collective-permute-start | bytes 393224 | tf_op jit(solution)/shard_map/ppermute | solution.py:610
  54.2 10.7 %collective-permute-start.9 = (f32[128,256]{1,0:T(8,128)S(1)}, f32[128,256]{1,0:T(8,128)S(1)}, u32[]{:S(2)}, u32[]{:S(2)}) collective-permute-start(f32[128,256]{1,0:T(8,128)S(1)} %get-tuple-element.57), channel_id=1, source_target_pairs={{8,0},{16,8},{24,16},{0,24},{9,1},{17,9},{25,17},{1,25},{10,2},{18... | collective-permute-start | bytes 393224 | tf_op jit(solution)/shard_map/ppermute | solution.py:610
  63.1 12.2 %collective-permute-start.12 = (f32[192,256]{1,0:T(8,128)S(1)}, f32[192,256]{1,0:T(8,128)S(1)}, u32[]{:S(2)}, u32[]{:S(2)}) collective-permute-start(f32[192,256]{1,0:T(8,128)S(1)} %get-tuple-element.73), channel_id=1, source_target_pairs={{0,8},{8,16},{16,24},{24,0},{1,9},{9,17},{17,25},{25,1},{2,10},{10... | collective-permute-start | bytes 589832 | tf_op jit(solution)/shard_map/ppermute | solution.py:610
  63.1 12.2 %collective-permute-start.13 = (f32[192,256]{1,0:T(8,128)S(1)}, f32[192,256]{1,0:T(8,128)S(1)}, u32[]{:S(2)}, u32[]{:S(2)}) collective-permute-start(f32[192,256]{1,0:T(8,128)S(1)} %get-tuple-element.74), channel_id=1, source_target_pairs={{8,0},{16,8},{24,16},{0,24},{9,1},{17,9},{25,17},{1,25},{10,2},{18... | collective-permute-start | bytes 589832 | tf_op jit(solution)/shard_map/ppermute | solution.py:610
  91.8 15.4 %collective-permute-start.14 = (f32[8,64,256]{2,1,0:T(8,128)S(1)}, f32[8,64,256]{2,1,0:T(8,128)S(1)}, u32[]{:S(2)}, u32[]{:S(2)}) collective-permute-start(f32[8,64,256]{2,1,0:T(8,128)S(1)} %get-tuple-element.81), channel_id=1, source_target_pairs={{0,8},{8,16},{16,24},{24,0},{1,9},{9,17},{17,25},{25,1},{2,10},{10... | collective-permute-start | bytes 1572872 | tf_op jit(solution)/shard_map/ppermute | solution.py:618
  91.9 13.1 %collective-permute-start.23 = (f32[8,64,256]{2,1,0:T(8,128)S(1)}, f32[8,64,256]{2,1,0:T(8,128)S(1)}, u32[]{:S(2)}, u32[]{:S(2)}) collective-permute-start(f32[8,64,256]{2,1,0:T(8,128)S(1)} %get-tuple-element.90), channel_id=1, source_target_pairs={{8,0},{16,8},{24,16},{0,24},{9,1},{17,9},{25,17},{1,25},{10,2},{18... | collective-permute-start | bytes 1572872 | tf_op jit(solution)/shard_map/ppermute | solution.py:619
  98.1 16.3 %collective-permute-start.38 = (f32[288,512]{1,0:T(8,128)S(1)}, f32[288,512]{1,0:T(8,128)S(1)}, u32[]{:S(2)}, u32[]{:S(2)}) collective-permute-start(f32[288,512]{1,0:T(8,128)S(1)} %get-tuple-element.106), channel_id=1, source_target_pairs={{0,8},{8,0},{16,24},{24,16},{1,9},{9,1},{17,25},{25,17},{2,10},{10... | collective-permute-start | bytes 1769480 | tf_op jit(solution)/shard_map/ppermute | solution.py:629
  98.2 17.9 %collective-permute-start.35 = (f32[288,512]{1,0:T(8,128)S(1)}, f32[288,512]{1,0:T(8,128)S(1)}, u32[]{:S(2)}, u32[]{:S(2)}) collective-permute-start(f32[288,512]{1,0:T(8,128)S(1)} %get-tuple-element.104), channel_id=1, source_target_pairs={{0,8},{8,0},{16,24},{24,16},{1,9},{9,1},{17,25},{25,17},{2,10},{10... | collective-permute-start | bytes 1769480 | tf_op jit(solution)/shard_map/ppermute | solution.py:629
  98.7 21.9 %collective-permute-start.32 = (f32[288,512]{1,0:T(8,128)S(1)}, f32[288,512]{1,0:T(8,128)S(1)}, u32[]{:S(2)}, u32[]{:S(2)}) collective-permute-start(f32[288,512]{1,0:T(8,128)S(1)} %get-tuple-element.102), channel_id=1, source_target_pairs={{0,8},{8,0},{16,24},{24,16},{1,9},{9,1},{17,25},{25,17},{2,10},{10... | collective-permute-start | bytes 1769480 | tf_op jit(solution)/shard_map/ppermute | solution.py:629
  105.6 11.9 %collective-permute-start.24 = (f32[32,1024]{1,0:T(8,128)S(1)}, f32[32,1024]{1,0:T(8,128)S(1)}, u32[]{:S(2)}, u32[]{:S(2)}) collective-permute-start(f32[32,1024]{1,0:T(8,128)S(1)} %get-tuple-element.91), channel_id=1, source_target_pairs={{0,2},{2,4},{4,6},{6,7},{7,5},{5,3},{3,1},{1,0},{8,10},{10,12},{12... | collective-permute-start | bytes 393224 | tf_op jit(solution)/shard_map/ppermute | solution.py:581
  107.2 11.1 %collective-permute-start.25 = (f32[32,1024]{1,0:T(8,128)S(1)}, f32[32,1024]{1,0:T(8,128)S(1)}, u32[]{:S(2)}, u32[]{:S(2)}) collective-permute-start(f32[32,1024]{1,0:T(8,128)S(1)} %get-tuple-element.92), channel_id=1, source_target_pairs={{2,0},{4,2},{6,4},{7,6},{5,7},{3,5},{1,3},{0,1},{10,8},{12,10},{14... | collective-permute-start | bytes 393224 | tf_op jit(solution)/shard_map/ppermute | solution.py:581
  116.1 26.0 %collective-permute-start.39 = (f32[288,512]{1,0:T(8,128)S(1)}, f32[288,512]{1,0:T(8,128)S(1)}, u32[]{:S(2)}, u32[]{:S(2)}) collective-permute-start(f32[288,512]{1,0:T(8,128)S(1)} %add.31), channel_id=1, source_target_pairs={{0,16},{8,24},{16,0},{24,8},{1,17},{9,25},{17,1},{25,9},{2,18},{10... | collective-permute-start | bytes 1769480 | tf_op jit(solution)/shard_map/ppermute | solution.py:629
  117.5 27.5 %collective-permute-start.36 = (f32[288,512]{1,0:T(8,128)S(1)}, f32[288,512]{1,0:T(8,128)S(1)}, u32[]{:S(2)}, u32[]{:S(2)}) collective-permute-start(f32[288,512]{1,0:T(8,128)S(1)} %add.29), channel_id=1, source_target_pairs={{0,16},{8,24},{16,0},{24,8},{1,17},{9,25},{17,1},{25,9},{2,18},{10... | collective-permute-start | bytes 1769480 | tf_op jit(solution)/shard_map/ppermute | solution.py:629
  119.0 13.9 %collective-permute-start.26 = (f32[64,1024]{1,0:T(8,128)S(1)}, f32[64,1024]{1,0:T(8,128)S(1)}, u32[]{:S(2)}, u32[]{:S(2)}) collective-permute-start(f32[64,1024]{1,0:T(8,128)S(1)} %get-tuple-element.93), channel_id=1, source_target_pairs={{0,2},{2,4},{4,6},{6,7},{7,5},{5,3},{3,1},{1,0},{8,10},{10,12},{12... | collective-permute-start | bytes 786440 | tf_op jit(solution)/shard_map/ppermute | solution.py:581
  120.6 13.9 %collective-permute-start.27 = (f32[64,1024]{1,0:T(8,128)S(1)}, f32[64,1024]{1,0:T(8,128)S(1)}, u32[]{:S(2)}, u32[]{:S(2)}) collective-permute-start(f32[64,1024]{1,0:T(8,128)S(1)} %get-tuple-element.94), channel_id=1, source_target_pairs={{2,0},{4,2},{6,4},{7,6},{5,7},{3,5},{1,3},{0,1},{10,8},{12,10},{14... | collective-permute-start | bytes 786440 | tf_op jit(solution)/shard_map/ppermute | solution.py:581
  130.7 25.9 %collective-permute-start.33 = (f32[288,512]{1,0:T(8,128)S(1)}, f32[288,512]{1,0:T(8,128)S(1)}, u32[]{:S(2)}, u32[]{:S(2)}) collective-permute-start(f32[288,512]{1,0:T(8,128)S(1)} %add.27), channel_id=1, source_target_pairs={{0,16},{8,24},{16,0},{24,8},{1,17},{9,25},{17,1},{25,9},{2,18},{10... | collective-permute-start | bytes 1769480 | tf_op jit(solution)/shard_map/ppermute | solution.py:629
  139.4 17.3 %collective-permute-start.28 = (f32[64,1024]{1,0:T(8,128)S(1)}, f32[64,1024]{1,0:T(8,128)S(1)}, u32[]{:S(2)}, u32[]{:S(2)}) collective-permute-start(f32[64,1024]{1,0:T(8,128)S(1)} %get-tuple-element.95), channel_id=1, source_target_pairs={{0,2},{2,4},{4,6},{6,7},{7,5},{5,3},{3,1},{1,0},{8,10},{10,12},{12... | collective-permute-start | bytes 786440 | tf_op jit(solution)/shard_map/ppermute | solution.py:581
  141.0 16.3 %collective-permute-start.29 = (f32[64,1024]{1,0:T(8,128)S(1)}, f32[64,1024]{1,0:T(8,128)S(1)}, u32[]{:S(2)}, u32[]{:S(2)}) collective-permute-start(f32[64,1024]{1,0:T(8,128)S(1)} %get-tuple-element.96), channel_id=1, source_target_pairs={{2,0},{4,2},{6,4},{7,6},{5,7},{3,5},{1,3},{0,1},{10,8},{12,10},{14... | collective-permute-start | bytes 786440 | tf_op jit(solution)/shard_map/ppermute | solution.py:581
  142.1 15.9 %collective-permute-start.19 = (f32[64,1024]{1,0:T(8,128)S(1)}, f32[64,1024]{1,0:T(8,128)S(1)}, u32[]{:S(2)}, u32[]{:S(2)}) collective-permute-start(f32[64,1024]{1,0:T(8,128)S(1)} %get-tuple-element.86), channel_id=1, source_target_pairs={{0,2},{2,4},{4,6},{6,7},{7,5},{5,3},{3,1},{1,0},{8,10},{10,12},{12... | collective-permute-start | bytes 786440 | tf_op jit(solution)/shard_map/ppermute | solution.py:581
  145.0 14.7 %collective-permute-start.20 = (f32[64,1024]{1,0:T(8,128)S(1)}, f32[64,1024]{1,0:T(8,128)S(1)}, u32[]{:S(2)}, u32[]{:S(2)}) collective-permute-start(f32[64,1024]{1,0:T(8,128)S(1)} %get-tuple-element.87), channel_id=1, source_target_pairs={{2,0},{4,2},{6,4},{7,6},{5,7},{3,5},{1,3},{0,1},{10,8},{12,10},{14... | collective-permute-start | bytes 786440 | tf_op jit(solution)/shard_map/ppermute | solution.py:581
  156.6 20.7 %collective-permute-start.40 = (f32[288,512]{1,0:T(8,128)S(1)}, f32[288,512]{1,0:T(8,128)S(1)}, u32[]{:S(2)}, u32[]{:S(2)}) collective-permute-start(f32[288,512]{1,0:T(8,128)S(1)} %add.32.refs_0_), channel_id=1, source_target_pairs={{0,8},{8,0},{16,24},{24,16},{1,9},{9,1},{17,25},{25,17},{2,10},{10... | collective-permute-start | bytes 1769480 | tf_op jit(solution)/shard_map/ppermute | solution.py:629
  156.7 22.2 %collective-permute-start.37 = (f32[288,512]{1,0:T(8,128)S(1)}, f32[288,512]{1,0:T(8,128)S(1)}, u32[]{:S(2)}, u32[]{:S(2)}) collective-permute-start(f32[288,512]{1,0:T(8,128)S(1)} %add.30.refs_0_), channel_id=1, source_target_pairs={{0,8},{8,0},{16,24},{24,16},{1,9},{9,1},{17,25},{25,17},{2,10},{10... | collective-permute-start | bytes 1769480 | tf_op jit(solution)/shard_map/ppermute | solution.py:629
  157.3 23.3 %collective-permute-start.34 = (f32[288,512]{1,0:T(8,128)S(1)}, f32[288,512]{1,0:T(8,128)S(1)}, u32[]{:S(2)}, u32[]{:S(2)}) collective-permute-start(f32[288,512]{1,0:T(8,128)S(1)} %add.28.refs_0_), channel_id=1, source_target_pairs={{0,8},{8,0},{16,24},{24,16},{1,9},{9,1},{17,25},{25,17},{2,10},{10... | collective-permute-start | bytes 1769480 | tf_op jit(solution)/shard_map/ppermute | solution.py:629
  (13 other events, 86.0 us)

commit v2 on v1

--- a/solution.py
+++ b/solution.py
@@ -273,7 +273,7 @@
 
 
 def middle_kernel(places, ring, total, grad, below, above, source, *refs):
-    active_out, spread_out, high_all, low_all, high_rim, low_rim, weights, sems, fetch_sems = refs[2:]
+    kept_out, spread_out, high_all, low_all, high_rim, low_rim, weights, sems, fetch_sems = refs[2:]
     depth, out_rows, area = total.shape
     chan = below.shape[0] // len(places)
     copies = []
@@ -302,23 +302,19 @@
             term = dot(weights[n, k], jnp.concatenate([high, high, low], axis=0))
             answer = term if answer is None else answer + term
         rim_sums.append(gathered(answer, out_rows))
-    positives = []
+    nothing = jnp.zeros((9 * out_rows, area), bf16)
+    for part in range(2):
+        spread_out[part, 0] = nothing
+        spread_out[part, depth + 1] = nothing
     for plane in range(depth):
         value = total[plane]
         if plane == 0:
             value = value + rim_sums[0]
         if plane == depth - 1:
             value = value + rim_sums[1]
-        positives.append(jnp.maximum(value, 0.0))
-    positives = jnp.stack(positives)
-    active_out[...] = jnp.swapaxes(positives * positives, 0, 1)
-    grads = jnp.swapaxes(grad[...], 0, 1)
-    nothing = jnp.zeros((9 * out_rows, area), bf16)
-    for part in range(2):
-        spread_out[part, 0] = nothing
-        spread_out[part, depth + 1] = nothing
-    for plane in range(depth):
-        pre_grad = 2.0 * positives[plane] * grads[plane]
+        positive = jnp.maximum(value, 0.0)
+        kept_out[plane] = positive
+        pre_grad = 2.0 * positive * grad[plane]
         for c in range(3):
             across = moved(pre_grad, 0, 1 - c)
             for b in range(3):
@@ -342,7 +338,7 @@
             in_specs=[whole(x.shape) for x in (total, grad, *outer)]
             + [keep, keep, keep],
             out_specs=[
-                whole((out_rows, depth, area)),
+                whole((depth, out_rows, area)),
                 whole((2, depth + 2, 9 * out_rows, area)),
                 keep,
                 keep,
@@ -356,7 +352,7 @@
             ],
         ),
         out_shape=[
-            jax.ShapeDtypeStruct((out_rows, depth, area), f32),
+            jax.ShapeDtypeStruct((depth, out_rows, area), f32),
             jax.ShapeDtypeStruct((2, depth + 2, 9 * out_rows, area), bf16),
             jax.ShapeDtypeStruct(high_all.shape, bf16),
             jax.ShapeDtypeStruct(low_all.shape, bf16),
@@ -366,6 +362,21 @@
         compiler_params=limit(),
         name="middle",
     )(ring, total, grad, *outer, weights, high_all, low_all)
+
+
+def turn_kernel(square, x, out):
+    value = x[...]
+    out[...] = jnp.swapaxes(value * value if square else value, 0, 1)
+
+
+def turned(x, square):
+    a, b, area = x.shape
+    return pl.pallas_call(
+        functools.partial(turn_kernel, square),
+        out_shape=jax.ShapeDtypeStruct((b, a, area), f32),
+        cost_estimate=cost(0, 8 * x.size),
+        compiler_params=limit(),
+    )(x)
 
 
 def inner_kernel(begin, planes, spread, high, low, out):
@@ -610,9 +621,11 @@
             outer = lax.ppermute(last, "slab", deeper), lax.ppermute(top, "slab", shallower)
             rim_places, held, held_places = held_places, [], ()
 
-    activated, spread, high_field, low_field = middle(
-        ring, carry, out_grad, rim_places, outer, ahead, chan
+    grads = turned(out_grad, False)
+    positives, spread, high_field, low_field = middle(
+        ring, carry, grads, rim_places, outer, ahead, chan
     )
+    activated = turned(positives, True)
 
     below, above = outer_terms(spread, back_high, back_low, chan)
     from_below = lax.ppermute(above, "slab", deeper)

time: 183 us -> 184 us (level)
  no operation moved by 1% of the time
where the time goes in v2:
time: 184 us; the launch traced here: 183 us
  Pallas kernels  79.2 us (43%)
  waiting for transfers between devices  60.7 us (33%)
  starting transfers between devices  38 us (21%)
  local copies, waits for them, and re-layouts  3.61 us (2%)
    ppermute x24, waiting for transfers between devices, send(): return lax.ppermute(x, 'filt', pairs)  48.3 us
    pallas_call x5, Pallas kernels, forward(): pl.pallas_call(functools.partial(forward_kernel, counts, places, rim_plac...  27 us
    ppermute x24, starting transfers between devices, send(): return lax.ppermute(x, 'filt', pairs)  25.9 us
    pallas_call x3, Pallas kernels, filter_terms(): pl.pallas_call(functools.partial(filter_kernel, tap), grid_spec=pltpu.Pre...  13.3 us
    ppermute x9, waiting for transfers between devices, swap(): return lax.ppermute(x, 'slab', [(i, i ^ bit) for i in range(slabs)])  12.3 us
    pallas_call x2, Pallas kernels, inner_terms(): pl.pallas_call(functools.partial(inner_kernel, begin, planes), out_shape=...  12.1 us
    pallas_call x1, Pallas kernels, prepare(): pl.pallas_call(functools.partial(prepare_kernel, chan), grid=(channels //...  7.36 us
    pallas_call x9, Pallas kernels, summed(): pl.pallas_call(kernel, grid_spec=pltpu.PrefetchScalarGridSpec(num_scalar_...  6.29 us
  transfers between devices with their start and end apart: 41, of which 10 were waited for; matrix products, arithmetic and copies ran while one was open for 1% of the time, Pallas kernels for 34%

profile of v2, /device:TPU:0, one launch (start us, length us, event | category | flops | bytes accessed | tf_op | source)
XLA Modules:
  0.0 183.2 jit_solution(8503143672794349987)
XLA Ops:
  0.6 3.0 %collective-permute-start.4 = (f32[64,8,256]{2,1,0:T(8,128)}, f32[64,8,256]{2,1,0:T(8,128)S(1)}, u32[]{:S(2)}, u32[]{:S(2)}) collective-permute-start(f32[64,8,256]{2,1,0:T(8,128)} %refs_0_.3), channel_id=1, source_target_pairs={{2,0},{4,2},{6,4},{7,6},{5,7},{3,5},{1,3},{0,1},{10,8},{12,10},{14... | collective-permute-start | bytes 1572872 | tf_op jit(solution)/shard_map/ppermute | solution.py:592
  3.8 12.1 %collective-permute-done.4.refs_2_.refs_1_ = f32[64,8,256]{2,1,0:T(8,128)S(1)} collective-permute-done((f32[64,8,256]{2,1,0:T(8,128)}, f32[64,8,256]{2,1,0:T(8,128)S(1)}, u32[]{:S(2)}, u32[]{:S(2)}) %collective-permute-start.4) | collective-permute-done | bytes 524320 | tf_op jit(solution)/shard_map/ppermute | solution.py:592
  15.9 1.7 collective-permute-start.5
  17.9 11.1 %collective-permute-done.5.refs_1_ = f32[64,8,256]{2,1,0:T(8,128)S(1)} collective-permute-done((f32[64,8,256]{2,1,0:T(8,128)S(1)}, f32[64,8,256]{2,1,0:T(8,128)S(1)}, u32[]{:S(2)}, u32[]{:S(2)}) %collective-permute-start.5) | collective-permute-done | bytes 524320 | tf_op jit(solution)/shard_map/ppermute | solution.py:592
  32.9 7.4 %prepare.1 = (bf16[3,8,576,192]{3,2,1,0:T(8,128)(2,1)}, bf16[512,1728]{1,0:T(8,128)(2,1)}, bf16[512,1728]{1,0:T(8,128)(2,1)}) custom-call(f32[27,64,512]{2,1,0:T(8,128)} %filters.1), custom_call_target="tpu_custom_call" | custom-call | bytes 17694720 | tf_op jit(solution)/shard_map/prepare/pallas_call | solution.py:82
  42.0 3.9 %forward.5 = (f32[8,64,256]{2,1,0:T(8,128)S(1)}, bf16[512,2560]{1,0:T(8,128)(2,1)S(1)}, bf16[512,2560]{1,0:T(8,128)(2,1)S(1)}) custom-call(s32[11]{0:T(128)S(1)} %dynamic-slice_bitcast_fusion.ring, f32[64,8,256]{2,1,0:T(8,128)S(1)} %copy-done, bf16[3,8,576,192]{3,2,1,0:T(8,128)(2,1)} %get-tuple-element.55.refs_1_.refs_2_.source), custom_call_target="tpu_custom_call" | custom-call | flops 1358954496 | bytes 1310720 | tf_op jit(solution)/shard_map/forward/pallas_call | solution.py:242
  46.2 1.7 collective-permute-start.11
  50.1 5.8 %forward.6 = (f32[8,64,256]{2,1,0:T(8,128)S(1)}, bf16[512,2560]{1,0:T(8,128)(2,1)S(1)}, bf16[512,2560]{1,0:T(8,128)(2,1)S(1)}) custom-call(s32[11]{0:T(128)S(1)} %dynamic-slice_bitcast_fusion.ring, f32[64,8,256]{2,1,0:T(8,128)S(1)} %collective-permute-done.refs_1_.refs_0_, ...), custom_call_target="tpu_custom_call", output_to_operand_aliasing={{0}: (4, {}), {1}: (5, {}), {2}: (6, {})} | custom-call | flops 2717908992 | bytes 2621440 | tf_op jit(solution)/shard_map/forward/pallas_call | solution.py:242
  56.1 1.7 collective-permute-start.9
  57.9 6.9 %forward.7 = (f32[8,64,256]{2,1,0:T(8,128)S(1)}, bf16[512,2560]{1,0:T(8,128)(2,1)S(1)}, bf16[512,2560]{1,0:T(8,128)(2,1)S(1)}) custom-call(s32[11]{0:T(128)S(1)} %dynamic-slice_bitcast_fusion.ring, f32[64,8,256]{2,1,0:T(8,128)S(1)} %collective-permute-done.1.refs_0_, ...), custom_call_target="tpu_custom_call", output_to_operand_aliasing={{0}: (6, {}), {1}: (7, {}), {2}: (8, {})} | custom-call | flops 2717908992 | bytes 2621440 | tf_op jit(solution)/shard_map/forward/pallas_call | solution.py:242
  65.1 1.7 collective-permute-start.13
  66.8 6.5 %forward.8 = (f32[8,64,256]{2,1,0:T(8,128)S(1)}, bf16[512,2560]{1,0:T(8,128)(2,1)S(1)}, bf16[512,2560]{1,0:T(8,128)(2,1)S(1)}) custom-call(s32[11]{0:T(128)S(1)} %dynamic-slice_bitcast_fusion.ring, f32[64,8,256]{2,1,0:T(8,128)S(1)} %collective-permute-done.2.refs_0_, ...), custom_call_target="tpu_custom_call", output_to_operand_aliasing={{0}: (6, {}), {1}: (7, {}), {2}: (8, {})} | custom-call | flops 2717908992 | bytes 2621440 | tf_op jit(solution)/shard_map/forward/pallas_call | solution.py:242
  73.3 3.9 %forward.9 = (f32[8,64,256]{2,1,0:T(8,128)S(1)}, bf16[512,2560]{1,0:T(8,128)(2,1)S(1)}, bf16[512,2560]{1,0:T(8,128)(2,1)S(1)}) custom-call(s32[11]{0:T(128)S(1)} %dynamic-slice_bitcast_fusion.ring, f32[32,8,256]{2,1,0:T(8,128)S(1)} %collective-permute-done.3.refs_0_.refs_2_, ...), custom_call_target="tpu_custom_call", output_to_operand_aliasing={{0}: (4, {}), {1}: (5, {}), {2}: (6, {})} | custom-call | flops 1358954496 | bytes 1310720 | tf_op jit(solution)/shard_map/forward/pallas_call | solution.py:242
  77.3 5.2 %middle.1 = (f32[8,64,256]{2,1,0:T(8,128)S(1)}, bf16[2,10,576,256]{3,2,1,0:T(8,128)(2,1)S(1)}, bf16[512,2560]{1,0:T(8,128)(2,1)S(1)}, bf16[512,2560]{1,0:T(8,128)(2,1)S(1)}) custom-call(s32[11]{0:T(128)S(1)} %dynamic-slice_bitcast_fusion.ring, f32[8,64,256]{2,1,0:T(8,128)S(1)} %get-tuple-element.72.total, ...), custom_call_target="tpu_custom_call", output_to_operand_aliasing={{2}: (6, {}), {3}: (7, {})} | custom-call | bytes 9437184 | tf_op jit(solution)/shard_map/middle/pallas_call | solution.py:333
  82.5 4.5 %filter_terms.5 = (f32[288,512]{1,0:T(8,128)S(1)}, f32[288,512]{1,0:T(8,128)S(1)}) custom-call(s32[11]{0:T(128)S(1)} %dynamic-slice_bitcast_fusion.ring, bf16[2,10,576,256]{3,2,1,0:T(8,128)(2,1)S(1)} %get-tuple-element.78.spread, bf16[512,2560]{1,0:T(8,128)(2,1)S(1)} %get-tuple-element.99.high, bf16[512,2560]{1,0:T(8,128)(2,1)S(1)} %get-tuple-element.100.low), custom_call_target="tpu_custom_call" | custom-call | flops 4529848320 | bytes 11141120 | tf_op jit(solution)/shard_map/filter_terms/pallas_call | solution.py:459
  86.9 4.5 %filter_terms.4 = (f32[288,512]{1,0:T(8,128)S(1)}, f32[288,512]{1,0:T(8,128)S(1)}) custom-call(s32[11]{0:T(128)S(1)} %dynamic-slice_bitcast_fusion.ring, bf16[2,10,576,256]{3,2,1,0:T(8,128)(2,1)S(1)} %get-tuple-element.78.spread, bf16[512,2560]{1,0:T(8,128)(2,1)S(1)} %get-tuple-element.99.high, bf16[512,2560]{1,0:T(8,128)(2,1)S(1)} %get-tuple-element.100.low), custom_call_target="tpu_custom_call" | custom-call | flops 4529848320 | bytes 11141120 | tf_op jit(solution)/shard_map/filter_terms/pallas_call | solution.py:459
  92.9 1.7 collective-permute-start.23
  94.6 4.4 %filter_terms.3 = (f32[288,512]{1,0:T(8,128)S(1)}, f32[288,512]{1,0:T(8,128)S(1)}) custom-call(s32[11]{0:T(128)S(1)} %dynamic-slice_bitcast_fusion.ring, bf16[2,10,576,256]{3,2,1,0:T(8,128)(2,1)S(1)} %get-tuple-element.78.spread, bf16[512,2560]{1,0:T(8,128)(2,1)S(1)} %get-tuple-element.99.high, bf16[512,2560]{1,0:T(8,128)(2,1)S(1)} %get-tuple-element.100.low), custom_call_target="tpu_custom_call" | custom-call | flops 4529848320 | bytes 11141120 | tf_op jit(solution)/shard_map/filter_terms/pallas_call | solution.py:459
  99.7 6.1 %inner_terms.3.inner.up_inner.down_inner.refs_4_ = f32[8,64,1024]{2,1,0:T(8,128)S(1)} custom-call(bf16[2,10,576,256]{3,2,1,0:T(8,128)(2,1)S(1)} %get-tuple-element.78.spread, bf16[512,1728]{1,0:T(8,128)(2,1)S(1)} %copy-done.3, bf16[512,1728]{1,0:T(8,128)(2,1)S(1)} %copy-done.4), custom_call_target="tpu_custom_call" | custom-call | flops 5435817984 | bytes 9437184 | tf_op jit(solution)/shard_map/inner_terms/pallas_call | solution.py:413
  108.7 6.1 %inner_terms.2.inner.up_inner.down_inner.refs_0_ = f32[8,64,1024]{2,1,0:T(8,128)S(1)} custom-call(bf16[2,10,576,256]{3,2,1,0:T(8,128)(2,1)S(1)} %get-tuple-element.78.spread, bf16[512,1728]{1,0:T(8,128)(2,1)S(1)} %copy-done.3, bf16[512,1728]{1,0:T(8,128)(2,1)S(1)} %copy-done.4), custom_call_target="tpu_custom_call" | custom-call | flops 5435817984 | bytes 9437184 | tf_op jit(solution)/shard_map/inner_terms/pallas_call | solution.py:413
  119.9 1.6 collective-permute-start.26
  122.6 9.1 %collective-permute-done.16.down = f32[32,1024]{1,0:T(8,128)S(1)} collective-permute-done((f32[32,1024]{1,0:T(8,128)S(1)}, f32[32,1024]{1,0:T(8,128)S(1)}, u32[]{:S(2)}, u32[]{:S(2)}) %collective-permute-start.16) | collective-permute-done | bytes 131104 | tf_op jit(solution)/shard_map/ppermute | solution.py:592
  133.8 1.6 collective-permute-start.17
  136.5 3.8 %collective-permute-done.17.up = f32[64,1024]{1,0:T(8,128)S(1)} collective-permute-done((f32[64,1024]{1,0:T(8,128)S(1)}, f32[64,1024]{1,0:T(8,128)S(1)}, u32[]{:S(2)}, u32[]{:S(2)}) %collective-permute-start.17) | collective-permute-done | bytes 262176 | tf_op jit(solution)/shard_map/ppermute | solution.py:592
  143.1 1.6 collective-permute-start.19
  146.6 11.0 %collective-permute-done.33 = f32[288,512]{1,0:T(8,128)S(1)} collective-permute-done((f32[288,512]{1,0:T(8,128)S(1)}, f32[288,512]{1,0:T(8,128)S(1)}, u32[]{:S(2)}, u32[]{:S(2)}) %collective-permute-start.33) | collective-permute-done | bytes 589856 | tf_op jit(solution)/shard_map/ppermute | solution.py:642
  159.0 1.6 collective-permute-start.30
  161.7 6.0 %collective-permute-done.30.refs_6_ = f32[64,1024]{1,0:T(8,128)S(1)} collective-permute-done((f32[64,1024]{1,0:T(8,128)S(1)}, f32[64,1024]{1,0:T(8,128)S(1)}, u32[]{:S(2)}, u32[]{:S(2)}) %collective-permute-start.30) | collective-permute-done | bytes 262176 | tf_op jit(solution)/shard_map/ppermute | solution.py:592
  170.6 4.8 %collective-permute-done.21.refs_2_ = f32[64,1024]{1,0:T(8,128)S(1)} collective-permute-done((f32[64,1024]{1,0:T(8,128)S(1)}, f32[64,1024]{1,0:T(8,128)S(1)}, u32[]{:S(2)}, u32[]{:S(2)}) %collective-permute-start.21) | collective-permute-done | bytes 262176 | tf_op jit(solution)/shard_map/ppermute | solution.py:592
  178.2 1.7 place.3.refs_2_
  179.9 1.7 place.4.refs_2_
  181.6 1.7 place.5
  (101 shorter events, 36.2 us)
Async XLA Ops:
  0.6 15.2 %collective-permute-start.4 = (f32[64,8,256]{2,1,0:T(8,128)}, f32[64,8,256]{2,1,0:T(8,128)S(1)}, u32[]{:S(2)}, u32[]{:S(2)}) collective-permute-start(f32[64,8,256]{2,1,0:T(8,128)} %refs_0_.3), channel_id=1, source_target_pairs={{2,0},{4,2},{6,4},{7,6},{5,7},{3,5},{1,3},{0,1},{10,8},{12,10},{14... | collective-permute-start | bytes 1572872 | tf_op jit(solution)/shard_map/ppermute | solution.py:592
  3.6 13.9 %collective-permute-start = (f32[64,8,256]{2,1,0:T(8,128)}, f32[64,8,256]{2,1,0:T(8,128)S(1)}, u32[]{:S(2)}, u32[]{:S(2)}) collective-permute-start(f32[64,8,256]{2,1,0:T(8,128)} %refs_0_.3), channel_id=1, source_target_pairs={{0,2},{2,4},{4,6},{6,7},{7,5},{5,3},{3,1},{1,0},{8,10},{10,12},{12... | collective-permute-start | bytes 1572872 | tf_op jit(solution)/shard_map/ppermute | solution.py:592
  15.9 13.1 %collective-permute-start.5 = (f32[64,8,256]{2,1,0:T(8,128)S(1)}, f32[64,8,256]{2,1,0:T(8,128)S(1)}, u32[]{:S(2)}, u32[]{:S(2)}) collective-permute-start(f32[64,8,256]{2,1,0:T(8,128)S(1)} %collective-permute-done.4.refs_2_.refs_1_), channel_id=1, source_target_pairs={{2,0},{4,2},{6,4},{7,6},{5,7},{3,5},{1,3},{0,1},{10,8},{12,10},{14... | collective-permute-start | bytes 1572872 | tf_op jit(solution)/shard_map/ppermute | solution.py:592
  17.5 12.8 %collective-permute-start.1 = (f32[64,8,256]{2,1,0:T(8,128)S(1)}, f32[64,8,256]{2,1,0:T(8,128)S(1)}, u32[]{:S(2)}, u32[]{:S(2)}) collective-permute-start(f32[64,8,256]{2,1,0:T(8,128)S(1)} %collective-permute-done.refs_1_.refs_0_), channel_id=1, source_target_pairs={{0,2},{2,4},{4,6},{6,7},{7,5},{5,3},{3,1},{1,0},{8,10},{10,12},{12... | collective-permute-start | bytes 1572872 | tf_op jit(solution)/shard_map/ppermute | solution.py:592
  29.0 18.9 %collective-permute-start.6 = (f32[64,8,256]{2,1,0:T(8,128)S(1)}, f32[64,8,256]{2,1,0:T(8,128)S(1)}, u32[]{:S(2)}, u32[]{:S(2)}) collective-permute-start(f32[64,8,256]{2,1,0:T(8,128)S(1)} %collective-permute-done.5.refs_1_), channel_id=1, source_target_pairs={{2,0},{4,2},{6,4},{7,6},{5,7},{3,5},{1,3},{0,1},{10,8},{12,10},{14... | collective-permute-start | bytes 1572872 | tf_op jit(solution)/shard_map/ppermute | solution.py:592
  30.3 19.0 %collective-permute-start.2 = (f32[64,8,256]{2,1,0:T(8,128)S(1)}, f32[64,8,256]{2,1,0:T(8,128)S(1)}, u32[]{:S(2)}, u32[]{:S(2)}) collective-permute-start(f32[64,8,256]{2,1,0:T(8,128)S(1)} %collective-permute-done.1.refs_0_), channel_id=1, source_target_pairs={{0,2},{2,4},{4,6},{6,7},{7,5},{5,3},{3,1},{1,0},{8,10},{10,12},{12... | collective-permute-start | bytes 1572872 | tf_op jit(solution)/shard_map/ppermute | solution.py:592
  46.2 11.7 %collective-permute-start.11 = (f32[192,256]{1,0:T(8,128)S(1)}, f32[192,256]{1,0:T(8,128)S(1)}, u32[]{:S(2)}, u32[]{:S(2)}) collective-permute-start(f32[192,256]{1,0:T(8,128)S(1)} %get-tuple-element.59), channel_id=1, source_target_pairs={{8,0},{16,8},{24,16},{0,24},{9,1},{17,9},{25,17},{1,25},{10,2},{18... | collective-permute-start | bytes 589832 | tf_op jit(solution)/shard_map/ppermute | solution.py:621
  47.9 16.9 %collective-permute-start.7 = (f32[32,8,256]{2,1,0:T(8,128)S(1)}, f32[32,8,256]{2,1,0:T(8,128)S(1)}, u32[]{:S(2)}, u32[]{:S(2)}) collective-permute-start(f32[32,8,256]{2,1,0:T(8,128)S(1)} %slice.9), channel_id=1, source_target_pairs={{2,0},{4,2},{6,4},{7,6},{5,7},{3,5},{1,3},{0,1},{10,8},{12,10},{14... | collective-permute-start | bytes 786440 | tf_op jit(solution)/shard_map/ppermute | solution.py:592
  49.4 15.4 %collective-permute-start.3 = (f32[32,8,256]{2,1,0:T(8,128)S(1)}, f32[32,8,256]{2,1,0:T(8,128)S(1)}, u32[]{:S(2)}, u32[]{:S(2)}) collective-permute-start(f32[32,8,256]{2,1,0:T(8,128)S(1)} %slice.8), channel_id=1, source_target_pairs={{0,2},{2,4},{4,6},{6,7},{7,5},{5,3},{3,1},{1,0},{8,10},{10,12},{12... | collective-permute-start | bytes 786440 | tf_op jit(solution)/shard_map/ppermute | solution.py:592
  56.1 10.7 %collective-permute-start.8 = (f32[128,256]{1,0:T(8,128)S(1)}, f32[128,256]{1,0:T(8,128)S(1)}, u32[]{:S(2)}, u32[]{:S(2)}) collective-permute-start(f32[128,256]{1,0:T(8,128)S(1)} %get-tuple-element.56), channel_id=1, source_target_pairs={{0,8},{8,16},{16,24},{24,0},{1,9},{9,17},{17,25},{25,1},{2,10},{10... | collective-permute-start | bytes 393224 | tf_op jit(solution)/shard_map/ppermute | solution.py:621
  56.1 10.7 %collective-permute-start.9 = (f32[128,256]{1,0:T(8,128)S(1)}, f32[128,256]{1,0:T(8,128)S(1)}, u32[]{:S(2)}, u32[]{:S(2)}) collective-permute-start(f32[128,256]{1,0:T(8,128)S(1)} %get-tuple-element.57), channel_id=1, source_target_pairs={{8,0},{16,8},{24,16},{0,24},{9,1},{17,9},{25,17},{1,25},{10,2},{18... | collective-permute-start | bytes 393224 | tf_op jit(solution)/shard_map/ppermute | solution.py:621
  65.0 12.2 %collective-permute-start.12 = (f32[192,256]{1,0:T(8,128)S(1)}, f32[192,256]{1,0:T(8,128)S(1)}, u32[]{:S(2)}, u32[]{:S(2)}) collective-permute-start(f32[192,256]{1,0:T(8,128)S(1)} %get-tuple-element.73), channel_id=1, source_target_pairs={{0,8},{8,16},{16,24},{24,0},{1,9},{9,17},{17,25},{25,1},{2,10},{10... | collective-permute-start | bytes 589832 | tf_op jit(solution)/shard_map/ppermute | solution.py:621
  65.1 12.2 %collective-permute-start.13 = (f32[192,256]{1,0:T(8,128)S(1)}, f32[192,256]{1,0:T(8,128)S(1)}, u32[]{:S(2)}, u32[]{:S(2)}) collective-permute-start(f32[192,256]{1,0:T(8,128)S(1)} %get-tuple-element.74), channel_id=1, source_target_pairs={{8,0},{16,8},{24,16},{0,24},{9,1},{17,9},{25,17},{1,25},{10,2},{18... | collective-permute-start | bytes 589832 | tf_op jit(solution)/shard_map/ppermute | solution.py:621
  92.8 15.4 %collective-permute-start.14 = (f32[8,64,256]{2,1,0:T(8,128)S(1)}, f32[8,64,256]{2,1,0:T(8,128)S(1)}, u32[]{:S(2)}, u32[]{:S(2)}) collective-permute-start(f32[8,64,256]{2,1,0:T(8,128)S(1)} %get-tuple-element.81), channel_id=1, source_target_pairs={{0,8},{8,16},{16,24},{24,0},{1,9},{9,17},{17,25},{25,1},{2,10},{10... | collective-permute-start | bytes 1572872 | tf_op jit(solution)/shard_map/ppermute | solution.py:631
  92.9 13.1 %collective-permute-start.23 = (f32[8,64,256]{2,1,0:T(8,128)S(1)}, f32[8,64,256]{2,1,0:T(8,128)S(1)}, u32[]{:S(2)}, u32[]{:S(2)}) collective-permute-start(f32[8,64,256]{2,1,0:T(8,128)S(1)} %get-tuple-element.90), channel_id=1, source_target_pairs={{8,0},{16,8},{24,16},{0,24},{9,1},{17,9},{25,17},{1,25},{10,2},{18... | collective-permute-start | bytes 1572872 | tf_op jit(solution)/shard_map/ppermute | solution.py:632
  99.1 16.3 %collective-permute-start.38 = (f32[288,512]{1,0:T(8,128)S(1)}, f32[288,512]{1,0:T(8,128)S(1)}, u32[]{:S(2)}, u32[]{:S(2)}) collective-permute-start(f32[288,512]{1,0:T(8,128)S(1)} %get-tuple-element.106), channel_id=1, source_target_pairs={{0,8},{8,0},{16,24},{24,16},{1,9},{9,1},{17,25},{25,17},{2,10},{10... | collective-permute-start | bytes 1769480 | tf_op jit(solution)/shard_map/ppermute | solution.py:642
  99.1 17.9 %collective-permute-start.35 = (f32[288,512]{1,0:T(8,128)S(1)}, f32[288,512]{1,0:T(8,128)S(1)}, u32[]{:S(2)}, u32[]{:S(2)}) collective-permute-start(f32[288,512]{1,0:T(8,128)S(1)} %get-tuple-element.104), channel_id=1, source_target_pairs={{0,8},{8,0},{16,24},{24,16},{1,9},{9,1},{17,25},{25,17},{2,10},{10... | collective-permute-start | bytes 1769480 | tf_op jit(solution)/shard_map/ppermute | solution.py:642
  99.6 21.9 %collective-permute-start.32 = (f32[288,512]{1,0:T(8,128)S(1)}, f32[288,512]{1,0:T(8,128)S(1)}, u32[]{:S(2)}, u32[]{:S(2)}) collective-permute-start(f32[288,512]{1,0:T(8,128)S(1)} %get-tuple-element.102), channel_id=1, source_target_pairs={{0,8},{8,0},{16,24},{24,16},{1,9},{9,1},{17,25},{25,17},{2,10},{10... | collective-permute-start | bytes 1769480 | tf_op jit(solution)/shard_map/ppermute | solution.py:642
  106.6 11.9 %collective-permute-start.24 = (f32[32,1024]{1,0:T(8,128)S(1)}, f32[32,1024]{1,0:T(8,128)S(1)}, u32[]{:S(2)}, u32[]{:S(2)}) collective-permute-start(f32[32,1024]{1,0:T(8,128)S(1)} %get-tuple-element.91), channel_id=1, source_target_pairs={{0,2},{2,4},{4,6},{6,7},{7,5},{5,3},{3,1},{1,0},{8,10},{10,12},{12... | collective-permute-start | bytes 393224 | tf_op jit(solution)/shard_map/ppermute | solution.py:592
  108.2 11.1 %collective-permute-start.25 = (f32[32,1024]{1,0:T(8,128)S(1)}, f32[32,1024]{1,0:T(8,128)S(1)}, u32[]{:S(2)}, u32[]{:S(2)}) collective-permute-start(f32[32,1024]{1,0:T(8,128)S(1)} %get-tuple-element.92), channel_id=1, source_target_pairs={{2,0},{4,2},{6,4},{7,6},{5,7},{3,5},{1,3},{0,1},{10,8},{12,10},{14... | collective-permute-start | bytes 393224 | tf_op jit(solution)/shard_map/ppermute | solution.py:592
  117.1 26.0 %collective-permute-start.39 = (f32[288,512]{1,0:T(8,128)S(1)}, f32[288,512]{1,0:T(8,128)S(1)}, u32[]{:S(2)}, u32[]{:S(2)}) collective-permute-start(f32[288,512]{1,0:T(8,128)S(1)} %add.31), channel_id=1, source_target_pairs={{0,16},{8,24},{16,0},{24,8},{1,17},{9,25},{17,1},{25,9},{2,18},{10... | collective-permute-start | bytes 1769480 | tf_op jit(solution)/shard_map/ppermute | solution.py:642
  118.5 27.5 %collective-permute-start.36 = (f32[288,512]{1,0:T(8,128)S(1)}, f32[288,512]{1,0:T(8,128)S(1)}, u32[]{:S(2)}, u32[]{:S(2)}) collective-permute-start(f32[288,512]{1,0:T(8,128)S(1)} %add.29), channel_id=1, source_target_pairs={{0,16},{8,24},{16,0},{24,8},{1,17},{9,25},{17,1},{25,9},{2,18},{10... | collective-permute-start | bytes 1769480 | tf_op jit(solution)/shard_map/ppermute | solution.py:642
  119.9 13.9 %collective-permute-start.26 = (f32[64,1024]{1,0:T(8,128)S(1)}, f32[64,1024]{1,0:T(8,128)S(1)}, u32[]{:S(2)}, u32[]{:S(2)}) collective-permute-start(f32[64,1024]{1,0:T(8,128)S(1)} %get-tuple-element.93), channel_id=1, source_target_pairs={{0,2},{2,4},{4,6},{6,7},{7,5},{5,3},{3,1},{1,0},{8,10},{10,12},{12... | collective-permute-start | bytes 786440 | tf_op jit(solution)/shard_map/ppermute | solution.py:592
  121.6 13.9 %collective-permute-start.27 = (f32[64,1024]{1,0:T(8,128)S(1)}, f32[64,1024]{1,0:T(8,128)S(1)}, u32[]{:S(2)}, u32[]{:S(2)}) collective-permute-start(f32[64,1024]{1,0:T(8,128)S(1)} %get-tuple-element.94), channel_id=1, source_target_pairs={{2,0},{4,2},{6,4},{7,6},{5,7},{3,5},{1,3},{0,1},{10,8},{12,10},{14... | collective-permute-start | bytes 786440 | tf_op jit(solution)/shard_map/ppermute | solution.py:592
  131.7 25.9 %collective-permute-start.33 = (f32[288,512]{1,0:T(8,128)S(1)}, f32[288,512]{1,0:T(8,128)S(1)}, u32[]{:S(2)}, u32[]{:S(2)}) collective-permute-start(f32[288,512]{1,0:T(8,128)S(1)} %add.27), channel_id=1, source_target_pairs={{0,16},{8,24},{16,0},{24,8},{1,17},{9,25},{17,1},{25,9},{2,18},{10... | collective-permute-start | bytes 1769480 | tf_op jit(solution)/shard_map/ppermute | solution.py:642
  140.4 17.3 %collective-permute-start.28 = (f32[64,1024]{1,0:T(8,128)S(1)}, f32[64,1024]{1,0:T(8,128)S(1)}, u32[]{:S(2)}, u32[]{:S(2)}) collective-permute-start(f32[64,1024]{1,0:T(8,128)S(1)} %get-tuple-element.95), channel_id=1, source_target_pairs={{0,2},{2,4},{4,6},{6,7},{7,5},{5,3},{3,1},{1,0},{8,10},{10,12},{12... | collective-permute-start | bytes 786440 | tf_op jit(solution)/shard_map/ppermute | solution.py:592
  142.0 16.3 %collective-permute-start.29 = (f32[64,1024]{1,0:T(8,128)S(1)}, f32[64,1024]{1,0:T(8,128)S(1)}, u32[]{:S(2)}, u32[]{:S(2)}) collective-permute-start(f32[64,1024]{1,0:T(8,128)S(1)} %get-tuple-element.96), channel_id=1, source_target_pairs={{2,0},{4,2},{6,4},{7,6},{5,7},{3,5},{1,3},{0,1},{10,8},{12,10},{14... | collective-permute-start | bytes 786440 | tf_op jit(solution)/shard_map/ppermute | solution.py:592
  143.1 15.9 %collective-permute-start.19 = (f32[64,1024]{1,0:T(8,128)S(1)}, f32[64,1024]{1,0:T(8,128)S(1)}, u32[]{:S(2)}, u32[]{:S(2)}) collective-permute-start(f32[64,1024]{1,0:T(8,128)S(1)} %get-tuple-element.86), channel_id=1, source_target_pairs={{0,2},{2,4},{4,6},{6,7},{7,5},{5,3},{3,1},{1,0},{8,10},{10,12},{12... | collective-permute-start | bytes 786440 | tf_op jit(solution)/shard_map/ppermute | solution.py:592
  146.0 14.7 %collective-permute-start.20 = (f32[64,1024]{1,0:T(8,128)S(1)}, f32[64,1024]{1,0:T(8,128)S(1)}, u32[]{:S(2)}, u32[]{:S(2)}) collective-permute-start(f32[64,1024]{1,0:T(8,128)S(1)} %get-tuple-element.87), channel_id=1, source_target_pairs={{2,0},{4,2},{6,4},{7,6},{5,7},{3,5},{1,3},{0,1},{10,8},{12,10},{14... | collective-permute-start | bytes 786440 | tf_op jit(solution)/shard_map/ppermute | solution.py:592
  157.6 20.7 %collective-permute-start.40 = (f32[288,512]{1,0:T(8,128)S(1)}, f32[288,512]{1,0:T(8,128)S(1)}, u32[]{:S(2)}, u32[]{:S(2)}) collective-permute-start(f32[288,512]{1,0:T(8,128)S(1)} %add.32.refs_0_), channel_id=1, source_target_pairs={{0,8},{8,0},{16,24},{24,16},{1,9},{9,1},{17,25},{25,17},{2,10},{10... | collective-permute-start | bytes 1769480 | tf_op jit(solution)/shard_map/ppermute | solution.py:642
  157.7 22.2 %collective-permute-start.37 = (f32[288,512]{1,0:T(8,128)S(1)}, f32[288,512]{1,0:T(8,128)S(1)}, u32[]{:S(2)}, u32[]{:S(2)}) collective-permute-start(f32[288,512]{1,0:T(8,128)S(1)} %add.30.refs_0_), channel_id=1, source_target_pairs={{0,8},{8,0},{16,24},{24,16},{1,9},{9,1},{17,25},{25,17},{2,10},{10... | collective-permute-start | bytes 1769480 | tf_op jit(solution)/shard_map/ppermute | solution.py:642
  158.3 23.3 %collective-permute-start.34 = (f32[288,512]{1,0:T(8,128)S(1)}, f32[288,512]{1,0:T(8,128)S(1)}, u32[]{:S(2)}, u32[]{:S(2)}) collective-permute-start(f32[288,512]{1,0:T(8,128)S(1)} %add.28.refs_0_), channel_id=1, source_target_pairs={{0,8},{8,0},{16,24},{24,16},{1,9},{9,1},{17,25},{25,17},{2,10},{10... | collective-permute-start | bytes 1769480 | tf_op jit(solution)/shard_map/ppermute | solution.py:642
  (15 other events, 87.8 us)

commit v3 on v2

--- a/solution.py
+++ b/solution.py
@@ -277,7 +277,6 @@
     depth, out_rows, area = total.shape
     chan = below.shape[0] // len(places)
     copies = []
-    rim_sums = []
     fetches = {}
     for n in range(2):
         for k, place in enumerate(places):
@@ -285,6 +284,25 @@
                 source.at[2 * n, ring[place]], weights.at[n, k], fetch_sems.at[n, k]
             )
             fetches[n, k].start()
+    nothing = jnp.zeros((9 * out_rows, area), bf16)
+    for part in range(2):
+        spread_out[part, 0] = nothing
+        spread_out[part, depth + 1] = nothing
+
+    def finish(plane, value):
+        positive = jnp.maximum(value, 0.0)
+        kept_out[plane] = positive
+        pre_grad = 2.0 * positive * grad[plane]
+        for c in range(3):
+            across = moved(pre_grad, 0, 1 - c)
+            for b in range(3):
+                high, low = parts_of(moved(across, 1 - b, 0))
+                at = (3 * b + c) * out_rows
+                spread_out[0, plane + 1, at : at + out_rows] = high
+                spread_out[1, plane + 1, at : at + out_rows] = low
+
+    for plane in range(1, depth - 1):
+        finish(plane, total[plane])
     for n, rim in enumerate((below, above)):
         answer = None
         for k, place in enumerate(places):
@@ -301,27 +319,8 @@
             fetches[n, k].wait()
             term = dot(weights[n, k], jnp.concatenate([high, high, low], axis=0))
             answer = term if answer is None else answer + term
-        rim_sums.append(gathered(answer, out_rows))
-    nothing = jnp.zeros((9 * out_rows, area), bf16)
-    for part in range(2):
-        spread_out[part, 0] = nothing
-        spread_out[part, depth + 1] = nothing
-    for plane in range(depth):
-        value = total[plane]
-        if plane == 0:
-            value = value + rim_sums[0]
-        if plane == depth - 1:
-            value = value + rim_sums[1]
-        positive = jnp.maximum(value, 0.0)
-        kept_out[plane] = positive
-        pre_grad = 2.0 * positive * grad[plane]
-        for c in range(3):
-            across = moved(pre_grad, 0, 1 - c)
-            for b in range(3):
-                high, low = parts_of(moved(across, 1 - b, 0))
-                at = (3 * b + c) * out_rows
-                spread_out[0, plane + 1, at : at + out_rows] = high
-                spread_out[1, plane + 1, at : at + out_rows] = low
+        edge = n * (depth - 1)
+        finish(edge, total[edge] + gathered(answer, out_rows))
     for copy in copies:
         copy.wait()
 
@@ -431,33 +430,39 @@
     )(spread, high, low)
 
 
-def filter_kernel(tap, ring, spread, high, low, keep_out, send_out, total):
+def filter_kernel(begin, end, scale, ring, spread, high, low, keep_out, send_out, total):
     depth = spread.shape[1] - 2
-    rows, area = spread.shape[2:]
-    half = rows // 2
+    area = spread.shape[3]
+    out_rows = spread.shape[2] // 9
+    half = (end - begin) * out_rows // 2
     channels = high.shape[0]
     step = min(256, channels)
-    for at in range(0, channels, step):
-        value = None
-        for plane in range(depth):
-            lanes = slice((tap + plane) * area, (tap + plane + 1) * area)
-            right = high[at : at + step, lanes]
-            term = dot_t(spread[0, plane + 1], right) + dot_t(spread[1, plane + 1], right)
-            term = term + dot_t(spread[0, plane + 1], low[at : at + step, lanes])
-            value = term if value is None else value + term
-        total[:, at : at + step] = value
+    for a in range(3):
+        first, last = max(begin, 9 * a), min(end, 9 * a + 9)
+        if first >= last:
+            continue
+        rows = slice((first - 9 * a) * out_rows, (last - 9 * a) * out_rows)
+        into = slice((first - begin) * out_rows, (last - begin) * out_rows)
+        for at in range(0, channels, step):
+            value = None
+            for plane in range(depth):
+                lanes = slice((a + plane) * area, (a + plane + 1) * area)
+                right = high[at : at + step, lanes]
+                near = spread[0, plane + 1, rows]
+                term = dot_t(near, right) + dot_t(spread[1, plane + 1, rows], right)
+                term = term + dot_t(near, low[at : at + step, lanes])
+                value = term if value is None else value + term
+            total[into, at : at + step] = value * (1.0 / scale)
     side = ring[ring.shape[0] - 1]
-    mine = pl.multiple_of(side * half, half)
-    other = pl.multiple_of((1 - side) * half, half)
-    keep_out[...] = total[pl.ds(mine, half), :]
-    send_out[...] = total[pl.ds(other, half), :]
-
-
-def filter_terms(tap, ring, spread, high, low):
-    rows = spread.shape[2]
+    keep_out[...] = total[pl.ds(pl.multiple_of(side * half, half), half), :]
+    send_out[...] = total[pl.ds(pl.multiple_of((1 - side) * half, half), half), :]
+
+
+def filter_terms(begin, end, scale, ring, spread, high, low):
     channels = high.shape[0]
-    return pl.pallas_call(
-        functools.partial(filter_kernel, tap),
+    rows = (end - begin) * (spread.shape[2] // 9)
+    return pl.pallas_call(
+        functools.partial(filter_kernel, begin, end, scale),
         grid_spec=pltpu.PrefetchScalarGridSpec(
             num_scalar_prefetch=1,
             grid=(1,),
@@ -472,32 +477,39 @@
     )(ring, spread, high, low)
 
 
-def place_kernel(scale, ring, *refs):
-    mine, other, out = refs[0], refs[1], refs[-1]
+def place_kernel(begin, ring, *refs):
+    mine, other, out, sems = refs[0], refs[1], refs[-2], refs[-1]
     half = mine.shape[0]
     side = ring[ring.shape[0] - 1]
-    out[0, pl.ds(pl.multiple_of(side * half, half), half), :] = mine[...] / scale
-    out[0, pl.ds(pl.multiple_of((1 - side) * half, half), half), :] = other[...] / scale
-
-
-def place(tap, ring, mine, other, carry, scale):
+    copies = []
+    for n, (part, at) in enumerate(((mine, side), (other, 1 - side))):
+        rows = pl.ds(pl.multiple_of(begin + at * half, 8), half)
+        copies.append(pltpu.make_async_copy(part, out.at[rows], sems.at[n]))
+        copies[-1].start()
+    for copy in copies:
+        copy.wait()
+
+
+def place(begin, ring, mine, other, carry, rows):
     half, channels = mine.shape
+    keep = pl.BlockSpec(memory_space=pltpu.HBM)
     args = [mine, other]
     in_specs = [whole(mine.shape)] * 2
     aliases = {}
     if carry is not None:
         args.append(carry)
-        in_specs.append(pl.BlockSpec(memory_space=pl.ANY))
+        in_specs.append(keep)
         aliases = {3: 0}
     return pl.pallas_call(
-        functools.partial(place_kernel, scale),
+        functools.partial(place_kernel, begin),
         grid_spec=pltpu.PrefetchScalarGridSpec(
             num_scalar_prefetch=1,
             grid=(1,),
             in_specs=in_specs,
-            out_specs=pl.BlockSpec((1, 2 * half, channels), lambda i, s: (tap, 0, 0)),
+            out_specs=keep,
+            scratch_shapes=[pltpu.SemaphoreType.DMA((2,))],
         ),
-        out_shape=jax.ShapeDtypeStruct((3, 2 * half, channels), f32),
+        out_shape=jax.ShapeDtypeStruct((rows, channels), f32),
         input_output_aliases=aliases,
         cost_estimate=cost(0, 16 * half * channels),
         compiler_params=limit(),
@@ -642,15 +654,19 @@
         return lax.ppermute(x, "slab", [(i, i ^ bit) for i in range(slabs)])
 
     weight_grad = None
-    for tap in range(3):
-        keep, give = filter_terms(tap, ring, spread, high_field, low_field)
+    taps = filters.shape[0]
+    cuts = (0, 12, 18, taps)
+    for begin, end in zip(cuts, cuts[1:]):
+        keep, give = filter_terms(begin, end, scale, ring, spread, high_field, low_field)
         keep = keep + swap(give, 1)
         bit = 2
         while bit < slabs:
             keep = keep + swap(keep, bit)
             bit *= 2
         other = swap(keep, 1)
-        weight_grad = place(tap, ring, keep, other, weight_grad, scale)
+        weight_grad = place(
+            begin * out_rows, ring, keep, other, weight_grad, taps * out_rows
+        )
 
     piece = (chan, run * area)
     part = (chan // 2, run * area)

time: 184 us -> 179 us (0.973)
  waiting for transfers between devices: 60.7 us -> 54.4 us
    ppermute x24, waiting for transfers between devices: 48.3 us -> 42.6 us  [send(): return lax.ppermute(x, 'filt', pairs)]
  transfers between devices with their start and end apart: 41 -> 41, of which waited for: 10 -> 11; matrix products, arithmetic and copies ran while one was open for 1% -> 1% of each run, Pallas kernels for 34% -> 37%
where the time goes in v3:
time: 179 us; the launch traced here: 178 us
  Pallas kernels  79.8 us (45%)
  waiting for transfers between devices  54.4 us (30%)
  starting transfers between devices  38.5 us (22%)
  local copies, waits for them, and re-layouts  3.61 us (2%)
    ppermute x24, waiting for transfers between devices, send(): return lax.ppermute(x, 'filt', pairs)  42.6 us
    pallas_call x5, Pallas kernels, forward(): pl.pallas_call(functools.partial(forward_kernel, counts, places, rim_plac...  27 us
    ppermute x24, starting transfers between devices, send(): return lax.ppermute(x, 'filt', pairs)  25.8 us
    pallas_call x3, Pallas kernels, filter_terms(): pl.pallas_call(functools.partial(filter_kernel, begin, end, scale), grid_...  14.1 us
    pallas_call x2, Pallas kernels, inner_terms(): pl.pallas_call(functools.partial(inner_kernel, begin, planes), out_shape=...  12.1 us
    ppermute x9, waiting for transfers between devices, swap(): return lax.ppermute(x, 'slab', [(i, i ^ bit) for i in range(slabs)])  11.8 us
    pallas_call x1, Pallas kernels, prepare(): pl.pallas_call(functools.partial(prepare_kernel, chan), grid=(channels //...  7.36 us
    pallas_call x9, Pallas kernels, summed(): pl.pallas_call(kernel, grid_spec=pltpu.PrefetchScalarGridSpec(num_scalar_...  6.23 us
  transfers between devices with their start and end apart: 41, of which 11 were waited for; matrix products, arithmetic and copies ran while one was open for 1% of the time, Pallas kernels for 37%

profile of v3, /device:TPU:0, one launch (start us, length us, event | category | flops | bytes accessed | tf_op | source)
XLA Modules:
  0.0 178.2 jit_solution(10580578543786929267)
XLA Ops:
  0.6 3.0 %collective-permute-start.4 = (f32[64,8,256]{2,1,0:T(8,128)}, f32[64,8,256]{2,1,0:T(8,128)S(1)}, u32[]{:S(2)}, u32[]{:S(2)}) collective-permute-start(f32[64,8,256]{2,1,0:T(8,128)} %refs_0_.3), channel_id=1, source_target_pairs={{2,0},{4,2},{6,4},{7,6},{5,7},{3,5},{1,3},{0,1},{10,8},{12,10},{14... | collective-permute-start | bytes 1572872 | tf_op jit(solution)/shard_map/ppermute | solution.py:604
  3.8 12.1 %collective-permute-done.4.refs_2_.refs_1_ = f32[64,8,256]{2,1,0:T(8,128)S(1)} collective-permute-done((f32[64,8,256]{2,1,0:T(8,128)}, f32[64,8,256]{2,1,0:T(8,128)S(1)}, u32[]{:S(2)}, u32[]{:S(2)}) %collective-permute-start.4) | collective-permute-done | bytes 524320 | tf_op jit(solution)/shard_map/ppermute | solution.py:604
  15.9 1.7 collective-permute-start.5
  17.9 11.1 %collective-permute-done.5.refs_1_ = f32[64,8,256]{2,1,0:T(8,128)S(1)} collective-permute-done((f32[64,8,256]{2,1,0:T(8,128)S(1)}, f32[64,8,256]{2,1,0:T(8,128)S(1)}, u32[]{:S(2)}, u32[]{:S(2)}) %collective-permute-start.5) | collective-permute-done | bytes 524320 | tf_op jit(solution)/shard_map/ppermute | solution.py:604
  32.9 7.4 %prepare.1 = (bf16[3,8,576,192]{3,2,1,0:T(8,128)(2,1)}, bf16[512,1728]{1,0:T(8,128)(2,1)}, bf16[512,1728]{1,0:T(8,128)(2,1)}) custom-call(f32[27,64,512]{2,1,0:T(8,128)} %filters.1), custom_call_target="tpu_custom_call" | custom-call | bytes 17694720 | tf_op jit(solution)/shard_map/prepare/pallas_call | solution.py:82
  42.0 3.9 %forward.5 = (f32[8,64,256]{2,1,0:T(8,128)S(1)}, bf16[512,2560]{1,0:T(8,128)(2,1)S(1)}, bf16[512,2560]{1,0:T(8,128)(2,1)S(1)}) custom-call(s32[11]{0:T(128)S(1)} %dynamic-slice_bitcast_fusion.ring, f32[64,8,256]{2,1,0:T(8,128)S(1)} %copy-done, bf16[3,8,576,192]{3,2,1,0:T(8,128)(2,1)} %get-tuple-element.55.refs_1_.refs_2_.source), custom_call_target="tpu_custom_call" | custom-call | flops 1358954496 | bytes 1310720 | tf_op jit(solution)/shard_map/forward/pallas_call | solution.py:242
  46.2 1.7 collective-permute-start.11
  50.1 5.8 %forward.6 = (f32[8,64,256]{2,1,0:T(8,128)S(1)}, bf16[512,2560]{1,0:T(8,128)(2,1)S(1)}, bf16[512,2560]{1,0:T(8,128)(2,1)S(1)}) custom-call(s32[11]{0:T(128)S(1)} %dynamic-slice_bitcast_fusion.ring, f32[64,8,256]{2,1,0:T(8,128)S(1)} %collective-permute-done.refs_1_.refs_0_, ...), custom_call_target="tpu_custom_call", output_to_operand_aliasing={{0}: (4, {}), {1}: (5, {}), {2}: (6, {})} | custom-call | flops 2717908992 | bytes 2621440 | tf_op jit(solution)/shard_map/forward/pallas_call | solution.py:242
  56.1 1.7 collective-permute-start.9
  57.9 6.9 %forward.7 = (f32[8,64,256]{2,1,0:T(8,128)S(1)}, bf16[512,2560]{1,0:T(8,128)(2,1)S(1)}, bf16[512,2560]{1,0:T(8,128)(2,1)S(1)}) custom-call(s32[11]{0:T(128)S(1)} %dynamic-slice_bitcast_fusion.ring, f32[64,8,256]{2,1,0:T(8,128)S(1)} %collective-permute-done.1.refs_0_, ...), custom_call_target="tpu_custom_call", output_to_operand_aliasing={{0}: (6, {}), {1}: (7, {}), {2}: (8, {})} | custom-call | flops 2717908992 | bytes 2621440 | tf_op jit(solution)/shard_map/forward/pallas_call | solution.py:242
  65.1 1.7 collective-permute-start.13
  66.8 6.5 %forward.8 = (f32[8,64,256]{2,1,0:T(8,128)S(1)}, bf16[512,2560]{1,0:T(8,128)(2,1)S(1)}, bf16[512,2560]{1,0:T(8,128)(2,1)S(1)}) custom-call(s32[11]{0:T(128)S(1)} %dynamic-slice_bitcast_fusion.ring, f32[64,8,256]{2,1,0:T(8,128)S(1)} %collective-permute-done.2.refs_0_, ...), custom_call_target="tpu_custom_call", output_to_operand_aliasing={{0}: (6, {}), {1}: (7, {}), {2}: (8, {})} | custom-call | flops 2717908992 | bytes 2621440 | tf_op jit(solution)/shard_map/forward/pallas_call | solution.py:242
  73.4 3.9 %forward.9 = (f32[8,64,256]{2,1,0:T(8,128)S(1)}, bf16[512,2560]{1,0:T(8,128)(2,1)S(1)}, bf16[512,2560]{1,0:T(8,128)(2,1)S(1)}) custom-call(s32[11]{0:T(128)S(1)} %dynamic-slice_bitcast_fusion.ring, f32[32,8,256]{2,1,0:T(8,128)S(1)} %collective-permute-done.3.refs_0_.refs_2_, ...), custom_call_target="tpu_custom_call", output_to_operand_aliasing={{0}: (4, {}), {1}: (5, {}), {2}: (6, {})} | custom-call | flops 1358954496 | bytes 1310720 | tf_op jit(solution)/shard_map/forward/pallas_call | solution.py:242
  77.3 5.3 %middle.1 = (f32[8,64,256]{2,1,0:T(8,128)S(1)}, bf16[2,10,576,256]{3,2,1,0:T(8,128)(2,1)S(1)}, bf16[512,2560]{1,0:T(8,128)(2,1)S(1)}, bf16[512,2560]{1,0:T(8,128)(2,1)S(1)}) custom-call(s32[11]{0:T(128)S(1)} %dynamic-slice_bitcast_fusion.ring, f32[8,64,256]{2,1,0:T(8,128)S(1)} %get-tuple-element.72.total, ...), custom_call_target="tpu_custom_call", output_to_operand_aliasing={{2}: (6, {}), {3}: (7, {})} | custom-call | bytes 9437184 | tf_op jit(solution)/shard_map/middle/pallas_call | solution.py:332
  84.0 6.1 %inner_terms.3.inner.up_inner.down_inner.refs_4_ = f32[8,64,1024]{2,1,0:T(8,128)S(1)} custom-call(bf16[2,10,576,256]{3,2,1,0:T(8,128)(2,1)S(1)} %get-tuple-element.78.spread, bf16[512,1728]{1,0:T(8,128)(2,1)S(1)} %copy-done.3, bf16[512,1728]{1,0:T(8,128)(2,1)S(1)} %copy-done.4), custom_call_target="tpu_custom_call" | custom-call | flops 5435817984 | bytes 9437184 | tf_op jit(solution)/shard_map/inner_terms/pallas_call | solution.py:412
  90.1 1.7 collective-permute-start.23
  91.9 6.5 %filter_terms.5 = (f32[384,512]{1,0:T(8,128)S(1)}, f32[384,512]{1,0:T(8,128)S(1)}) custom-call(s32[11]{0:T(128)S(1)} %dynamic-slice_bitcast_fusion.ring, bf16[2,10,576,256]{3,2,1,0:T(8,128)(2,1)S(1)} %get-tuple-element.78.spread, bf16[512,2560]{1,0:T(8,128)(2,1)S(1)} %get-tuple-element.99.high, bf16[512,2560]{1,0:T(8,128)(2,1)S(1)} %get-tuple-element.100.low), custom_call_target="tpu_custom_call" | custom-call | flops 6039797760 | bytes 11141120 | tf_op jit(solution)/shard_map/filter_terms/pallas_call | solution.py:464
  98.4 4.5 %filter_terms.3 = (f32[288,512]{1,0:T(8,128)S(1)}, f32[288,512]{1,0:T(8,128)S(1)}) custom-call(s32[11]{0:T(128)S(1)} %dynamic-slice_bitcast_fusion.ring, bf16[2,10,576,256]{3,2,1,0:T(8,128)(2,1)S(1)} %get-tuple-element.78.spread, bf16[512,2560]{1,0:T(8,128)(2,1)S(1)} %get-tuple-element.99.high, bf16[512,2560]{1,0:T(8,128)(2,1)S(1)} %get-tuple-element.100.low), custom_call_target="tpu_custom_call" | custom-call | flops 4529848320 | bytes 11141120 | tf_op jit(solution)/shard_map/filter_terms/pallas_call | solution.py:464
  106.1 6.1 %inner_terms.2.inner.up_inner.down_inner.refs_0_ = f32[8,64,1024]{2,1,0:T(8,128)S(1)} custom-call(bf16[2,10,576,256]{3,2,1,0:T(8,128)(2,1)S(1)} %get-tuple-element.78.spread, bf16[512,1728]{1,0:T(8,128)(2,1)S(1)} %copy-done.3, bf16[512,1728]{1,0:T(8,128)(2,1)S(1)} %copy-done.4), custom_call_target="tpu_custom_call" | custom-call | flops 5435817984 | bytes 9437184 | tf_op jit(solution)/shard_map/inner_terms/pallas_call | solution.py:412
  114.9 1.6 collective-permute-start.26
  118.3 3.2 %filter_terms.4 = (f32[192,512]{1,0:T(8,128)S(1)}, f32[192,512]{1,0:T(8,128)S(1)}) custom-call(s32[11]{0:T(128)S(1)} %dynamic-slice_bitcast_fusion.ring, bf16[2,10,576,256]{3,2,1,0:T(8,128)(2,1)S(1)} %get-tuple-element.78.spread, bf16[512,2560]{1,0:T(8,128)(2,1)S(1)} %get-tuple-element.99.high, bf16[512,2560]{1,0:T(8,128)(2,1)S(1)} %get-tuple-element.100.low), custom_call_target="tpu_custom_call" | custom-call | flops 3019898880 | bytes 11141120 | tf_op jit(solution)/shard_map/filter_terms/pallas_call | solution.py:464
  122.6 5.4 %collective-permute-done.16.down = f32[32,1024]{1,0:T(8,128)S(1)} collective-permute-done((f32[32,1024]{1,0:T(8,128)S(1)}, f32[32,1024]{1,0:T(8,128)S(1)}, u32[]{:S(2)}, u32[]{:S(2)}) %collective-permute-start.16) | collective-permute-done | bytes 131104 | tf_op jit(solution)/shard_map/ppermute | solution.py:604
  130.7 2.3 %collective-permute-done.27.down = f32[64,1024]{1,0:T(8,128)S(1)} collective-permute-done((f32[64,1024]{1,0:T(8,128)S(1)}, f32[64,1024]{1,0:T(8,128)S(1)}, u32[]{:S(2)}, u32[]{:S(2)}) %collective-permute-start.27) | collective-permute-done | bytes 262176 | tf_op jit(solution)/shard_map/ppermute | solution.py:604
  134.1 1.6 collective-permute-start.28
  136.2 2.5 %collective-permute-start.36 = (f32[192,512]{1,0:T(8,128)S(1)}, f32[192,512]{1,0:T(8,128)S(1)}, u32[]{:S(2)}, u32[]{:S(2)}) collective-permute-start(f32[192,512]{1,0:T(8,128)S(1)} %add.29), channel_id=1, source_target_pairs={{0,16},{8,24},{16,0},{24,8},{1,17},{9,25},{17,1},{25,9},{2,18},{10... | collective-permute-start | bytes 1179656 | tf_op jit(solution)/shard_map/ppermute | solution.py:654
  138.7 2.1 %collective-permute-done.18.down = f32[64,1024]{1,0:T(8,128)S(1)} collective-permute-done((f32[64,1024]{1,0:T(8,128)S(1)}, f32[64,1024]{1,0:T(8,128)S(1)}, u32[]{:S(2)}, u32[]{:S(2)}) %collective-permute-start.18) | collective-permute-done | bytes 262176 | tf_op jit(solution)/shard_map/ppermute | solution.py:604
  141.9 1.6 collective-permute-start.19
  143.8 6.0 %collective-permute-done.33 = f32[288,512]{1,0:T(8,128)S(1)} collective-permute-done((f32[288,512]{1,0:T(8,128)S(1)}, f32[288,512]{1,0:T(8,128)S(1)}, u32[]{:S(2)}, u32[]{:S(2)}) %collective-permute-start.33) | collective-permute-done | bytes 589856 | tf_op jit(solution)/shard_map/ppermute | solution.py:654
  151.0 5.8 %collective-permute-done.36 = f32[192,512]{1,0:T(8,128)S(1)} collective-permute-done((f32[192,512]{1,0:T(8,128)S(1)}, f32[192,512]{1,0:T(8,128)S(1)}, u32[]{:S(2)}, u32[]{:S(2)}) %collective-permute-start.36) | collective-permute-done | bytes 393248 | tf_op jit(solution)/shard_map/ppermute | solution.py:654
  159.7 4.2 %collective-permute-done.30.refs_6_ = f32[64,1024]{1,0:T(8,128)S(1)} collective-permute-done((f32[64,1024]{1,0:T(8,128)S(1)}, f32[64,1024]{1,0:T(8,128)S(1)}, u32[]{:S(2)}, u32[]{:S(2)}) %collective-permute-start.30) | collective-permute-done | bytes 262176 | tf_op jit(solution)/shard_map/ppermute | solution.py:604
  166.8 3.4 %collective-permute-done.21.refs_2_ = f32[64,1024]{1,0:T(8,128)S(1)} collective-permute-done((f32[64,1024]{1,0:T(8,128)S(1)}, f32[64,1024]{1,0:T(8,128)S(1)}, u32[]{:S(2)}, u32[]{:S(2)}) %collective-permute-start.21) | collective-permute-done | bytes 262176 | tf_op jit(solution)/shard_map/ppermute | solution.py:604
  173.2 1.7 place.3.refs_2_
  (101 shorter events, 37.8 us)
Async XLA Ops:
  0.6 15.2 %collective-permute-start.4 = (f32[64,8,256]{2,1,0:T(8,128)}, f32[64,8,256]{2,1,0:T(8,128)S(1)}, u32[]{:S(2)}, u32[]{:S(2)}) collective-permute-start(f32[64,8,256]{2,1,0:T(8,128)} %refs_0_.3), channel_id=1, source_target_pairs={{2,0},{4,2},{6,4},{7,6},{5,7},{3,5},{1,3},{0,1},{10,8},{12,10},{14... | collective-permute-start | bytes 1572872 | tf_op jit(solution)/shard_map/ppermute | solution.py:604
  3.6 13.9 %collective-permute-start = (f32[64,8,256]{2,1,0:T(8,128)}, f32[64,8,256]{2,1,0:T(8,128)S(1)}, u32[]{:S(2)}, u32[]{:S(2)}) collective-permute-start(f32[64,8,256]{2,1,0:T(8,128)} %refs_0_.3), channel_id=1, source_target_pairs={{0,2},{2,4},{4,6},{6,7},{7,5},{5,3},{3,1},{1,0},{8,10},{10,12},{12... | collective-permute-start | bytes 1572872 | tf_op jit(solution)/shard_map/ppermute | solution.py:604
  15.9 13.1 %collective-permute-start.5 = (f32[64,8,256]{2,1,0:T(8,128)S(1)}, f32[64,8,256]{2,1,0:T(8,128)S(1)}, u32[]{:S(2)}, u32[]{:S(2)}) collective-permute-start(f32[64,8,256]{2,1,0:T(8,128)S(1)} %collective-permute-done.4.refs_2_.refs_1_), channel_id=1, source_target_pairs={{2,0},{4,2},{6,4},{7,6},{5,7},{3,5},{1,3},{0,1},{10,8},{12,10},{14... | collective-permute-start | bytes 1572872 | tf_op jit(solution)/shard_map/ppermute | solution.py:604
  17.5 12.8 %collective-permute-start.1 = (f32[64,8,256]{2,1,0:T(8,128)S(1)}, f32[64,8,256]{2,1,0:T(8,128)S(1)}, u32[]{:S(2)}, u32[]{:S(2)}) collective-permute-start(f32[64,8,256]{2,1,0:T(8,128)S(1)} %collective-permute-done.refs_1_.refs_0_), channel_id=1, source_target_pairs={{0,2},{2,4},{4,6},{6,7},{7,5},{5,3},{3,1},{1,0},{8,10},{10,12},{12... | collective-permute-start | bytes 1572872 | tf_op jit(solution)/shard_map/ppermute | solution.py:604
  29.0 18.9 %collective-permute-start.6 = (f32[64,8,256]{2,1,0:T(8,128)S(1)}, f32[64,8,256]{2,1,0:T(8,128)S(1)}, u32[]{:S(2)}, u32[]{:S(2)}) collective-permute-start(f32[64,8,256]{2,1,0:T(8,128)S(1)} %collective-permute-done.5.refs_1_), channel_id=1, source_target_pairs={{2,0},{4,2},{6,4},{7,6},{5,7},{3,5},{1,3},{0,1},{10,8},{12,10},{14... | collective-permute-start | bytes 1572872 | tf_op jit(solution)/shard_map/ppermute | solution.py:604
  30.3 19.0 %collective-permute-start.2 = (f32[64,8,256]{2,1,0:T(8,128)S(1)}, f32[64,8,256]{2,1,0:T(8,128)S(1)}, u32[]{:S(2)}, u32[]{:S(2)}) collective-permute-start(f32[64,8,256]{2,1,0:T(8,128)S(1)} %collective-permute-done.1.refs_0_), channel_id=1, source_target_pairs={{0,2},{2,4},{4,6},{6,7},{7,5},{5,3},{3,1},{1,0},{8,10},{10,12},{12... | collective-permute-start | bytes 1572872 | tf_op jit(solution)/shard_map/ppermute | solution.py:604
  46.1 10.0 %collective-permute-start.10 = (f32[192,256]{1,0:T(8,128)S(1)}, f32[192,256]{1,0:T(8,128)S(1)}, u32[]{:S(2)}, u32[]{:S(2)}) collective-permute-start(f32[192,256]{1,0:T(8,128)S(1)} %get-tuple-element.58), channel_id=1, source_target_pairs={{0,8},{8,16},{16,24},{24,0},{1,9},{9,17},{17,25},{25,1},{2,10},{10... | collective-permute-start | bytes 589832 | tf_op jit(solution)/shard_map/ppermute | solution.py:633
  46.2 11.7 %collective-permute-start.11 = (f32[192,256]{1,0:T(8,128)S(1)}, f32[192,256]{1,0:T(8,128)S(1)}, u32[]{:S(2)}, u32[]{:S(2)}) collective-permute-start(f32[192,256]{1,0:T(8,128)S(1)} %get-tuple-element.59), channel_id=1, source_target_pairs={{8,0},{16,8},{24,16},{0,24},{9,1},{17,9},{25,17},{1,25},{10,2},{18... | collective-permute-start | bytes 589832 | tf_op jit(solution)/shard_map/ppermute | solution.py:633
  47.9 16.9 %collective-permute-start.7 = (f32[32,8,256]{2,1,0:T(8,128)S(1)}, f32[32,8,256]{2,1,0:T(8,128)S(1)}, u32[]{:S(2)}, u32[]{:S(2)}) collective-permute-start(f32[32,8,256]{2,1,0:T(8,128)S(1)} %slice.9), channel_id=1, source_target_pairs={{2,0},{4,2},{6,4},{7,6},{5,7},{3,5},{1,3},{0,1},{10,8},{12,10},{14... | collective-permute-start | bytes 786440 | tf_op jit(solution)/shard_map/ppermute | solution.py:604
  49.4 15.4 %collective-permute-start.3 = (f32[32,8,256]{2,1,0:T(8,128)S(1)}, f32[32,8,256]{2,1,0:T(8,128)S(1)}, u32[]{:S(2)}, u32[]{:S(2)}) collective-permute-start(f32[32,8,256]{2,1,0:T(8,128)S(1)} %slice.8), channel_id=1, source_target_pairs={{0,2},{2,4},{4,6},{6,7},{7,5},{5,3},{3,1},{1,0},{8,10},{10,12},{12... | collective-permute-start | bytes 786440 | tf_op jit(solution)/shard_map/ppermute | solution.py:604
  56.1 10.8 %collective-permute-start.8 = (f32[128,256]{1,0:T(8,128)S(1)}, f32[128,256]{1,0:T(8,128)S(1)}, u32[]{:S(2)}, u32[]{:S(2)}) collective-permute-start(f32[128,256]{1,0:T(8,128)S(1)} %get-tuple-element.56), channel_id=1, source_target_pairs={{0,8},{8,16},{16,24},{24,0},{1,9},{9,17},{17,25},{25,1},{2,10},{10... | collective-permute-start | bytes 393224 | tf_op jit(solution)/shard_map/ppermute | solution.py:633
  56.1 10.7 %collective-permute-start.9 = (f32[128,256]{1,0:T(8,128)S(1)}, f32[128,256]{1,0:T(8,128)S(1)}, u32[]{:S(2)}, u32[]{:S(2)}) collective-permute-start(f32[128,256]{1,0:T(8,128)S(1)} %get-tuple-element.57), channel_id=1, source_target_pairs={{8,0},{16,8},{24,16},{0,24},{9,1},{17,9},{25,17},{1,25},{10,2},{18... | collective-permute-start | bytes 393224 | tf_op jit(solution)/shard_map/ppermute | solution.py:633
  65.0 12.2 %collective-permute-start.12 = (f32[192,256]{1,0:T(8,128)S(1)}, f32[192,256]{1,0:T(8,128)S(1)}, u32[]{:S(2)}, u32[]{:S(2)}) collective-permute-start(f32[192,256]{1,0:T(8,128)S(1)} %get-tuple-element.73), channel_id=1, source_target_pairs={{0,8},{8,16},{16,24},{24,0},{1,9},{9,17},{17,25},{25,1},{2,10},{10... | collective-permute-start | bytes 589832 | tf_op jit(solution)/shard_map/ppermute | solution.py:633
  65.1 12.2 %collective-permute-start.13 = (f32[192,256]{1,0:T(8,128)S(1)}, f32[192,256]{1,0:T(8,128)S(1)}, u32[]{:S(2)}, u32[]{:S(2)}) collective-permute-start(f32[192,256]{1,0:T(8,128)S(1)} %get-tuple-element.74), channel_id=1, source_target_pairs={{8,0},{16,8},{24,16},{0,24},{9,1},{17,9},{25,17},{1,25},{10,2},{18... | collective-permute-start | bytes 589832 | tf_op jit(solution)/shard_map/ppermute | solution.py:633
  90.1 22.1 %collective-permute-start.14 = (f32[8,64,256]{2,1,0:T(8,128)S(1)}, f32[8,64,256]{2,1,0:T(8,128)S(1)}, u32[]{:S(2)}, u32[]{:S(2)}) collective-permute-start(f32[8,64,256]{2,1,0:T(8,128)S(1)} %get-tuple-element.81), channel_id=1, source_target_pairs={{0,8},{8,16},{16,24},{24,0},{1,9},{9,17},{17,25},{25,1},{2,10},{10... | collective-permute-start | bytes 1572872 | tf_op jit(solution)/shard_map/ppermute | solution.py:643
  90.1 13.3 %collective-permute-start.23 = (f32[8,64,256]{2,1,0:T(8,128)S(1)}, f32[8,64,256]{2,1,0:T(8,128)S(1)}, u32[]{:S(2)}, u32[]{:S(2)}) collective-permute-start(f32[8,64,256]{2,1,0:T(8,128)S(1)} %get-tuple-element.90), channel_id=1, source_target_pairs={{8,0},{16,8},{24,16},{0,24},{9,1},{17,9},{25,17},{1,25},{10,2},{18... | collective-permute-start | bytes 1572872 | tf_op jit(solution)/shard_map/ppermute | solution.py:644
  98.3 18.2 %collective-permute-start.38 = (f32[384,512]{1,0:T(8,128)S(1)}, f32[384,512]{1,0:T(8,128)S(1)}, u32[]{:S(2)}, u32[]{:S(2)}) collective-permute-start(f32[384,512]{1,0:T(8,128)S(1)} %get-tuple-element.106), channel_id=1, source_target_pairs={{0,8},{8,0},{16,24},{24,16},{1,9},{9,1},{17,25},{25,17},{2,10},{10... | collective-permute-start | bytes 2359304 | tf_op jit(solution)/shard_map/ppermute | solution.py:654
  102.9 18.7 %collective-permute-start.32 = (f32[288,512]{1,0:T(8,128)S(1)}, f32[288,512]{1,0:T(8,128)S(1)}, u32[]{:S(2)}, u32[]{:S(2)}) collective-permute-start(f32[288,512]{1,0:T(8,128)S(1)} %get-tuple-element.102), channel_id=1, source_target_pairs={{0,8},{8,0},{16,24},{24,16},{1,9},{9,1},{17,25},{25,17},{2,10},{10... | collective-permute-start | bytes 1769480 | tf_op jit(solution)/shard_map/ppermute | solution.py:654
  104.0 10.3 %collective-permute-start.24 = (f32[32,1024]{1,0:T(8,128)S(1)}, f32[32,1024]{1,0:T(8,128)S(1)}, u32[]{:S(2)}, u32[]{:S(2)}) collective-permute-start(f32[32,1024]{1,0:T(8,128)S(1)} %get-tuple-element.91), channel_id=1, source_target_pairs={{0,2},{2,4},{4,6},{6,7},{7,5},{5,3},{3,1},{1,0},{8,10},{10,12},{12... | collective-permute-start | bytes 393224 | tf_op jit(solution)/shard_map/ppermute | solution.py:604
  112.8 9.3 %collective-permute-start.15 = (f32[32,1024]{1,0:T(8,128)S(1)}, f32[32,1024]{1,0:T(8,128)S(1)}, u32[]{:S(2)}, u32[]{:S(2)}) collective-permute-start(f32[32,1024]{1,0:T(8,128)S(1)} %get-tuple-element.82), channel_id=1, source_target_pairs={{0,2},{2,4},{4,6},{6,7},{7,5},{5,3},{3,1},{1,0},{8,10},{10,12},{12... | collective-permute-start | bytes 393224 | tf_op jit(solution)/shard_map/ppermute | solution.py:604
  114.9 14.2 %collective-permute-start.26 = (f32[64,1024]{1,0:T(8,128)S(1)}, f32[64,1024]{1,0:T(8,128)S(1)}, u32[]{:S(2)}, u32[]{:S(2)}) collective-permute-start(f32[64,1024]{1,0:T(8,128)S(1)} %get-tuple-element.93), channel_id=1, source_target_pairs={{0,2},{2,4},{4,6},{6,7},{7,5},{5,3},{3,1},{1,0},{8,10},{10,12},{12... | collective-permute-start | bytes 786440 | tf_op jit(solution)/shard_map/ppermute | solution.py:604
  116.7 25.3 %collective-permute-start.39 = (f32[384,512]{1,0:T(8,128)S(1)}, f32[384,512]{1,0:T(8,128)S(1)}, u32[]{:S(2)}, u32[]{:S(2)}) collective-permute-start(f32[384,512]{1,0:T(8,128)S(1)} %add.31), channel_id=1, source_target_pairs={{0,16},{8,24},{16,0},{24,8},{1,17},{9,25},{17,1},{25,9},{2,18},{10... | collective-permute-start | bytes 2359304 | tf_op jit(solution)/shard_map/ppermute | solution.py:654
  121.5 12.7 %collective-permute-start.35 = (f32[192,512]{1,0:T(8,128)S(1)}, f32[192,512]{1,0:T(8,128)S(1)}, u32[]{:S(2)}, u32[]{:S(2)}) collective-permute-start(f32[192,512]{1,0:T(8,128)S(1)} %get-tuple-element.104), channel_id=1, source_target_pairs={{0,8},{8,0},{16,24},{24,16},{1,9},{9,1},{17,25},{25,17},{2,10},{10... | collective-permute-start | bytes 1179656 | tf_op jit(solution)/shard_map/ppermute | solution.py:654
  122.1 11.0 %collective-permute-start.27 = (f32[64,1024]{1,0:T(8,128)S(1)}, f32[64,1024]{1,0:T(8,128)S(1)}, u32[]{:S(2)}, u32[]{:S(2)}) collective-permute-start(f32[64,1024]{1,0:T(8,128)S(1)} %get-tuple-element.94), channel_id=1, source_target_pairs={{2,0},{4,2},{6,4},{7,6},{5,7},{3,5},{1,3},{0,1},{10,8},{12,10},{14... | collective-permute-start | bytes 786440 | tf_op jit(solution)/shard_map/ppermute | solution.py:604
  128.0 21.8 %collective-permute-start.33 = (f32[288,512]{1,0:T(8,128)S(1)}, f32[288,512]{1,0:T(8,128)S(1)}, u32[]{:S(2)}, u32[]{:S(2)}) collective-permute-start(f32[288,512]{1,0:T(8,128)S(1)} %add.27), channel_id=1, source_target_pairs={{0,16},{8,24},{16,0},{24,8},{1,17},{9,25},{17,1},{25,9},{2,18},{10... | collective-permute-start | bytes 1769480 | tf_op jit(solution)/shard_map/ppermute | solution.py:654
  134.1 9.6 %collective-permute-start.28 = (f32[64,1024]{1,0:T(8,128)S(1)}, f32[64,1024]{1,0:T(8,128)S(1)}, u32[]{:S(2)}, u32[]{:S(2)}) collective-permute-start(f32[64,1024]{1,0:T(8,128)S(1)} %get-tuple-element.95), channel_id=1, source_target_pairs={{0,2},{2,4},{4,6},{6,7},{7,5},{5,3},{3,1},{1,0},{8,10},{10,12},{12... | collective-permute-start | bytes 786440 | tf_op jit(solution)/shard_map/ppermute | solution.py:604
  136.2 20.7 %collective-permute-start.36 = (f32[192,512]{1,0:T(8,128)S(1)}, f32[192,512]{1,0:T(8,128)S(1)}, u32[]{:S(2)}, u32[]{:S(2)}) collective-permute-start(f32[192,512]{1,0:T(8,128)S(1)} %add.29), channel_id=1, source_target_pairs={{0,16},{8,24},{16,0},{24,8},{1,17},{9,25},{17,1},{25,9},{2,18},{10... | collective-permute-start | bytes 1179656 | tf_op jit(solution)/shard_map/ppermute | solution.py:654
  140.9 9.5 %collective-permute-start.29 = (f32[64,1024]{1,0:T(8,128)S(1)}, f32[64,1024]{1,0:T(8,128)S(1)}, u32[]{:S(2)}, u32[]{:S(2)}) collective-permute-start(f32[64,1024]{1,0:T(8,128)S(1)} %get-tuple-element.96), channel_id=1, source_target_pairs={{2,0},{4,2},{6,4},{7,6},{5,7},{3,5},{1,3},{0,1},{10,8},{12,10},{14... | collective-permute-start | bytes 786440 | tf_op jit(solution)/shard_map/ppermute | solution.py:604
  141.9 16.5 %collective-permute-start.19 = (f32[64,1024]{1,0:T(8,128)S(1)}, f32[64,1024]{1,0:T(8,128)S(1)}, u32[]{:S(2)}, u32[]{:S(2)}) collective-permute-start(f32[64,1024]{1,0:T(8,128)S(1)} %get-tuple-element.86), channel_id=1, source_target_pairs={{0,2},{2,4},{4,6},{6,7},{7,5},{5,3},{3,1},{1,0},{8,10},{10,12},{12... | collective-permute-start | bytes 786440 | tf_op jit(solution)/shard_map/ppermute | solution.py:604
  143.7 29.5 %collective-permute-start.40 = (f32[384,512]{1,0:T(8,128)S(1)}, f32[384,512]{1,0:T(8,128)S(1)}, u32[]{:S(2)}, u32[]{:S(2)}) collective-permute-start(f32[384,512]{1,0:T(8,128)S(1)} %add.32.refs_0_), channel_id=1, source_target_pairs={{0,8},{8,0},{16,24},{24,16},{1,9},{9,1},{17,25},{25,17},{2,10},{10... | collective-permute-start | bytes 2359304 | tf_op jit(solution)/shard_map/ppermute | solution.py:654
  150.3 26.1 %collective-permute-start.34 = (f32[288,512]{1,0:T(8,128)S(1)}, f32[288,512]{1,0:T(8,128)S(1)}, u32[]{:S(2)}, u32[]{:S(2)}) collective-permute-start(f32[288,512]{1,0:T(8,128)S(1)} %add.28.refs_0_), channel_id=1, source_target_pairs={{0,8},{8,0},{16,24},{24,16},{1,9},{9,1},{17,25},{25,17},{2,10},{10... | collective-permute-start | bytes 1769480 | tf_op jit(solution)/shard_map/ppermute | solution.py:654
  159.0 16.0 %collective-permute-start.37 = (f32[192,512]{1,0:T(8,128)S(1)}, f32[192,512]{1,0:T(8,128)S(1)}, u32[]{:S(2)}, u32[]{:S(2)}) collective-permute-start(f32[192,512]{1,0:T(8,128)S(1)} %add.30.refs_0_), channel_id=1, source_target_pairs={{0,8},{8,0},{16,24},{24,16},{1,9},{9,1},{17,25},{25,17},{2,10},{10... | collective-permute-start | bytes 1179656 | tf_op jit(solution)/shard_map/ppermute | solution.py:654
  (15 other events, 83.3 us)

commit v4 on v3

--- a/solution.py
+++ b/solution.py
@@ -546,14 +546,54 @@
         down_out[0:rest] = value[0:rest]
 
 
-def closing_kernel(ring, *refs):
-    chains, out = (refs[0:4], refs[4:8]), refs[8]
+def closing_kernel(begin, ring, *refs):
+    chains, (mine, other, _, out, whole_out, sems) = (refs[0:4], refs[4:8]), refs[8:]
+    half = mine.shape[0]
+    side = ring[ring.shape[0] - 1]
+    copies = []
+    for n, (part, at) in enumerate(((mine, side), (other, 1 - side))):
+        rows = pl.ds(pl.multiple_of(begin + at * half, 8), half)
+        copies.append(pltpu.make_async_copy(part, whole_out.at[rows], sems.at[n]))
+        copies[-1].start()
     area = out.shape[2]
     values = []
     for first, (inner, rim, up, down) in zip((True, False), chains):
         value = local_sum(ring, inner, rim, first) + up[...] + down[...]
         values += [value[:, at : at + area] for at in range(0, value.shape[1], area)]
     out[...] = jnp.swapaxes(jnp.stack(values), 0, 1)
+    for copy in copies:
+        copy.wait()
+
+
+def closing(ring, pieces, shape, begin, mine, other, carry):
+    keep = pl.BlockSpec(memory_space=pltpu.HBM)
+    specs, args = [], []
+    for piece in pieces:
+        if isinstance(piece, tuple):
+            array, k = piece
+            specs.append(pl.BlockSpec((1,) + array.shape[1:], lambda i, s, k=k: (s[k], 0, 0)))
+            args.append(array)
+        else:
+            specs.append(whole(piece.shape))
+            args.append(piece)
+    return pl.pallas_call(
+        functools.partial(closing_kernel, begin),
+        grid_spec=pltpu.PrefetchScalarGridSpec(
+            num_scalar_prefetch=1,
+            grid=(1,),
+            in_specs=specs + [whole(mine.shape), whole(other.shape), keep],
+            out_specs=[whole(shape), keep],
+            scratch_shapes=[pltpu.SemaphoreType.DMA((2,))],
+        ),
+        out_shape=[
+            jax.ShapeDtypeStruct(shape, f32),
+            jax.ShapeDtypeStruct(carry.shape, f32),
+        ],
+        input_output_aliases={len(args) + 3: 1},
+        cost_estimate=cost(0, 12 * math.prod(shape)),
+        compiler_params=limit(),
+        name="closing",
+    )(ring, *args, mine, other, carry)
 
 
 def summed(kernel, ring, pieces, outs):
@@ -642,10 +682,11 @@
     below, above = outer_terms(spread, back_high, back_low, chan)
     from_below = lax.ppermute(above, "slab", deeper)
     from_above = lax.ppermute(below, "slab", shallower)
-    run = depth // 2
+    runs = (depth * 5 // 8, depth - depth * 5 // 8)
     inner = []
     for c in range(2):
-        inner.append(inner_terms(c * run, run, spread, back_high, back_low, chan))
+        begin = 0 if c == 0 else runs[0]
+        inner.append(inner_terms(begin, runs[c], spread, back_high, back_low, chan))
     edge = [from_below, from_above]
 
     scale = math.sqrt(depth * slabs * area)
@@ -655,7 +696,7 @@
 
     weight_grad = None
     taps = filters.shape[0]
-    cuts = (0, 12, 18, taps)
+    cuts = (0, 13, 20, taps)
     for begin, end in zip(cuts, cuts[1:]):
         keep, give = filter_terms(begin, end, scale, ring, spread, high_field, low_field)
         keep = keep + swap(give, 1)
@@ -664,28 +705,29 @@
             keep = keep + swap(keep, bit)
             bit *= 2
         other = swap(keep, 1)
-        weight_grad = place(
-            begin * out_rows, ring, keep, other, weight_grad, taps * out_rows
-        )
-
-    piece = (chan, run * area)
-    part = (chan // 2, run * area)
+        if end < taps:
+            weight_grad = place(begin * out_rows, ring, keep, other, weight_grad, taps * out_rows)
+
+    pieces_of = [(chan, run * area) for run in runs]
+    parts_for = [(chan // 2, run * area) for run in runs]
     flows = []
     for c in range(2):
         kernel = functools.partial(opening_kernel, c == 0)
-        flows.append(summed(kernel, ring, [(inner[c], half), (edge[c], half)], [part, part]))
+        flows.append(summed(kernel, ring, [(inner[c], half), (edge[c], half)], [parts_for[c]] * 2))
     for step in range(half - 1, 0, -1):
         for c in range(2):
             up, down = flows[c]
             up, down = send(up, ring_up), send(down, ring_down)
             kernel = functools.partial(running_kernel, c == 0)
             pieces = [(x, p) for p in (step, count - step) for x in (inner[c], edge[c])]
-            flows[c] = summed(kernel, ring, pieces + [up, down], [piece, piece])
+            flows[c] = summed(kernel, ring, pieces + [up, down], [pieces_of[c]] * 2)
     pieces = []
     for c in range(2):
         up, down = flows[c]
         pieces += [(inner[c], 0), (edge[c], 0), send(up, ring_up), send(down, ring_down)]
-    (input_grad,) = summed(closing_kernel, ring, pieces, [(chan, depth, area)])
+    input_grad, weight_grad = closing(
+        ring, pieces, (chan, depth, area), cuts[-2] * out_rows, keep, other, weight_grad
+    )
     return activated, input_grad, weight_grad.reshape(filters.shape)
 
 

time: 179 us -> 169 us (0.944)
  waiting for transfers between devices: 54.4 us -> 46.4 us
    ppermute x9, waiting for transfers between devices: 11.8 us -> 2.92 us  [swap(): return lax.ppermute(x, 'slab', [(i, i ^ bit) for i in range(slabs)])]
    ppermute x9, starting transfers between devices: 5.53 us -> 2.83 us  [swap(): return lax.ppermute(x, 'slab', [(i, i ^ bit) for i in range(slabs)])]
    pallas_call x0 -> x1, Pallas kernels: none -> 2.28 us  [closing(): pl.pallas_call(functools.partial(closing_kernel, begin), grid_spec=pltpu....]
    pallas_call x3 -> x2, Pallas kernels: 4.71 us -> 3.23 us  [place(): pl.pallas_call(functools.partial(place_kernel, begin), grid_spec=pltpu.Pr...]
    pallas_call x9 -> x8, Pallas kernels: 6.23 us -> 4.79 us  [summed(): pl.pallas_call(kernel, grid_spec=pltpu.PrefetchScalarGridSpec(num_scalar_...]
  transfers between devices with their start and end apart: 41 -> 41, of which waited for: 11 -> 11; matrix products, arithmetic and copies ran while one was open for 1% -> 1% of each run, Pallas kernels for 37% -> 39%
where the time goes in v4:
time: 169 us
  Pallas kernels  80.1 us (47%)
  waiting for transfers between devices  46.4 us (27%)
  starting transfers between devices  36.9 us (22%)
  local copies, waits for them, and re-layouts  3.61 us (2%)
    ppermute x24, waiting for transfers between devices, send(): return lax.ppermute(x, 'filt', pairs)  43.4 us
    pallas_call x5, Pallas kernels, forward(): pl.pallas_call(functools.partial(forward_kernel, counts, places, rim_plac...  27 us
    ppermute x24, starting transfers between devices, send(): return lax.ppermute(x, 'filt', pairs)  26.9 us
    pallas_call x3, Pallas kernels, filter_terms(): pl.pallas_call(functools.partial(filter_kernel, begin, end, scale), grid_...  14.5 us
    pallas_call x2, Pallas kernels, inner_terms(): pl.pallas_call(functools.partial(inner_kernel, begin, planes), out_shape=...  12.7 us
    pallas_call x1, Pallas kernels, prepare(): pl.pallas_call(functools.partial(prepare_kernel, chan), grid=(channels //...  7.36 us
    pallas_call x1, Pallas kernels, middle(): pl.pallas_call(functools.partial(middle_kernel, places), grid_spec=pltpu....  5.29 us
    ppermute x3, starting transfers between devices, shards(): lax.ppermute(top, 'slab', shallower)  5.19 us
  transfers between devices with their start and end apart: 41, of which 11 were waited for; matrix products, arithmetic and copies ran while one was open for 1% of the time, Pallas kernels for 39%

profile of v4, /device:TPU:0, one launch (start us, length us, event | category | flops | bytes accessed | tf_op | source)
XLA Modules:
  0.0 168.8 jit_solution(10235938474434321692)
XLA Ops:
  0.6 3.0 %collective-permute-start.4 = (f32[64,8,256]{2,1,0:T(8,128)}, f32[64,8,256]{2,1,0:T(8,128)S(1)}, u32[]{:S(2)}, u32[]{:S(2)}) collective-permute-start(f32[64,8,256]{2,1,0:T(8,128)} %refs_0_.3), channel_id=1, source_target_pairs={{2,0},{4,2},{6,4},{7,6},{5,7},{3,5},{1,3},{0,1},{10,8},{12,10},{14... | collective-permute-start | bytes 1572872 | tf_op jit(solution)/shard_map/ppermute | solution.py:644
  3.8 12.1 %collective-permute-done.4.refs_2_.refs_1_ = f32[64,8,256]{2,1,0:T(8,128)S(1)} collective-permute-done((f32[64,8,256]{2,1,0:T(8,128)}, f32[64,8,256]{2,1,0:T(8,128)S(1)}, u32[]{:S(2)}, u32[]{:S(2)}) %collective-permute-start.4) | collective-permute-done | bytes 524320 | tf_op jit(solution)/shard_map/ppermute | solution.py:644
  15.9 1.7 collective-permute-start.5
  17.9 11.1 %collective-permute-done.5.refs_1_ = f32[64,8,256]{2,1,0:T(8,128)S(1)} collective-permute-done((f32[64,8,256]{2,1,0:T(8,128)S(1)}, f32[64,8,256]{2,1,0:T(8,128)S(1)}, u32[]{:S(2)}, u32[]{:S(2)}) %collective-permute-start.5) | collective-permute-done | bytes 524320 | tf_op jit(solution)/shard_map/ppermute | solution.py:644
  32.9 7.4 %prepare.1 = (bf16[3,8,576,192]{3,2,1,0:T(8,128)(2,1)}, bf16[512,1728]{1,0:T(8,128)(2,1)}, bf16[512,1728]{1,0:T(8,128)(2,1)}) custom-call(f32[27,64,512]{2,1,0:T(8,128)} %filters.1), custom_call_target="tpu_custom_call" | custom-call | bytes 17694720 | tf_op jit(solution)/shard_map/prepare/pallas_call | solution.py:82
  42.0 3.9 %forward.5 = (f32[8,64,256]{2,1,0:T(8,128)S(1)}, bf16[512,2560]{1,0:T(8,128)(2,1)S(1)}, bf16[512,2560]{1,0:T(8,128)(2,1)S(1)}) custom-call(s32[11]{0:T(128)S(1)} %dynamic-slice_bitcast_fusion.ring, f32[64,8,256]{2,1,0:T(8,128)S(1)} %copy-done, bf16[3,8,576,192]{3,2,1,0:T(8,128)(2,1)} %get-tuple-element.57.refs_1_.refs_2_.source), custom_call_target="tpu_custom_call" | custom-call | flops 1358954496 | bytes 1310720 | tf_op jit(solution)/shard_map/forward/pallas_call | solution.py:242
  46.2 1.7 %collective-permute-start.11 = (f32[192,256]{1,0:T(8,128)S(1)}, f32[192,256]{1,0:T(8,128)S(1)}, u32[]{:S(2)}, u32[]{:S(2)}) collective-permute-start(f32[192,256]{1,0:T(8,128)S(1)} %get-tuple-element.61), channel_id=1, source_target_pairs={{8,0},{16,8},{24,16},{0,24},{9,1},{17,9},{25,17},{1,25},{10,2},{18... | collective-permute-start | bytes 589832 | tf_op jit(solution)/shard_map/ppermute | solution.py:673
  50.1 5.8 %forward.6 = (f32[8,64,256]{2,1,0:T(8,128)S(1)}, bf16[512,2560]{1,0:T(8,128)(2,1)S(1)}, bf16[512,2560]{1,0:T(8,128)(2,1)S(1)}) custom-call(s32[11]{0:T(128)S(1)} %dynamic-slice_bitcast_fusion.ring, f32[64,8,256]{2,1,0:T(8,128)S(1)} %collective-permute-done.refs_1_.refs_0_, ...), custom_call_target="tpu_custom_call", output_to_operand_aliasing={{0}: (4, {}), {1}: (5, {}), {2}: (6, {})} | custom-call | flops 2717908992 | bytes 2621440 | tf_op jit(solution)/shard_map/forward/pallas_call | solution.py:242
  56.1 1.7 %collective-permute-start.9 = (f32[128,256]{1,0:T(8,128)S(1)}, f32[128,256]{1,0:T(8,128)S(1)}, u32[]{:S(2)}, u32[]{:S(2)}) collective-permute-start(f32[128,256]{1,0:T(8,128)S(1)} %get-tuple-element.59), channel_id=1, source_target_pairs={{8,0},{16,8},{24,16},{0,24},{9,1},{17,9},{25,17},{1,25},{10,2},{18... | collective-permute-start | bytes 393224 | tf_op jit(solution)/shard_map/ppermute | solution.py:673
  57.9 6.9 %forward.7 = (f32[8,64,256]{2,1,0:T(8,128)S(1)}, bf16[512,2560]{1,0:T(8,128)(2,1)S(1)}, bf16[512,2560]{1,0:T(8,128)(2,1)S(1)}) custom-call(s32[11]{0:T(128)S(1)} %dynamic-slice_bitcast_fusion.ring, f32[64,8,256]{2,1,0:T(8,128)S(1)} %collective-permute-done.1.refs_0_, ...), custom_call_target="tpu_custom_call", output_to_operand_aliasing={{0}: (6, {}), {1}: (7, {}), {2}: (8, {})} | custom-call | flops 2717908992 | bytes 2621440 | tf_op jit(solution)/shard_map/forward/pallas_call | solution.py:242
  65.1 1.7 %collective-permute-start.13 = (f32[192,256]{1,0:T(8,128)S(1)}, f32[192,256]{1,0:T(8,128)S(1)}, u32[]{:S(2)}, u32[]{:S(2)}) collective-permute-start(f32[192,256]{1,0:T(8,128)S(1)} %get-tuple-element.76), channel_id=1, source_target_pairs={{8,0},{16,8},{24,16},{0,24},{9,1},{17,9},{25,17},{1,25},{10,2},{18... | collective-permute-start | bytes 589832 | tf_op jit(solution)/shard_map/ppermute | solution.py:673
  66.8 6.5 %forward.8 = (f32[8,64,256]{2,1,0:T(8,128)S(1)}, bf16[512,2560]{1,0:T(8,128)(2,1)S(1)}, bf16[512,2560]{1,0:T(8,128)(2,1)S(1)}) custom-call(s32[11]{0:T(128)S(1)} %dynamic-slice_bitcast_fusion.ring, f32[64,8,256]{2,1,0:T(8,128)S(1)} %collective-permute-done.2.refs_0_, ...), custom_call_target="tpu_custom_call", output_to_operand_aliasing={{0}: (6, {}), {1}: (7, {}), {2}: (8, {})} | custom-call | flops 2717908992 | bytes 2621440 | tf_op jit(solution)/shard_map/forward/pallas_call | solution.py:242
  73.4 3.9 %forward.9 = (f32[8,64,256]{2,1,0:T(8,128)S(1)}, bf16[512,2560]{1,0:T(8,128)(2,1)S(1)}, bf16[512,2560]{1,0:T(8,128)(2,1)S(1)}) custom-call(s32[11]{0:T(128)S(1)} %dynamic-slice_bitcast_fusion.ring, f32[32,8,256]{2,1,0:T(8,128)S(1)} %collective-permute-done.3.refs_0_.refs_2_, ...), custom_call_target="tpu_custom_call", output_to_operand_aliasing={{0}: (4, {}), {1}: (5, {}), {2}: (6, {})} | custom-call | flops 1358954496 | bytes 1310720 | tf_op jit(solution)/shard_map/forward/pallas_call | solution.py:242
  77.3 5.3 %middle.1 = (f32[8,64,256]{2,1,0:T(8,128)S(1)}, bf16[2,10,576,256]{3,2,1,0:T(8,128)(2,1)S(1)}, bf16[512,2560]{1,0:T(8,128)(2,1)S(1)}, bf16[512,2560]{1,0:T(8,128)(2,1)S(1)}) custom-call(s32[11]{0:T(128)S(1)} %dynamic-slice_bitcast_fusion.ring, f32[8,64,256]{2,1,0:T(8,128)S(1)} %get-tuple-element.74.total, ...), custom_call_target="tpu_custom_call", output_to_operand_aliasing={{2}: (6, {}), {3}: (7, {})} | custom-call | bytes 9437184 | tf_op jit(solution)/shard_map/middle/pallas_call | solution.py:332
  82.6 6.1 %filter_terms.5 = (f32[416,512]{1,0:T(8,128)S(1)}, f32[416,512]{1,0:T(8,128)S(1)}) custom-call(s32[11]{0:T(128)S(1)} %dynamic-slice_bitcast_fusion.ring, bf16[2,10,576,256]{3,2,1,0:T(8,128)(2,1)S(1)} %get-tuple-element.80.spread, bf16[512,2560]{1,0:T(8,128)(2,1)S(1)} %get-tuple-element.101.high, bf16[512,2560]{1,0:T(8,128)(2,1)S(1)} %get-tuple-element.102.low), custom_call_target="tpu_custom_call" | custom-call | flops 6543114240 | bytes 11141120 | tf_op jit(solution)/shard_map/filter_terms/pallas_call | solution.py:464
  92.0 8.0 %inner_terms.2.inner.up_inner.down_inner.refs_0_ = f32[8,64,1280]{2,1,0:T(8,128)S(1)} custom-call(bf16[2,10,576,256]{3,2,1,0:T(8,128)(2,1)S(1)} %get-tuple-element.80.spread, bf16[512,1728]{1,0:T(8,128)(2,1)S(1)} %copy-done.3, bf16[512,1728]{1,0:T(8,128)(2,1)S(1)} %copy-done.4), custom_call_target="tpu_custom_call" | custom-call | flops 6794772480 | bytes 9437184 | tf_op jit(solution)/shard_map/inner_terms/pallas_call | solution.py:412
  100.0 4.7 %filter_terms.4 = (f32[224,512]{1,0:T(8,128)S(1)}, f32[224,512]{1,0:T(8,128)S(1)}) custom-call(s32[11]{0:T(128)S(1)} %dynamic-slice_bitcast_fusion.ring, bf16[2,10,576,256]{3,2,1,0:T(8,128)(2,1)S(1)} %get-tuple-element.80.spread, bf16[512,2560]{1,0:T(8,128)(2,1)S(1)} %get-tuple-element.101.high, bf16[512,2560]{1,0:T(8,128)(2,1)S(1)} %get-tuple-element.102.low), custom_call_target="tpu_custom_call" | custom-call | flops 3523215360 | bytes 11141120 | tf_op jit(solution)/shard_map/filter_terms/pallas_call | solution.py:464
  106.4 3.6 %filter_terms.3 = (f32[224,512]{1,0:T(8,128)S(1)}, f32[224,512]{1,0:T(8,128)S(1)}) custom-call(s32[11]{0:T(128)S(1)} %dynamic-slice_bitcast_fusion.ring, bf16[2,10,576,256]{3,2,1,0:T(8,128)(2,1)S(1)} %get-tuple-element.80.spread, bf16[512,2560]{1,0:T(8,128)(2,1)S(1)} %get-tuple-element.101.high, bf16[512,2560]{1,0:T(8,128)(2,1)S(1)} %get-tuple-element.102.low), custom_call_target="tpu_custom_call" | custom-call | flops 3523215360 | bytes 11141120 | tf_op jit(solution)/shard_map/filter_terms/pallas_call | solution.py:464
  110.9 1.6 collective-permute-start.15
  113.0 4.8 %inner_terms.3.inner.up_inner.down_inner.refs_4_ = f32[8,64,768]{2,1,0:T(8,128)S(1)} custom-call(bf16[2,10,576,256]{3,2,1,0:T(8,128)(2,1)S(1)} %get-tuple-element.80.spread, bf16[512,1728]{1,0:T(8,128)(2,1)S(1)} %copy-done.3, bf16[512,1728]{1,0:T(8,128)(2,1)S(1)} %copy-done.4), custom_call_target="tpu_custom_call" | custom-call | flops 4076863488 | bytes 9437184 | tf_op jit(solution)/shard_map/inner_terms/pallas_call | solution.py:412
  118.4 1.6 collective-permute-start.24
  120.6 1.6 collective-permute-start.17
  124.0 2.9 %collective-permute-done.25.down = f32[32,768]{1,0:T(8,128)S(1)} collective-permute-done((f32[32,768]{1,0:T(8,128)S(1)}, f32[32,768]{1,0:T(8,128)S(1)}, u32[]{:S(2)}, u32[]{:S(2)}) %collective-permute-start.25) | collective-permute-done | bytes 98336 | tf_op jit(solution)/shard_map/ppermute | solution.py:644
  131.4 3.4 %collective-permute-done.18.down = f32[64,1280]{1,0:T(8,128)S(1)} collective-permute-done((f32[64,1280]{1,0:T(8,128)S(1)}, f32[64,1280]{1,0:T(8,128)S(1)}, u32[]{:S(2)}, u32[]{:S(2)}) %collective-permute-start.18) | collective-permute-done | bytes 327712 | tf_op jit(solution)/shard_map/ppermute | solution.py:644
  135.9 1.6 collective-permute-start.19
  139.1 3.5 %collective-permute-done.27.down = f32[64,768]{1,0:T(8,128)S(1)} collective-permute-done((f32[64,768]{1,0:T(8,128)S(1)}, f32[64,768]{1,0:T(8,128)S(1)}, u32[]{:S(2)}, u32[]{:S(2)}) %collective-permute-start.27) | collective-permute-done | bytes 196640 | tf_op jit(solution)/shard_map/ppermute | solution.py:644
  143.2 2.9 %collective-permute-done.33 = f32[224,512]{1,0:T(8,128)S(1)} collective-permute-done((f32[224,512]{1,0:T(8,128)S(1)}, f32[224,512]{1,0:T(8,128)S(1)}, u32[]{:S(2)}, u32[]{:S(2)}) %collective-permute-start.33) | collective-permute-done | bytes 458784 | tf_op jit(solution)/shard_map/ppermute | solution.py:695
  148.9 3.6 %collective-permute-done.28.up = f32[64,768]{1,0:T(8,128)S(1)} collective-permute-done((f32[64,768]{1,0:T(8,128)S(1)}, f32[64,768]{1,0:T(8,128)S(1)}, u32[]{:S(2)}, u32[]{:S(2)}) %collective-permute-start.28) | collective-permute-done | bytes 196640 | tf_op jit(solution)/shard_map/ppermute | solution.py:644
  155.1 1.6 collective-permute-start.30
  158.1 1.7 %place.2.refs_2_ = f32[1728,512]{1,0:T(8,128)} custom-call(s32[11]{0:T(128)S(1)} %dynamic-slice_bitcast_fusion.ring, f32[416,512]{1,0:T(8,128)S(1)} %add.32.refs_0_, f32[416,512]{1,0:T(8,128)S(1)} %collective-permute-done.40.refs_1_), custom_call_target="tpu_custom_call" | custom-call | bytes 3407872 | tf_op jit(solution)/shard_map/place/pallas_call | solution.py:503
  161.3 3.7 %collective-permute-done.30.refs_6_ = f32[64,768]{1,0:T(8,128)S(1)} collective-permute-done((f32[64,768]{1,0:T(8,128)S(1)}, f32[64,768]{1,0:T(8,128)S(1)}, u32[]{:S(2)}, u32[]{:S(2)}) %collective-permute-start.30) | collective-permute-done | bytes 196640 | tf_op jit(solution)/shard_map/ppermute | solution.py:644
  166.3 2.3 %closing.1 = (f32[64,8,256]{2,1,0:T(8,128)}, f32[1728,512]{1,0:T(8,128)}) custom-call(s32[11]{0:T(128)S(1)} %dynamic-slice_bitcast_fusion.ring, f32[8,64,1280]{2,1,0:T(8,128)S(1)} %inner_terms.2.inner.up_inner.down_inner.refs_0_, f32[8,64,256]{2,1,0:T(8,128)S(1)} %collective-permute-done.14.rim.up_rim.down_rim.refs_1_, ...), custom_call_target="tpu_custom_call", output_to_operand_aliasing={{1}: (11, {})} | custom-call | bytes 1572864 | tf_op jit(solution)/shard_map/closing/pallas_call | solution.py:579
  (100 shorter events, 35.6 us)
Async XLA Ops:
  0.6 15.2 %collective-permute-start.4 = (f32[64,8,256]{2,1,0:T(8,128)}, f32[64,8,256]{2,1,0:T(8,128)S(1)}, u32[]{:S(2)}, u32[]{:S(2)}) collective-permute-start(f32[64,8,256]{2,1,0:T(8,128)} %refs_0_.3), channel_id=1, source_target_pairs={{2,0},{4,2},{6,4},{7,6},{5,7},{3,5},{1,3},{0,1},{10,8},{12,10},{14... | collective-permute-start | bytes 1572872 | tf_op jit(solution)/shard_map/ppermute | solution.py:644
  3.6 13.9 %collective-permute-start = (f32[64,8,256]{2,1,0:T(8,128)}, f32[64,8,256]{2,1,0:T(8,128)S(1)}, u32[]{:S(2)}, u32[]{:S(2)}) collective-permute-start(f32[64,8,256]{2,1,0:T(8,128)} %refs_0_.3), channel_id=1, source_target_pairs={{0,2},{2,4},{4,6},{6,7},{7,5},{5,3},{3,1},{1,0},{8,10},{10,12},{12... | collective-permute-start | bytes 1572872 | tf_op jit(solution)/shard_map/ppermute | solution.py:644
  15.9 13.1 %collective-permute-start.5 = (f32[64,8,256]{2,1,0:T(8,128)S(1)}, f32[64,8,256]{2,1,0:T(8,128)S(1)}, u32[]{:S(2)}, u32[]{:S(2)}) collective-permute-start(f32[64,8,256]{2,1,0:T(8,128)S(1)} %collective-permute-done.4.refs_2_.refs_1_), channel_id=1, source_target_pairs={{2,0},{4,2},{6,4},{7,6},{5,7},{3,5},{1,3},{0,1},{10,8},{12,10},{14... | collective-permute-start | bytes 1572872 | tf_op jit(solution)/shard_map/ppermute | solution.py:644
  17.5 12.8 %collective-permute-start.1 = (f32[64,8,256]{2,1,0:T(8,128)S(1)}, f32[64,8,256]{2,1,0:T(8,128)S(1)}, u32[]{:S(2)}, u32[]{:S(2)}) collective-permute-start(f32[64,8,256]{2,1,0:T(8,128)S(1)} %collective-permute-done.refs_1_.refs_0_), channel_id=1, source_target_pairs={{0,2},{2,4},{4,6},{6,7},{7,5},{5,3},{3,1},{1,0},{8,10},{10,12},{12... | collective-permute-start | bytes 1572872 | tf_op jit(solution)/shard_map/ppermute | solution.py:644
  29.0 18.9 %collective-permute-start.6 = (f32[64,8,256]{2,1,0:T(8,128)S(1)}, f32[64,8,256]{2,1,0:T(8,128)S(1)}, u32[]{:S(2)}, u32[]{:S(2)}) collective-permute-start(f32[64,8,256]{2,1,0:T(8,128)S(1)} %collective-permute-done.5.refs_1_), channel_id=1, source_target_pairs={{2,0},{4,2},{6,4},{7,6},{5,7},{3,5},{1,3},{0,1},{10,8},{12,10},{14... | collective-permute-start | bytes 1572872 | tf_op jit(solution)/shard_map/ppermute | solution.py:644
  30.3 19.0 %collective-permute-start.2 = (f32[64,8,256]{2,1,0:T(8,128)S(1)}, f32[64,8,256]{2,1,0:T(8,128)S(1)}, u32[]{:S(2)}, u32[]{:S(2)}) collective-permute-start(f32[64,8,256]{2,1,0:T(8,128)S(1)} %collective-permute-done.1.refs_0_), channel_id=1, source_target_pairs={{0,2},{2,4},{4,6},{6,7},{7,5},{5,3},{3,1},{1,0},{8,10},{10,12},{12... | collective-permute-start | bytes 1572872 | tf_op jit(solution)/shard_map/ppermute | solution.py:644
  46.1 10.0 %collective-permute-start.10 = (f32[192,256]{1,0:T(8,128)S(1)}, f32[192,256]{1,0:T(8,128)S(1)}, u32[]{:S(2)}, u32[]{:S(2)}) collective-permute-start(f32[192,256]{1,0:T(8,128)S(1)} %get-tuple-element.60), channel_id=1, source_target_pairs={{0,8},{8,16},{16,24},{24,0},{1,9},{9,17},{17,25},{25,1},{2,10},{10... | collective-permute-start | bytes 589832 | tf_op jit(solution)/shard_map/ppermute | solution.py:673
  46.2 11.7 %collective-permute-start.11 = (f32[192,256]{1,0:T(8,128)S(1)}, f32[192,256]{1,0:T(8,128)S(1)}, u32[]{:S(2)}, u32[]{:S(2)}) collective-permute-start(f32[192,256]{1,0:T(8,128)S(1)} %get-tuple-element.61), channel_id=1, source_target_pairs={{8,0},{16,8},{24,16},{0,24},{9,1},{17,9},{25,17},{1,25},{10,2},{18... | collective-permute-start | bytes 589832 | tf_op jit(solution)/shard_map/ppermute | solution.py:673
  47.9 16.9 %collective-permute-start.7 = (f32[32,8,256]{2,1,0:T(8,128)S(1)}, f32[32,8,256]{2,1,0:T(8,128)S(1)}, u32[]{:S(2)}, u32[]{:S(2)}) collective-permute-start(f32[32,8,256]{2,1,0:T(8,128)S(1)} %slice.9), channel_id=1, source_target_pairs={{2,0},{4,2},{6,4},{7,6},{5,7},{3,5},{1,3},{0,1},{10,8},{12,10},{14... | collective-permute-start | bytes 786440 | tf_op jit(solution)/shard_map/ppermute | solution.py:644
  49.4 15.4 %collective-permute-start.3 = (f32[32,8,256]{2,1,0:T(8,128)S(1)}, f32[32,8,256]{2,1,0:T(8,128)S(1)}, u32[]{:S(2)}, u32[]{:S(2)}) collective-permute-start(f32[32,8,256]{2,1,0:T(8,128)S(1)} %slice.8), channel_id=1, source_target_pairs={{0,2},{2,4},{4,6},{6,7},{7,5},{5,3},{3,1},{1,0},{8,10},{10,12},{12... | collective-permute-start | bytes 786440 | tf_op jit(solution)/shard_map/ppermute | solution.py:644
  56.1 10.8 %collective-permute-start.8 = (f32[128,256]{1,0:T(8,128)S(1)}, f32[128,256]{1,0:T(8,128)S(1)}, u32[]{:S(2)}, u32[]{:S(2)}) collective-permute-start(f32[128,256]{1,0:T(8,128)S(1)} %get-tuple-element.58), channel_id=1, source_target_pairs={{0,8},{8,16},{16,24},{24,0},{1,9},{9,17},{17,25},{25,1},{2,10},{10... | collective-permute-start | bytes 393224 | tf_op jit(solution)/shard_map/ppermute | solution.py:673
  56.1 10.7 %collective-permute-start.9 = (f32[128,256]{1,0:T(8,128)S(1)}, f32[128,256]{1,0:T(8,128)S(1)}, u32[]{:S(2)}, u32[]{:S(2)}) collective-permute-start(f32[128,256]{1,0:T(8,128)S(1)} %get-tuple-element.59), channel_id=1, source_target_pairs={{8,0},{16,8},{24,16},{0,24},{9,1},{17,9},{25,17},{1,25},{10,2},{18... | collective-permute-start | bytes 393224 | tf_op jit(solution)/shard_map/ppermute | solution.py:673
  65.0 12.2 %collective-permute-start.12 = (f32[192,256]{1,0:T(8,128)S(1)}, f32[192,256]{1,0:T(8,128)S(1)}, u32[]{:S(2)}, u32[]{:S(2)}) collective-permute-start(f32[192,256]{1,0:T(8,128)S(1)} %get-tuple-element.75), channel_id=1, source_target_pairs={{0,8},{8,16},{16,24},{24,0},{1,9},{9,17},{17,25},{25,1},{2,10},{10... | collective-permute-start | bytes 589832 | tf_op jit(solution)/shard_map/ppermute | solution.py:673
  65.1 12.2 %collective-permute-start.13 = (f32[192,256]{1,0:T(8,128)S(1)}, f32[192,256]{1,0:T(8,128)S(1)}, u32[]{:S(2)}, u32[]{:S(2)}) collective-permute-start(f32[192,256]{1,0:T(8,128)S(1)} %get-tuple-element.76), channel_id=1, source_target_pairs={{8,0},{16,8},{24,16},{0,24},{9,1},{17,9},{25,17},{1,25},{10,2},{18... | collective-permute-start | bytes 589832 | tf_op jit(solution)/shard_map/ppermute | solution.py:673
  88.7 16.1 %collective-permute-start.38 = (f32[416,512]{1,0:T(8,128)S(1)}, f32[416,512]{1,0:T(8,128)S(1)}, u32[]{:S(2)}, u32[]{:S(2)}) collective-permute-start(f32[416,512]{1,0:T(8,128)S(1)} %get-tuple-element.108), channel_id=1, source_target_pairs={{0,8},{8,0},{16,24},{24,16},{1,9},{9,1},{17,25},{25,17},{2,10},{10... | collective-permute-start | bytes 2555912 | tf_op jit(solution)/shard_map/ppermute | solution.py:695
  90.2 20.1 %collective-permute-start.14 = (f32[8,64,256]{2,1,0:T(8,128)S(1)}, f32[8,64,256]{2,1,0:T(8,128)S(1)}, u32[]{:S(2)}, u32[]{:S(2)}) collective-permute-start(f32[8,64,256]{2,1,0:T(8,128)S(1)} %get-tuple-element.83), channel_id=1, source_target_pairs={{0,8},{8,16},{16,24},{24,0},{1,9},{9,17},{17,25},{25,1},{2,10},{10... | collective-permute-start | bytes 1572872 | tf_op jit(solution)/shard_map/ppermute | solution.py:683
  90.7 21.8 %collective-permute-start.23 = (f32[8,64,256]{2,1,0:T(8,128)S(1)}, f32[8,64,256]{2,1,0:T(8,128)S(1)}, u32[]{:S(2)}, u32[]{:S(2)}) collective-permute-start(f32[8,64,256]{2,1,0:T(8,128)S(1)} %get-tuple-element.92), channel_id=1, source_target_pairs={{8,0},{16,8},{24,16},{0,24},{9,1},{17,9},{25,17},{1,25},{10,2},{18... | collective-permute-start | bytes 1572872 | tf_op jit(solution)/shard_map/ppermute | solution.py:684
  104.8 17.5 %collective-permute-start.35 = (f32[224,512]{1,0:T(8,128)S(1)}, f32[224,512]{1,0:T(8,128)S(1)}, u32[]{:S(2)}, u32[]{:S(2)}) collective-permute-start(f32[224,512]{1,0:T(8,128)S(1)} %get-tuple-element.106), channel_id=1, source_target_pairs={{0,8},{8,0},{16,24},{24,16},{1,9},{9,1},{17,25},{25,17},{2,10},{10... | collective-permute-start | bytes 1376264 | tf_op jit(solution)/shard_map/ppermute | solution.py:695
  105.0 22.9 %collective-permute-start.39 = (f32[416,512]{1,0:T(8,128)S(1)}, f32[416,512]{1,0:T(8,128)S(1)}, u32[]{:S(2)}, u32[]{:S(2)}) collective-permute-start(f32[416,512]{1,0:T(8,128)S(1)} %add.31), channel_id=1, source_target_pairs={{0,16},{8,24},{16,0},{24,8},{1,17},{9,25},{17,1},{25,9},{2,18},{10... | collective-permute-start | bytes 2555912 | tf_op jit(solution)/shard_map/ppermute | solution.py:695
  110.1 19.6 %collective-permute-start.32 = (f32[224,512]{1,0:T(8,128)S(1)}, f32[224,512]{1,0:T(8,128)S(1)}, u32[]{:S(2)}, u32[]{:S(2)}) collective-permute-start(f32[224,512]{1,0:T(8,128)S(1)} %get-tuple-element.104), channel_id=1, source_target_pairs={{0,8},{8,0},{16,24},{24,16},{1,9},{9,1},{17,25},{25,17},{2,10},{10... | collective-permute-start | bytes 1376264 | tf_op jit(solution)/shard_map/ppermute | solution.py:695
  120.6 10.6 %collective-permute-start.17 = (f32[64,1280]{1,0:T(8,128)S(1)}, f32[64,1280]{1,0:T(8,128)S(1)}, u32[]{:S(2)}, u32[]{:S(2)}) collective-permute-start(f32[64,1280]{1,0:T(8,128)S(1)} %get-tuple-element.86), channel_id=1, source_target_pairs={{0,2},{2,4},{4,6},{6,7},{7,5},{5,3},{3,1},{1,0},{8,10},{10,12},{12... | collective-permute-start | bytes 983048 | tf_op jit(solution)/shard_map/ppermute | solution.py:644
  123.4 14.2 %collective-permute-start.36 = (f32[224,512]{1,0:T(8,128)S(1)}, f32[224,512]{1,0:T(8,128)S(1)}, u32[]{:S(2)}, u32[]{:S(2)}) collective-permute-start(f32[224,512]{1,0:T(8,128)S(1)} %add.29), channel_id=1, source_target_pairs={{0,16},{8,24},{16,0},{24,8},{1,17},{9,25},{17,1},{25,9},{2,18},{10... | collective-permute-start | bytes 1376264 | tf_op jit(solution)/shard_map/ppermute | solution.py:695
  129.7 27.0 %collective-permute-start.40 = (f32[416,512]{1,0:T(8,128)S(1)}, f32[416,512]{1,0:T(8,128)S(1)}, u32[]{:S(2)}, u32[]{:S(2)}) collective-permute-start(f32[416,512]{1,0:T(8,128)S(1)} %add.32.refs_0_), channel_id=1, source_target_pairs={{0,8},{8,0},{16,24},{24,16},{1,9},{9,1},{17,25},{25,17},{2,10},{10... | collective-permute-start | bytes 2555912 | tf_op jit(solution)/shard_map/ppermute | solution.py:695
  131.3 14.8 %collective-permute-start.33 = (f32[224,512]{1,0:T(8,128)S(1)}, f32[224,512]{1,0:T(8,128)S(1)}, u32[]{:S(2)}, u32[]{:S(2)}) collective-permute-start(f32[224,512]{1,0:T(8,128)S(1)} %add.27), channel_id=1, source_target_pairs={{0,16},{8,24},{16,0},{24,8},{1,17},{9,25},{17,1},{25,9},{2,18},{10... | collective-permute-start | bytes 1376264 | tf_op jit(solution)/shard_map/ppermute | solution.py:695
  135.9 11.7 %collective-permute-start.19 = (f32[64,1280]{1,0:T(8,128)S(1)}, f32[64,1280]{1,0:T(8,128)S(1)}, u32[]{:S(2)}, u32[]{:S(2)}) collective-permute-start(f32[64,1280]{1,0:T(8,128)S(1)} %get-tuple-element.88), channel_id=1, source_target_pairs={{0,2},{2,4},{4,6},{6,7},{7,5},{5,3},{3,1},{1,0},{8,10},{10,12},{12... | collective-permute-start | bytes 983048 | tf_op jit(solution)/shard_map/ppermute | solution.py:644
  137.5 10.6 %collective-permute-start.20 = (f32[64,1280]{1,0:T(8,128)S(1)}, f32[64,1280]{1,0:T(8,128)S(1)}, u32[]{:S(2)}, u32[]{:S(2)}) collective-permute-start(f32[64,1280]{1,0:T(8,128)S(1)} %get-tuple-element.89), channel_id=1, source_target_pairs={{2,0},{4,2},{6,4},{7,6},{5,7},{3,5},{1,3},{0,1},{10,8},{12,10},{14... | collective-permute-start | bytes 983048 | tf_op jit(solution)/shard_map/ppermute | solution.py:644
  142.6 12.5 %collective-permute-start.37 = (f32[224,512]{1,0:T(8,128)S(1)}, f32[224,512]{1,0:T(8,128)S(1)}, u32[]{:S(2)}, u32[]{:S(2)}) collective-permute-start(f32[224,512]{1,0:T(8,128)S(1)} %add.30.refs_0_), channel_id=1, source_target_pairs={{0,8},{8,0},{16,24},{24,16},{1,9},{9,1},{17,25},{25,17},{2,10},{10... | collective-permute-start | bytes 1376264 | tf_op jit(solution)/shard_map/ppermute | solution.py:695
  148.2 18.1 %collective-permute-start.34 = (f32[224,512]{1,0:T(8,128)S(1)}, f32[224,512]{1,0:T(8,128)S(1)}, u32[]{:S(2)}, u32[]{:S(2)}) collective-permute-start(f32[224,512]{1,0:T(8,128)S(1)} %add.28.refs_8_), channel_id=1, source_target_pairs={{0,8},{8,0},{16,24},{24,16},{1,9},{9,1},{17,25},{25,17},{2,10},{10... | collective-permute-start | bytes 1376264 | tf_op jit(solution)/shard_map/ppermute | solution.py:695
  152.5 13.9 %collective-permute-start.21 = (f32[64,1280]{1,0:T(8,128)S(1)}, f32[64,1280]{1,0:T(8,128)S(1)}, u32[]{:S(2)}, u32[]{:S(2)}) collective-permute-start(f32[64,1280]{1,0:T(8,128)S(1)} %get-tuple-element.90), channel_id=1, source_target_pairs={{0,2},{2,4},{4,6},{6,7},{7,5},{5,3},{3,1},{1,0},{8,10},{10,12},{12... | collective-permute-start | bytes 983048 | tf_op jit(solution)/shard_map/ppermute | solution.py:644
  154.0 12.3 %collective-permute-start.22 = (f32[64,1280]{1,0:T(8,128)S(1)}, f32[64,1280]{1,0:T(8,128)S(1)}, u32[]{:S(2)}, u32[]{:S(2)}) collective-permute-start(f32[64,1280]{1,0:T(8,128)S(1)} %get-tuple-element.91), channel_id=1, source_target_pairs={{2,0},{4,2},{6,4},{7,6},{5,7},{3,5},{1,3},{0,1},{10,8},{12,10},{14... | collective-permute-start | bytes 983048 | tf_op jit(solution)/shard_map/ppermute | solution.py:644
  155.1 9.9 %collective-permute-start.30 = (f32[64,768]{1,0:T(8,128)S(1)}, f32[64,768]{1,0:T(8,128)S(1)}, u32[]{:S(2)}, u32[]{:S(2)}) collective-permute-start(f32[64,768]{1,0:T(8,128)S(1)} %get-tuple-element.99), channel_id=1, source_target_pairs={{0,2},{2,4},{4,6},{6,7},{7,5},{5,3},{3,1},{1,0},{8,10},{10,12},{12... | collective-permute-start | bytes 589832 | tf_op jit(solution)/shard_map/ppermute | solution.py:644
  156.7 9.6 %collective-permute-start.31 = (f32[64,768]{1,0:T(8,128)S(1)}, f32[64,768]{1,0:T(8,128)S(1)}, u32[]{:S(2)}, u32[]{:S(2)}) collective-permute-start(f32[64,768]{1,0:T(8,128)S(1)} %get-tuple-element.100), channel_id=1, source_target_pairs={{2,0},{4,2},{6,4},{7,6},{5,7},{3,5},{1,3},{0,1},{10,8},{12,10},{14... | collective-permute-start | bytes 589832 | tf_op jit(solution)/shard_map/ppermute | solution.py:644
  (15 other events, 80.2 us)

commit v5 on v4

--- a/solution.py
+++ b/solution.py
@@ -272,8 +272,10 @@
     )(ring, *args)
 
 
-def middle_kernel(places, ring, total, grad, below, above, source, *refs):
-    kept_out, spread_out, high_all, low_all, high_rim, low_rim, weights, sems, fetch_sems = refs[2:]
+def middle_kernel(places, ring, total, grad, shifts, below, above, source, *refs):
+    kept_out, spread_out, high_all, low_all, high_rim, low_rim, weights = refs[2:9]
+    sems, fetch_sems = refs[9:]
+    left = {}
     depth, out_rows, area = total.shape
     chan = below.shape[0] // len(places)
     copies = []
@@ -289,20 +291,26 @@
         spread_out[part, 0] = nothing
         spread_out[part, depth + 1] = nothing
 
-    def finish(plane, value):
+    def keep(plane, value):
         positive = jnp.maximum(value, 0.0)
         kept_out[plane] = positive
-        pre_grad = 2.0 * positive * grad[plane]
-        for c in range(3):
-            across = moved(pre_grad, 0, 1 - c)
-            for b in range(3):
-                high, low = parts_of(moved(across, 1 - b, 0))
-                at = (3 * b + c) * out_rows
-                spread_out[0, plane + 1, at : at + out_rows] = high
-                spread_out[1, plane + 1, at : at + out_rows] = low
+        high, low = parts_of(2.0 * positive * grad[plane])
+        left[plane] = [high, low]
+
+    def scatter(planes, lines):
+        for t in range(9):
+            copies_of = lines if t == 4 else dot(lines, shifts[t]).astype(bf16)
+            at = slice(t * out_rows, (t + 1) * out_rows)
+            for k, plane in enumerate(planes):
+                for part in range(2):
+                    from_row = (2 * k + part) * out_rows
+                    spread_out[part, plane + 1, at] = copies_of[from_row : from_row + out_rows]
 
     for plane in range(1, depth - 1):
-        finish(plane, total[plane])
+        keep(plane, total[plane])
+    middle_of = depth // 2
+    for planes in (range(1, middle_of), range(middle_of, depth - 1)):
+        scatter(planes, jnp.concatenate([x for p in planes for x in left[p]], axis=0))
     for n, rim in enumerate((below, above)):
         answer = None
         for k, place in enumerate(places):
@@ -320,12 +328,13 @@
             term = dot(weights[n, k], jnp.concatenate([high, high, low], axis=0))
             answer = term if answer is None else answer + term
         edge = n * (depth - 1)
-        finish(edge, total[edge] + gathered(answer, out_rows))
+        keep(edge, total[edge] + gathered(answer, out_rows))
+    scatter((0, depth - 1), jnp.concatenate(left[0] + left[depth - 1], axis=0))
     for copy in copies:
         copy.wait()
 
 
-def middle(ring, carry, grad, places, outer, weights, chan):
+def middle(ring, carry, grad, shifts, places, outer, weights, chan):
     total, high_all, low_all = carry
     depth, out_rows, area = total.shape
     keep = pl.BlockSpec(memory_space=pltpu.HBM)
@@ -334,7 +343,7 @@
         grid_spec=pltpu.PrefetchScalarGridSpec(
             num_scalar_prefetch=1,
             grid=(1,),
-            in_specs=[whole(x.shape) for x in (total, grad, *outer)]
+            in_specs=[whole(x.shape) for x in (total, grad, shifts, *outer)]
             + [keep, keep, keep],
             out_specs=[
                 whole((depth, out_rows, area)),
@@ -356,11 +365,11 @@
             jax.ShapeDtypeStruct(high_all.shape, bf16),
             jax.ShapeDtypeStruct(low_all.shape, bf16),
         ],
-        input_output_aliases={6: 2, 7: 3},
+        input_output_aliases={7: 2, 8: 3},
         cost_estimate=cost(0, 4 * 18 * out_rows * depth * area),
         compiler_params=limit(),
         name="middle",
-    )(ring, total, grad, *outer, weights, high_all, low_all)
+    )(ring, total, grad, shifts, *outer, weights, high_all, low_all)
 
 
 def turn_kernel(square, x, out):
@@ -375,6 +384,32 @@
         out_shape=jax.ShapeDtypeStruct((b, a, area), f32),
         cost_estimate=cost(0, 8 * x.size),
         compiler_params=limit(),
+    )(x)
+
+
+def opening_turn_kernel(x, out, shifts):
+    out[...] = jnp.swapaxes(x[...], 0, 1)
+    area = x.shape[2]
+    source = lax.broadcasted_iota(jnp.int32, (area, area), 0)
+    target = lax.broadcasted_iota(jnp.int32, (area, area), 1)
+    down = target // WIDTH - source // WIDTH
+    across = target % WIDTH - source % WIDTH
+    for t in range(9):
+        hit = (down == t // 3 - 1) & (across == t % 3 - 1)
+        shifts[t] = jnp.where(hit, 1.0, 0.0).astype(bf16)
+
+
+def opening_turn(x):
+    a, b, area = x.shape
+    return pl.pallas_call(
+        opening_turn_kernel,
+        out_shape=[
+            jax.ShapeDtypeStruct((b, a, area), f32),
+            jax.ShapeDtypeStruct((9, area, area), bf16),
+        ],
+        cost_estimate=cost(0, 8 * x.size),
+        compiler_params=limit(),
+        name="turn",
     )(x)
 
 
@@ -673,9 +708,9 @@
             outer = lax.ppermute(last, "slab", deeper), lax.ppermute(top, "slab", shallower)
             rim_places, held, held_places = held_places, [], ()
 
-    grads = turned(out_grad, False)
+    grads, shifts = opening_turn(out_grad)
     positives, spread, high_field, low_field = middle(
-        ring, carry, grads, rim_places, outer, ahead, chan
+        ring, carry, grads, shifts, rim_places, outer, ahead, chan
     )
     activated = turned(positives, True)
 

time: 169 us -> 169 us (level)
    unnamed x12 -> x16, local copies, waits for them, and re-layouts: 2.89 us -> 3.9 us
where the time goes in v5:
time: 169 us
  Pallas kernels  78.8 us (47%)
  waiting for transfers between devices  46.4 us (27%)
  starting transfers between devices  37.1 us (22%)
  local copies, waits for them, and re-layouts  4.62 us (3%)
    ppermute x24, waiting for transfers between devices, send(): return lax.ppermute(x, 'filt', pairs)  43.4 us
    pallas_call x5, Pallas kernels, forward(): pl.pallas_call(functools.partial(forward_kernel, counts, places, rim_plac...  27 us
    ppermute x24, starting transfers between devices, send(): return lax.ppermute(x, 'filt', pairs)  26.9 us
    pallas_call x3, Pallas kernels, filter_terms(): pl.pallas_call(functools.partial(filter_kernel, begin, end, scale), grid_...  14.5 us
    pallas_call x2, Pallas kernels, inner_terms(): pl.pallas_call(functools.partial(inner_kernel, begin, planes), out_shape=...  12.7 us
    pallas_call x1, Pallas kernels, prepare(): pl.pallas_call(functools.partial(prepare_kernel, chan), grid=(channels //...  7.37 us
    ppermute x3, starting transfers between devices, shards(): lax.ppermute(top, 'slab', shallower)  5.19 us
    pallas_call x8, Pallas kernels, summed(): pl.pallas_call(kernel, grid_spec=pltpu.PrefetchScalarGridSpec(num_scalar_...  4.79 us
  transfers between devices with their start and end apart: 41, of which 11 were waited for; matrix products, arithmetic and copies ran while one was open for 1% of the time, Pallas kernels for 39%

profile of v5, /device:TPU:0, one launch (start us, length us, event | category | flops | bytes accessed | tf_op | source)
XLA Modules:
  0.0 168.7 jit_solution(11929498144879026690)
XLA Ops:
  0.6 3.0 %collective-permute-start.4 = (f32[64,8,256]{2,1,0:T(8,128)}, f32[64,8,256]{2,1,0:T(8,128)S(1)}, u32[]{:S(2)}, u32[]{:S(2)}) collective-permute-start(f32[64,8,256]{2,1,0:T(8,128)} %refs_0_.3), channel_id=1, source_target_pairs={{2,0},{4,2},{6,4},{7,6},{5,7},{3,5},{1,3},{0,1},{10,8},{12,10},{14... | collective-permute-start | bytes 1572872 | tf_op jit(solution)/shard_map/ppermute | solution.py:679
  3.8 12.1 %collective-permute-done.4.refs_2_.refs_1_ = f32[64,8,256]{2,1,0:T(8,128)S(1)} collective-permute-done((f32[64,8,256]{2,1,0:T(8,128)}, f32[64,8,256]{2,1,0:T(8,128)S(1)}, u32[]{:S(2)}, u32[]{:S(2)}) %collective-permute-start.4) | collective-permute-done | bytes 524320 | tf_op jit(solution)/shard_map/ppermute | solution.py:679
  15.9 1.7 collective-permute-start.5
  17.9 11.1 %collective-permute-done.5.refs_1_ = f32[64,8,256]{2,1,0:T(8,128)S(1)} collective-permute-done((f32[64,8,256]{2,1,0:T(8,128)S(1)}, f32[64,8,256]{2,1,0:T(8,128)S(1)}, u32[]{:S(2)}, u32[]{:S(2)}) %collective-permute-start.5) | collective-permute-done | bytes 524320 | tf_op jit(solution)/shard_map/ppermute | solution.py:679
  34.2 7.4 %prepare.1 = (bf16[3,8,576,192]{3,2,1,0:T(8,128)(2,1)}, bf16[512,1728]{1,0:T(8,128)(2,1)}, bf16[512,1728]{1,0:T(8,128)(2,1)}) custom-call(f32[27,64,512]{2,1,0:T(8,128)} %filters.1), custom_call_target="tpu_custom_call" | custom-call | bytes 17694720 | tf_op jit(solution)/shard_map/prepare/pallas_call | solution.py:82
  43.3 3.9 %forward.5 = (f32[8,64,256]{2,1,0:T(8,128)S(1)}, bf16[512,2560]{1,0:T(8,128)(2,1)S(1)}, bf16[512,2560]{1,0:T(8,128)(2,1)S(1)}) custom-call(s32[11]{0:T(128)S(1)} %dynamic-slice_bitcast_fusion.ring, f32[64,8,256]{2,1,0:T(8,128)S(1)} %copy-done, bf16[3,8,576,192]{3,2,1,0:T(8,128)(2,1)} %get-tuple-element.59.refs_1_.refs_2_.source), custom_call_target="tpu_custom_call" | custom-call | flops 1358954496 | bytes 1310720 | tf_op jit(solution)/shard_map/forward/pallas_call | solution.py:242
  47.4 1.7 %collective-permute-start.11 = (f32[192,256]{1,0:T(8,128)S(1)}, f32[192,256]{1,0:T(8,128)S(1)}, u32[]{:S(2)}, u32[]{:S(2)}) collective-permute-start(f32[192,256]{1,0:T(8,128)S(1)} %get-tuple-element.63), channel_id=1, source_target_pairs={{8,0},{16,8},{24,16},{0,24},{9,1},{17,9},{25,17},{1,25},{10,2},{18... | collective-permute-start | bytes 589832 | tf_op jit(solution)/shard_map/ppermute | solution.py:708
  51.3 5.8 %forward.6 = (f32[8,64,256]{2,1,0:T(8,128)S(1)}, bf16[512,2560]{1,0:T(8,128)(2,1)S(1)}, bf16[512,2560]{1,0:T(8,128)(2,1)S(1)}) custom-call(s32[11]{0:T(128)S(1)} %dynamic-slice_bitcast_fusion.ring, f32[64,8,256]{2,1,0:T(8,128)S(1)} %collective-permute-done.refs_1_.refs_0_, ...), custom_call_target="tpu_custom_call", output_to_operand_aliasing={{0}: (4, {}), {1}: (5, {}), {2}: (6, {})} | custom-call | flops 2717908992 | bytes 2621440 | tf_op jit(solution)/shard_map/forward/pallas_call | solution.py:242
  57.4 1.7 %collective-permute-start.9 = (f32[128,256]{1,0:T(8,128)S(1)}, f32[128,256]{1,0:T(8,128)S(1)}, u32[]{:S(2)}, u32[]{:S(2)}) collective-permute-start(f32[128,256]{1,0:T(8,128)S(1)} %get-tuple-element.61), channel_id=1, source_target_pairs={{8,0},{16,8},{24,16},{0,24},{9,1},{17,9},{25,17},{1,25},{10,2},{18... | collective-permute-start | bytes 393224 | tf_op jit(solution)/shard_map/ppermute | solution.py:708
  59.1 6.9 %forward.7 = (f32[8,64,256]{2,1,0:T(8,128)S(1)}, bf16[512,2560]{1,0:T(8,128)(2,1)S(1)}, bf16[512,2560]{1,0:T(8,128)(2,1)S(1)}) custom-call(s32[11]{0:T(128)S(1)} %dynamic-slice_bitcast_fusion.ring, f32[64,8,256]{2,1,0:T(8,128)S(1)} %collective-permute-done.1.refs_0_, ...), custom_call_target="tpu_custom_call", output_to_operand_aliasing={{0}: (6, {}), {1}: (7, {}), {2}: (8, {})} | custom-call | flops 2717908992 | bytes 2621440 | tf_op jit(solution)/shard_map/forward/pallas_call | solution.py:242
  66.5 1.7 %collective-permute-start.13 = (f32[192,256]{1,0:T(8,128)S(1)}, f32[192,256]{1,0:T(8,128)S(1)}, u32[]{:S(2)}, u32[]{:S(2)}) collective-permute-start(f32[192,256]{1,0:T(8,128)S(1)} %get-tuple-element.80), channel_id=1, source_target_pairs={{8,0},{16,8},{24,16},{0,24},{9,1},{17,9},{25,17},{1,25},{10,2},{18... | collective-permute-start | bytes 589832 | tf_op jit(solution)/shard_map/ppermute | solution.py:708
  68.2 6.5 %forward.8 = (f32[8,64,256]{2,1,0:T(8,128)S(1)}, bf16[512,2560]{1,0:T(8,128)(2,1)S(1)}, bf16[512,2560]{1,0:T(8,128)(2,1)S(1)}) custom-call(s32[11]{0:T(128)S(1)} %dynamic-slice_bitcast_fusion.ring, f32[64,8,256]{2,1,0:T(8,128)S(1)} %collective-permute-done.2.refs_0_, ...), custom_call_target="tpu_custom_call", output_to_operand_aliasing={{0}: (6, {}), {1}: (7, {}), {2}: (8, {})} | custom-call | flops 2717908992 | bytes 2621440 | tf_op jit(solution)/shard_map/forward/pallas_call | solution.py:242
  74.8 3.9 %forward.9 = (f32[8,64,256]{2,1,0:T(8,128)S(1)}, bf16[512,2560]{1,0:T(8,128)(2,1)S(1)}, bf16[512,2560]{1,0:T(8,128)(2,1)S(1)}) custom-call(s32[11]{0:T(128)S(1)} %dynamic-slice_bitcast_fusion.ring, f32[32,8,256]{2,1,0:T(8,128)S(1)} %collective-permute-done.3.refs_0_.refs_2_, ...), custom_call_target="tpu_custom_call", output_to_operand_aliasing={{0}: (4, {}), {1}: (5, {}), {2}: (6, {})} | custom-call | flops 1358954496 | bytes 1310720 | tf_op jit(solution)/shard_map/forward/pallas_call | solution.py:242
  78.7 3.8 %middle.1 = (f32[8,64,256]{2,1,0:T(8,128)S(1)}, bf16[2,10,576,256]{3,2,1,0:T(8,128)(2,1)S(1)}, bf16[512,2560]{1,0:T(8,128)(2,1)S(1)}, bf16[512,2560]{1,0:T(8,128)(2,1)S(1)}) custom-call(s32[11]{0:T(128)S(1)} %dynamic-slice_bitcast_fusion.ring, f32[8,64,256]{2,1,0:T(8,128)S(1)} %get-tuple-element.76.total, ...), custom_call_target="tpu_custom_call", output_to_operand_aliasing={{2}: (7, {}), {3}: (8, {})} | custom-call | bytes 9437184 | tf_op jit(solution)/shard_map/middle/pallas_call | solution.py:341
  82.5 6.1 %filter_terms.5 = (f32[416,512]{1,0:T(8,128)S(1)}, f32[416,512]{1,0:T(8,128)S(1)}) custom-call(s32[11]{0:T(128)S(1)} %dynamic-slice_bitcast_fusion.ring, bf16[2,10,576,256]{3,2,1,0:T(8,128)(2,1)S(1)} %get-tuple-element.84.spread, bf16[512,2560]{1,0:T(8,128)(2,1)S(1)} %get-tuple-element.105.high, bf16[512,2560]{1,0:T(8,128)(2,1)S(1)} %get-tuple-element.106.low), custom_call_target="tpu_custom_call" | custom-call | flops 6543114240 | bytes 11141120 | tf_op jit(solution)/shard_map/filter_terms/pallas_call | solution.py:499
  91.9 8.0 %inner_terms.2.inner.up_inner.down_inner.refs_0_ = f32[8,64,1280]{2,1,0:T(8,128)S(1)} custom-call(bf16[2,10,576,256]{3,2,1,0:T(8,128)(2,1)S(1)} %get-tuple-element.84.spread, bf16[512,1728]{1,0:T(8,128)(2,1)S(1)} %copy-done.1, bf16[512,1728]{1,0:T(8,128)(2,1)S(1)} %copy-done.2), custom_call_target="tpu_custom_call" | custom-call | flops 6794772480 | bytes 9437184 | tf_op jit(solution)/shard_map/inner_terms/pallas_call | solution.py:447
  99.9 4.7 %filter_terms.4 = (f32[224,512]{1,0:T(8,128)S(1)}, f32[224,512]{1,0:T(8,128)S(1)}) custom-call(s32[11]{0:T(128)S(1)} %dynamic-slice_bitcast_fusion.ring, bf16[2,10,576,256]{3,2,1,0:T(8,128)(2,1)S(1)} %get-tuple-element.84.spread, bf16[512,2560]{1,0:T(8,128)(2,1)S(1)} %get-tuple-element.105.high, bf16[512,2560]{1,0:T(8,128)(2,1)S(1)} %get-tuple-element.106.low), custom_call_target="tpu_custom_call" | custom-call | flops 3523215360 | bytes 11141120 | tf_op jit(solution)/shard_map/filter_terms/pallas_call | solution.py:499
  106.4 3.6 %filter_terms.3 = (f32[224,512]{1,0:T(8,128)S(1)}, f32[224,512]{1,0:T(8,128)S(1)}) custom-call(s32[11]{0:T(128)S(1)} %dynamic-slice_bitcast_fusion.ring, bf16[2,10,576,256]{3,2,1,0:T(8,128)(2,1)S(1)} %get-tuple-element.84.spread, bf16[512,2560]{1,0:T(8,128)(2,1)S(1)} %get-tuple-element.105.high, bf16[512,2560]{1,0:T(8,128)(2,1)S(1)} %get-tuple-element.106.low), custom_call_target="tpu_custom_call" | custom-call | flops 3523215360 | bytes 11141120 | tf_op jit(solution)/shard_map/filter_terms/pallas_call | solution.py:499
  110.8 1.6 collective-permute-start.15
  112.9 4.8 %inner_terms.3.inner.up_inner.down_inner.refs_4_ = f32[8,64,768]{2,1,0:T(8,128)S(1)} custom-call(bf16[2,10,576,256]{3,2,1,0:T(8,128)(2,1)S(1)} %get-tuple-element.84.spread, bf16[512,1728]{1,0:T(8,128)(2,1)S(1)} %copy-done.1, bf16[512,1728]{1,0:T(8,128)(2,1)S(1)} %copy-done.2), custom_call_target="tpu_custom_call" | custom-call | flops 4076863488 | bytes 9437184 | tf_op jit(solution)/shard_map/inner_terms/pallas_call | solution.py:447
  118.3 1.6 collective-permute-start.24
  123.9 2.9 %collective-permute-done.25.down = f32[32,768]{1,0:T(8,128)S(1)} collective-permute-done((f32[32,768]{1,0:T(8,128)S(1)}, f32[32,768]{1,0:T(8,128)S(1)}, u32[]{:S(2)}, u32[]{:S(2)}) %collective-permute-start.25) | collective-permute-done | bytes 98336 | tf_op jit(solution)/shard_map/ppermute | solution.py:679
  127.8 1.6 collective-permute-start.26
  131.4 3.4 %collective-permute-done.18.down = f32[64,1280]{1,0:T(8,128)S(1)} collective-permute-done((f32[64,1280]{1,0:T(8,128)S(1)}, f32[64,1280]{1,0:T(8,128)S(1)}, u32[]{:S(2)}, u32[]{:S(2)}) %collective-permute-start.18) | collective-permute-done | bytes 327712 | tf_op jit(solution)/shard_map/ppermute | solution.py:679
  135.8 1.6 collective-permute-start.19
  139.0 3.5 %collective-permute-done.27.down = f32[64,768]{1,0:T(8,128)S(1)} collective-permute-done((f32[64,768]{1,0:T(8,128)S(1)}, f32[64,768]{1,0:T(8,128)S(1)}, u32[]{:S(2)}, u32[]{:S(2)}) %collective-permute-start.27) | collective-permute-done | bytes 196640 | tf_op jit(solution)/shard_map/ppermute | solution.py:679
  143.1 2.9 %collective-permute-done.33 = f32[224,512]{1,0:T(8,128)S(1)} collective-permute-done((f32[224,512]{1,0:T(8,128)S(1)}, f32[224,512]{1,0:T(8,128)S(1)}, u32[]{:S(2)}, u32[]{:S(2)}) %collective-permute-start.33) | collective-permute-done | bytes 458784 | tf_op jit(solution)/shard_map/ppermute | solution.py:730
  148.8 3.6 %collective-permute-done.28.up = f32[64,768]{1,0:T(8,128)S(1)} collective-permute-done((f32[64,768]{1,0:T(8,128)S(1)}, f32[64,768]{1,0:T(8,128)S(1)}, u32[]{:S(2)}, u32[]{:S(2)}) %collective-permute-start.28) | collective-permute-done | bytes 196640 | tf_op jit(solution)/shard_map/ppermute | solution.py:679
  155.0 1.6 collective-permute-start.30
  158.0 1.7 %place.2.refs_2_ = f32[1728,512]{1,0:T(8,128)} custom-call(s32[11]{0:T(128)S(1)} %dynamic-slice_bitcast_fusion.ring, f32[416,512]{1,0:T(8,128)S(1)} %add.32.refs_0_, f32[416,512]{1,0:T(8,128)S(1)} %collective-permute-done.40.refs_1_), custom_call_target="tpu_custom_call" | custom-call | bytes 3407872 | tf_op jit(solution)/shard_map/place/pallas_call | solution.py:538
  161.3 3.7 %collective-permute-done.30.refs_6_ = f32[64,768]{1,0:T(8,128)S(1)} collective-permute-done((f32[64,768]{1,0:T(8,128)S(1)}, f32[64,768]{1,0:T(8,128)S(1)}, u32[]{:S(2)}, u32[]{:S(2)}) %collective-permute-start.30) | collective-permute-done | bytes 196640 | tf_op jit(solution)/shard_map/ppermute | solution.py:679
  166.3 2.3 %closing.1 = (f32[64,8,256]{2,1,0:T(8,128)}, f32[1728,512]{1,0:T(8,128)}) custom-call(s32[11]{0:T(128)S(1)} %dynamic-slice_bitcast_fusion.ring, f32[8,64,1280]{2,1,0:T(8,128)S(1)} %inner_terms.2.inner.up_inner.down_inner.refs_0_, f32[8,64,256]{2,1,0:T(8,128)S(1)} %collective-permute-done.14.rim.up_rim.down_rim.refs_1_, ...), custom_call_target="tpu_custom_call", output_to_operand_aliasing={{1}: (11, {})} | custom-call | bytes 1572864 | tf_op jit(solution)/shard_map/closing/pallas_call | solution.py:614
  (104 shorter events, 37.0 us)
Async XLA Ops:
  0.6 15.2 %collective-permute-start.4 = (f32[64,8,256]{2,1,0:T(8,128)}, f32[64,8,256]{2,1,0:T(8,128)S(1)}, u32[]{:S(2)}, u32[]{:S(2)}) collective-permute-start(f32[64,8,256]{2,1,0:T(8,128)} %refs_0_.3), channel_id=1, source_target_pairs={{2,0},{4,2},{6,4},{7,6},{5,7},{3,5},{1,3},{0,1},{10,8},{12,10},{14... | collective-permute-start | bytes 1572872 | tf_op jit(solution)/shard_map/ppermute | solution.py:679
  3.6 13.9 %collective-permute-start = (f32[64,8,256]{2,1,0:T(8,128)}, f32[64,8,256]{2,1,0:T(8,128)S(1)}, u32[]{:S(2)}, u32[]{:S(2)}) collective-permute-start(f32[64,8,256]{2,1,0:T(8,128)} %refs_0_.3), channel_id=1, source_target_pairs={{0,2},{2,4},{4,6},{6,7},{7,5},{5,3},{3,1},{1,0},{8,10},{10,12},{12... | collective-permute-start | bytes 1572872 | tf_op jit(solution)/shard_map/ppermute | solution.py:679
  15.9 13.1 %collective-permute-start.5 = (f32[64,8,256]{2,1,0:T(8,128)S(1)}, f32[64,8,256]{2,1,0:T(8,128)S(1)}, u32[]{:S(2)}, u32[]{:S(2)}) collective-permute-start(f32[64,8,256]{2,1,0:T(8,128)S(1)} %collective-permute-done.4.refs_2_.refs_1_), channel_id=1, source_target_pairs={{2,0},{4,2},{6,4},{7,6},{5,7},{3,5},{1,3},{0,1},{10,8},{12,10},{14... | collective-permute-start | bytes 1572872 | tf_op jit(solution)/shard_map/ppermute | solution.py:679
  17.5 12.8 %collective-permute-start.1 = (f32[64,8,256]{2,1,0:T(8,128)S(1)}, f32[64,8,256]{2,1,0:T(8,128)S(1)}, u32[]{:S(2)}, u32[]{:S(2)}) collective-permute-start(f32[64,8,256]{2,1,0:T(8,128)S(1)} %collective-permute-done.refs_1_.refs_0_), channel_id=1, source_target_pairs={{0,2},{2,4},{4,6},{6,7},{7,5},{5,3},{3,1},{1,0},{8,10},{10,12},{12... | collective-permute-start | bytes 1572872 | tf_op jit(solution)/shard_map/ppermute | solution.py:679
  29.0 20.2 %collective-permute-start.6 = (f32[64,8,256]{2,1,0:T(8,128)S(1)}, f32[64,8,256]{2,1,0:T(8,128)S(1)}, u32[]{:S(2)}, u32[]{:S(2)}) collective-permute-start(f32[64,8,256]{2,1,0:T(8,128)S(1)} %collective-permute-done.5.refs_1_), channel_id=1, source_target_pairs={{2,0},{4,2},{6,4},{7,6},{5,7},{3,5},{1,3},{0,1},{10,8},{12,10},{14... | collective-permute-start | bytes 1572872 | tf_op jit(solution)/shard_map/ppermute | solution.py:679
  30.3 20.3 %collective-permute-start.2 = (f32[64,8,256]{2,1,0:T(8,128)S(1)}, f32[64,8,256]{2,1,0:T(8,128)S(1)}, u32[]{:S(2)}, u32[]{:S(2)}) collective-permute-start(f32[64,8,256]{2,1,0:T(8,128)S(1)} %collective-permute-done.1.refs_0_), channel_id=1, source_target_pairs={{0,2},{2,4},{4,6},{6,7},{7,5},{5,3},{3,1},{1,0},{8,10},{10,12},{12... | collective-permute-start | bytes 1572872 | tf_op jit(solution)/shard_map/ppermute | solution.py:679
  47.3 10.0 %collective-permute-start.10 = (f32[192,256]{1,0:T(8,128)S(1)}, f32[192,256]{1,0:T(8,128)S(1)}, u32[]{:S(2)}, u32[]{:S(2)}) collective-permute-start(f32[192,256]{1,0:T(8,128)S(1)} %get-tuple-element.62), channel_id=1, source_target_pairs={{0,8},{8,16},{16,24},{24,0},{1,9},{9,17},{17,25},{25,1},{2,10},{10... | collective-permute-start | bytes 589832 | tf_op jit(solution)/shard_map/ppermute | solution.py:708
  47.4 11.7 %collective-permute-start.11 = (f32[192,256]{1,0:T(8,128)S(1)}, f32[192,256]{1,0:T(8,128)S(1)}, u32[]{:S(2)}, u32[]{:S(2)}) collective-permute-start(f32[192,256]{1,0:T(8,128)S(1)} %get-tuple-element.63), channel_id=1, source_target_pairs={{8,0},{16,8},{24,16},{0,24},{9,1},{17,9},{25,17},{1,25},{10,2},{18... | collective-permute-start | bytes 589832 | tf_op jit(solution)/shard_map/ppermute | solution.py:708
  49.2 16.9 %collective-permute-start.7 = (f32[32,8,256]{2,1,0:T(8,128)S(1)}, f32[32,8,256]{2,1,0:T(8,128)S(1)}, u32[]{:S(2)}, u32[]{:S(2)}) collective-permute-start(f32[32,8,256]{2,1,0:T(8,128)S(1)} %slice.9), channel_id=1, source_target_pairs={{2,0},{4,2},{6,4},{7,6},{5,7},{3,5},{1,3},{0,1},{10,8},{12,10},{14... | collective-permute-start | bytes 786440 | tf_op jit(solution)/shard_map/ppermute | solution.py:679
  50.6 15.4 %collective-permute-start.3 = (f32[32,8,256]{2,1,0:T(8,128)S(1)}, f32[32,8,256]{2,1,0:T(8,128)S(1)}, u32[]{:S(2)}, u32[]{:S(2)}) collective-permute-start(f32[32,8,256]{2,1,0:T(8,128)S(1)} %slice.8), channel_id=1, source_target_pairs={{0,2},{2,4},{4,6},{6,7},{7,5},{5,3},{3,1},{1,0},{8,10},{10,12},{12... | collective-permute-start | bytes 786440 | tf_op jit(solution)/shard_map/ppermute | solution.py:679
  57.3 10.9 %collective-permute-start.8 = (f32[128,256]{1,0:T(8,128)S(1)}, f32[128,256]{1,0:T(8,128)S(1)}, u32[]{:S(2)}, u32[]{:S(2)}) collective-permute-start(f32[128,256]{1,0:T(8,128)S(1)} %get-tuple-element.60), channel_id=1, source_target_pairs={{0,8},{8,16},{16,24},{24,0},{1,9},{9,17},{17,25},{25,1},{2,10},{10... | collective-permute-start | bytes 393224 | tf_op jit(solution)/shard_map/ppermute | solution.py:708
  57.4 10.9 %collective-permute-start.9 = (f32[128,256]{1,0:T(8,128)S(1)}, f32[128,256]{1,0:T(8,128)S(1)}, u32[]{:S(2)}, u32[]{:S(2)}) collective-permute-start(f32[128,256]{1,0:T(8,128)S(1)} %get-tuple-element.61), channel_id=1, source_target_pairs={{8,0},{16,8},{24,16},{0,24},{9,1},{17,9},{25,17},{1,25},{10,2},{18... | collective-permute-start | bytes 393224 | tf_op jit(solution)/shard_map/ppermute | solution.py:708
  66.2 12.4 %collective-permute-start.12 = (f32[192,256]{1,0:T(8,128)S(1)}, f32[192,256]{1,0:T(8,128)S(1)}, u32[]{:S(2)}, u32[]{:S(2)}) collective-permute-start(f32[192,256]{1,0:T(8,128)S(1)} %get-tuple-element.79), channel_id=1, source_target_pairs={{0,8},{8,16},{16,24},{24,0},{1,9},{9,17},{17,25},{25,1},{2,10},{10... | collective-permute-start | bytes 589832 | tf_op jit(solution)/shard_map/ppermute | solution.py:708
  66.5 12.2 %collective-permute-start.13 = (f32[192,256]{1,0:T(8,128)S(1)}, f32[192,256]{1,0:T(8,128)S(1)}, u32[]{:S(2)}, u32[]{:S(2)}) collective-permute-start(f32[192,256]{1,0:T(8,128)S(1)} %get-tuple-element.80), channel_id=1, source_target_pairs={{8,0},{16,8},{24,16},{0,24},{9,1},{17,9},{25,17},{1,25},{10,2},{18... | collective-permute-start | bytes 589832 | tf_op jit(solution)/shard_map/ppermute | solution.py:708
  88.6 16.1 %collective-permute-start.38 = (f32[416,512]{1,0:T(8,128)S(1)}, f32[416,512]{1,0:T(8,128)S(1)}, u32[]{:S(2)}, u32[]{:S(2)}) collective-permute-start(f32[416,512]{1,0:T(8,128)S(1)} %get-tuple-element.112), channel_id=1, source_target_pairs={{0,8},{8,0},{16,24},{24,16},{1,9},{9,1},{17,25},{25,17},{2,10},{10... | collective-permute-start | bytes 2555912 | tf_op jit(solution)/shard_map/ppermute | solution.py:730
  90.1 20.1 %collective-permute-start.14 = (f32[8,64,256]{2,1,0:T(8,128)S(1)}, f32[8,64,256]{2,1,0:T(8,128)S(1)}, u32[]{:S(2)}, u32[]{:S(2)}) collective-permute-start(f32[8,64,256]{2,1,0:T(8,128)S(1)} %get-tuple-element.87), channel_id=1, source_target_pairs={{0,8},{8,16},{16,24},{24,0},{1,9},{9,17},{17,25},{25,1},{2,10},{10... | collective-permute-start | bytes 1572872 | tf_op jit(solution)/shard_map/ppermute | solution.py:718
  90.6 21.8 %collective-permute-start.23 = (f32[8,64,256]{2,1,0:T(8,128)S(1)}, f32[8,64,256]{2,1,0:T(8,128)S(1)}, u32[]{:S(2)}, u32[]{:S(2)}) collective-permute-start(f32[8,64,256]{2,1,0:T(8,128)S(1)} %get-tuple-element.96), channel_id=1, source_target_pairs={{8,0},{16,8},{24,16},{0,24},{9,1},{17,9},{25,17},{1,25},{10,2},{18... | collective-permute-start | bytes 1572872 | tf_op jit(solution)/shard_map/ppermute | solution.py:719
  104.7 17.5 %collective-permute-start.35 = (f32[224,512]{1,0:T(8,128)S(1)}, f32[224,512]{1,0:T(8,128)S(1)}, u32[]{:S(2)}, u32[]{:S(2)}) collective-permute-start(f32[224,512]{1,0:T(8,128)S(1)} %get-tuple-element.110), channel_id=1, source_target_pairs={{0,8},{8,0},{16,24},{24,16},{1,9},{9,1},{17,25},{25,17},{2,10},{10... | collective-permute-start | bytes 1376264 | tf_op jit(solution)/shard_map/ppermute | solution.py:730
  104.9 22.9 %collective-permute-start.39 = (f32[416,512]{1,0:T(8,128)S(1)}, f32[416,512]{1,0:T(8,128)S(1)}, u32[]{:S(2)}, u32[]{:S(2)}) collective-permute-start(f32[416,512]{1,0:T(8,128)S(1)} %add.31), channel_id=1, source_target_pairs={{0,16},{8,24},{16,0},{24,8},{1,17},{9,25},{17,1},{25,9},{2,18},{10... | collective-permute-start | bytes 2555912 | tf_op jit(solution)/shard_map/ppermute | solution.py:730
  110.0 19.6 %collective-permute-start.32 = (f32[224,512]{1,0:T(8,128)S(1)}, f32[224,512]{1,0:T(8,128)S(1)}, u32[]{:S(2)}, u32[]{:S(2)}) collective-permute-start(f32[224,512]{1,0:T(8,128)S(1)} %get-tuple-element.108), channel_id=1, source_target_pairs={{0,8},{8,0},{16,24},{24,16},{1,9},{9,1},{17,25},{25,17},{2,10},{10... | collective-permute-start | bytes 1376264 | tf_op jit(solution)/shard_map/ppermute | solution.py:730
  120.5 10.6 %collective-permute-start.17 = (f32[64,1280]{1,0:T(8,128)S(1)}, f32[64,1280]{1,0:T(8,128)S(1)}, u32[]{:S(2)}, u32[]{:S(2)}) collective-permute-start(f32[64,1280]{1,0:T(8,128)S(1)} %get-tuple-element.90), channel_id=1, source_target_pairs={{0,2},{2,4},{4,6},{6,7},{7,5},{5,3},{3,1},{1,0},{8,10},{10,12},{12... | collective-permute-start | bytes 983048 | tf_op jit(solution)/shard_map/ppermute | solution.py:679
  123.3 14.2 %collective-permute-start.36 = (f32[224,512]{1,0:T(8,128)S(1)}, f32[224,512]{1,0:T(8,128)S(1)}, u32[]{:S(2)}, u32[]{:S(2)}) collective-permute-start(f32[224,512]{1,0:T(8,128)S(1)} %add.29), channel_id=1, source_target_pairs={{0,16},{8,24},{16,0},{24,8},{1,17},{9,25},{17,1},{25,9},{2,18},{10... | collective-permute-start | bytes 1376264 | tf_op jit(solution)/shard_map/ppermute | solution.py:730
  129.6 27.0 %collective-permute-start.40 = (f32[416,512]{1,0:T(8,128)S(1)}, f32[416,512]{1,0:T(8,128)S(1)}, u32[]{:S(2)}, u32[]{:S(2)}) collective-permute-start(f32[416,512]{1,0:T(8,128)S(1)} %add.32.refs_0_), channel_id=1, source_target_pairs={{0,8},{8,0},{16,24},{24,16},{1,9},{9,1},{17,25},{25,17},{2,10},{10... | collective-permute-start | bytes 2555912 | tf_op jit(solution)/shard_map/ppermute | solution.py:730
  131.2 14.8 %collective-permute-start.33 = (f32[224,512]{1,0:T(8,128)S(1)}, f32[224,512]{1,0:T(8,128)S(1)}, u32[]{:S(2)}, u32[]{:S(2)}) collective-permute-start(f32[224,512]{1,0:T(8,128)S(1)} %add.27), channel_id=1, source_target_pairs={{0,16},{8,24},{16,0},{24,8},{1,17},{9,25},{17,1},{25,9},{2,18},{10... | collective-permute-start | bytes 1376264 | tf_op jit(solution)/shard_map/ppermute | solution.py:730
  135.8 11.7 %collective-permute-start.19 = (f32[64,1280]{1,0:T(8,128)S(1)}, f32[64,1280]{1,0:T(8,128)S(1)}, u32[]{:S(2)}, u32[]{:S(2)}) collective-permute-start(f32[64,1280]{1,0:T(8,128)S(1)} %get-tuple-element.92), channel_id=1, source_target_pairs={{0,2},{2,4},{4,6},{6,7},{7,5},{5,3},{3,1},{1,0},{8,10},{10,12},{12... | collective-permute-start | bytes 983048 | tf_op jit(solution)/shard_map/ppermute | solution.py:679
  137.5 10.6 %collective-permute-start.20 = (f32[64,1280]{1,0:T(8,128)S(1)}, f32[64,1280]{1,0:T(8,128)S(1)}, u32[]{:S(2)}, u32[]{:S(2)}) collective-permute-start(f32[64,1280]{1,0:T(8,128)S(1)} %get-tuple-element.93), channel_id=1, source_target_pairs={{2,0},{4,2},{6,4},{7,6},{5,7},{3,5},{1,3},{0,1},{10,8},{12,10},{14... | collective-permute-start | bytes 983048 | tf_op jit(solution)/shard_map/ppermute | solution.py:679
  142.5 12.5 %collective-permute-start.37 = (f32[224,512]{1,0:T(8,128)S(1)}, f32[224,512]{1,0:T(8,128)S(1)}, u32[]{:S(2)}, u32[]{:S(2)}) collective-permute-start(f32[224,512]{1,0:T(8,128)S(1)} %add.30.refs_0_), channel_id=1, source_target_pairs={{0,8},{8,0},{16,24},{24,16},{1,9},{9,1},{17,25},{25,17},{2,10},{10... | collective-permute-start | bytes 1376264 | tf_op jit(solution)/shard_map/ppermute | solution.py:730
  148.1 18.2 %collective-permute-start.34 = (f32[224,512]{1,0:T(8,128)S(1)}, f32[224,512]{1,0:T(8,128)S(1)}, u32[]{:S(2)}, u32[]{:S(2)}) collective-permute-start(f32[224,512]{1,0:T(8,128)S(1)} %add.28.refs_8_), channel_id=1, source_target_pairs={{0,8},{8,0},{16,24},{24,16},{1,9},{9,1},{17,25},{25,17},{2,10},{10... | collective-permute-start | bytes 1376264 | tf_op jit(solution)/shard_map/ppermute | solution.py:730
  152.4 13.9 %collective-permute-start.21 = (f32[64,1280]{1,0:T(8,128)S(1)}, f32[64,1280]{1,0:T(8,128)S(1)}, u32[]{:S(2)}, u32[]{:S(2)}) collective-permute-start(f32[64,1280]{1,0:T(8,128)S(1)} %get-tuple-element.94), channel_id=1, source_target_pairs={{0,2},{2,4},{4,6},{6,7},{7,5},{5,3},{3,1},{1,0},{8,10},{10,12},{12... | collective-permute-start | bytes 983048 | tf_op jit(solution)/shard_map/ppermute | solution.py:679
  154.0 12.3 %collective-permute-start.22 = (f32[64,1280]{1,0:T(8,128)S(1)}, f32[64,1280]{1,0:T(8,128)S(1)}, u32[]{:S(2)}, u32[]{:S(2)}) collective-permute-start(f32[64,1280]{1,0:T(8,128)S(1)} %get-tuple-element.95), channel_id=1, source_target_pairs={{2,0},{4,2},{6,4},{7,6},{5,7},{3,5},{1,3},{0,1},{10,8},{12,10},{14... | collective-permute-start | bytes 983048 | tf_op jit(solution)/shard_map/ppermute | solution.py:679
  155.0 9.9 %collective-permute-start.30 = (f32[64,768]{1,0:T(8,128)S(1)}, f32[64,768]{1,0:T(8,128)S(1)}, u32[]{:S(2)}, u32[]{:S(2)}) collective-permute-start(f32[64,768]{1,0:T(8,128)S(1)} %get-tuple-element.103), channel_id=1, source_target_pairs={{0,2},{2,4},{4,6},{6,7},{7,5},{5,3},{3,1},{1,0},{8,10},{10,12},{12... | collective-permute-start | bytes 589832 | tf_op jit(solution)/shard_map/ppermute | solution.py:679
  156.7 9.6 %collective-permute-start.31 = (f32[64,768]{1,0:T(8,128)S(1)}, f32[64,768]{1,0:T(8,128)S(1)}, u32[]{:S(2)}, u32[]{:S(2)}) collective-permute-start(f32[64,768]{1,0:T(8,128)S(1)} %get-tuple-element.104), channel_id=1, source_target_pairs={{2,0},{4,2},{6,4},{7,6},{5,7},{3,5},{1,3},{0,1},{10,8},{12,10},{14... | collective-permute-start | bytes 589832 | tf_op jit(solution)/shard_map/ppermute | solution.py:679
  (17 other events, 85.1 us)
